TPU v7x, 256 devices: a whole 4x4x8 slice. The times are simulated.
256 devices in a mesh: comp: 2 (over y_hi), lon: 64 (over z, x, core), ch: 2 (over y_lo).
Axes of the slice: x: 4, y: 4 (y_hi: 2, y_lo: 2; y = y_hi * 2 + y_lo), z: 8, core: 2. Of those that a mesh axis runs over, the one named last changes fastest.
Arguments:
- ocean_state: bfloat16 [3, 128, 512, 256], P(None, 'ch', ('comp', 'lon')), may hold values from -6 to 6
- ocean_mask: int32 [512, 256], P(('comp', 'lon')), may hold values 0 or 1
- air_state: bfloat16 [2, 192, 256, 2, 256], P(None, 'ch', 'lon', None, 'comp'), may hold values from -6 to 6
- surface_temp: float32 [512, 256], P(('comp', 'lon')), may hold values from -6 to 6
- air_fluxes: float32 [4, 256, 2, 256], P(None, 'lon', None, 'comp'), may hold values from -6 to 6
- ocean_kernel: float32 [128, 3, 7, 7], P('ch'), may hold values from -0.5 to 0.5
- ocean_gain: float32 [128], replicated, may hold values from 0.5 to 1.5
- ocean_up: bfloat16 [128, 512], replicated, may hold values from -0.5 to 0.5
- ocean_down: bfloat16 [512, 128], replicated, may hold values from -0.25 to 0.25
- air_kernel: float32 [192, 3, 7, 7], P('ch'), may hold values from -0.5 to 0.5
- air_gain: float32 [192], replicated, may hold values from 0.5 to 1.5
- air_up: bfloat16 [192, 768], replicated, may hold values from -0.4375 to 0.4375
- air_down: bfloat16 [768, 192], replicated, may hold values from -0.21875 to 0.21875
- flux_weight: float32 [4, 128], P(None, 'ch'), may hold values from -3 to 3
- temp_weight: float32 [192], P('ch'), may hold values from -1 to 1
Outputs:
- ocean_next: bfloat16 [3, 128, 512, 256], P(None, 'ch', ('comp', 'lon'))
- air_next: bfloat16 [2, 192, 256, 2, 256], P(None, 'ch', 'lon', None, 'comp')
All inputs are finite; a program needn't handle non-finite values. No bound on the sum of `ocean_mask` on one device may be relied on, other than what follows from the above.
Results may differ from a plain program's by a relative error of at most 0.007.
Values may be sent and summed in bfloat16 or wider, within the bound.
No kernel may reach another device: no remote copies, remote signals or barrier semaphores. Data moves between devices by JAX's collectives and lax.ppermute only.
A program may use at most 64 MiB of HBM per device.

v0:
```python
import jax
import jax.numpy as jnp
from jax import lax
from jax.sharding import PartitionSpec as P


def padded_2(block, sides, width):
    for axis, dim in sides:
        count = lax.axis_size(axis)
        forward = [(i, i + 1) for i in range(count - 1)]
        forward.append((count - 1, 0))
        backward = [(target, source) for source, target in forward]
        low = lax.ppermute(
            lax.slice_in_dim(block, block.shape[dim] - width, None, axis=dim), axis, forward
        )
        high = lax.ppermute(lax.slice_in_dim(block, 0, width, axis=dim), axis, backward)
        block = jnp.concatenate([low, block, high], axis=dim)
    return block


def depthwise(padded, kernel, out_shape):
    levels = out_shape[0]
    widths = out_shape[2]
    lat_cells = out_shape[-1]
    ones_tail = (1,) * (padded.ndim - 2)
    summed = jnp.zeros(out_shape, jnp.float32)
    for level_off in range(3):
        for lon_off in range(7):
            for lat_off in range(7):
                weight = kernel[:, level_off, lon_off, lat_off].reshape(
                    (1, kernel.shape[0]) + ones_tail
                )
                window = lax.slice_in_dim(padded, level_off, level_off + levels, axis=0)
                window = lax.slice_in_dim(window, lon_off, lon_off + widths, axis=2)
                window = lax.slice_in_dim(
                    window, lat_off, lat_off + lat_cells, axis=padded.ndim - 1
                )
                summed = summed + weight * window
    return summed


def channel_norm(conv_out, gain_vec):
    values = conv_out.astype(jnp.float32)
    center = jnp.mean(values, axis=1, keepdims=True)
    spread = jnp.mean(jnp.square(values - center), axis=1, keepdims=True)
    scaled = gain_vec.reshape((1, gain_vec.shape[0]) + (1,) * (values.ndim - 2))
    return ((values - center) * lax.rsqrt(spread + 1e-06) * scaled).astype(jnp.bfloat16)


def feed_forward(normed, up_proj, down_proj):
    hidden = jax.nn.gelu(
        jnp.einsum("ch,lc...->lh...", up_proj, normed, preferred_element_type=jnp.float32)
    ).astype(jnp.bfloat16)
    return jnp.einsum("hc,lh...->lc...", down_proj, hidden, preferred_element_type=jnp.float32)


def mend_edges(edged, band_cells, lat_part, groups):
    row_index = jnp.arange(lat_part + 6)
    comp_index = lax.axis_index("comp")
    drop_rows = (row_index < 3) & (comp_index == 0) | (row_index >= lat_part + 3) & (
        comp_index == groups - 1
    )
    edged = jnp.where(drop_rows, 0.0, edged)
    column_index = jnp.arange(band_cells + 6)
    lon_index = lax.axis_index("lon")
    bands = lax.axis_size("lon")
    west_cols = ((column_index < 3) & (lon_index == 0))[:, None, None]
    east_cols = ((column_index >= band_cells + 3) & (lon_index == bands - 1))[:, None, None]
    return jnp.where(
        west_cols,
        jnp.roll(edged, 1, axis=3),
        jnp.where(east_cols, jnp.roll(edged, -1, axis=3), edged),
    )


def per_device(
    ocean_state,
    ocean_mask,
    air_state,
    surface_temp,
    air_fluxes,
    ocean_kernel,
    ocean_gain,
    ocean_up,
    ocean_down,
    air_kernel,
    air_gain,
    air_up,
    air_down,
    flux_weight,
    temp_weight,
):
    sea_mask = ocean_mask.astype(jnp.float32)
    band_cells = ocean_state.shape[2]
    lat_cells = ocean_state.shape[3]
    groups = lax.axis_size("comp")
    lat_part = lat_cells // groups
    flux_count = air_fluxes.shape[0]
    sent_temp = (surface_temp * sea_mask).reshape(1, band_cells, 1, groups, lat_part)
    sent_flux = air_fluxes.reshape(flux_count, band_cells, 1, groups, lat_part)
    got_temp, got_flux = (
        lax.all_to_all(sent_temp, "comp", split_axis=3, concat_axis=2, tiled=True),
        lax.all_to_all(sent_flux, "comp", split_axis=3, concat_axis=2, tiled=True),
    )
    air_temp = got_temp.reshape(band_cells, groups, lat_part)
    ocean_flux = got_flux.reshape(flux_count, band_cells, lat_cells)
    inject = jnp.einsum("kc,kxy->cxy", flux_weight, ocean_flux, precision=lax.Precision.HIGHEST)
    ocean_states = ocean_state.astype(jnp.float32)
    ocean_forced = (
        jnp.concatenate([ocean_states[:1] + inject[None], ocean_states[1:]], axis=0) * sea_mask
    )
    rimmed = padded_2(ocean_forced, ((("comp", "lon"), 2),), 3)
    air_states = air_state.astype(jnp.float32)
    heating = temp_weight[:, None, None, None] * air_temp[None]
    air_forced = jnp.concatenate([air_states[:1] + heating[None], air_states[1:]], axis=0)
    edged = padded_2(air_forced, (("comp", 4), ("lon", 2)), 3)
    edged = mend_edges(edged, band_cells, lat_part, groups)
    rimmed = jnp.pad(rimmed, ((1, 1), (0, 0), (0, 0), (3, 3)))
    ocean_conv = depthwise(rimmed, ocean_kernel, ocean_forced.shape).astype(jnp.bfloat16)
    edged = jnp.pad(edged, ((1, 1), (0, 0), (0, 0), (0, 0), (0, 0)))
    air_conv = depthwise(edged, air_kernel, air_forced.shape).astype(jnp.bfloat16)
    whole_ocean, whole_air = (
        lax.all_gather(ocean_conv, "ch", axis=1, tiled=True),
        lax.all_gather(air_conv, "ch", axis=1, tiled=True),
    )
    part_index = lax.axis_index("ch")
    parts = lax.axis_size("ch")
    ocean_width = ocean_up.shape[1] // parts
    air_width = air_up.shape[1] // parts
    ocean_part = feed_forward(
        channel_norm(whole_ocean, ocean_gain),
        lax.dynamic_slice_in_dim(ocean_up, part_index * ocean_width, ocean_width, 1),
        lax.dynamic_slice_in_dim(ocean_down, part_index * ocean_width, ocean_width, 0),
    )
    air_part = feed_forward(
        channel_norm(whole_air, air_gain),
        lax.dynamic_slice_in_dim(air_up, part_index * air_width, air_width, 1),
        lax.dynamic_slice_in_dim(air_down, part_index * air_width, air_width, 0),
    )
    ocean_summed, air_summed = (
        lax.psum_scatter(ocean_part, "ch", scatter_dimension=1, tiled=True),
        lax.psum_scatter(air_part, "ch", scatter_dimension=1, tiled=True),
    )
    ocean_update = ocean_summed.astype(jnp.bfloat16)
    air_update = air_summed.astype(jnp.bfloat16)
    ocean_next = ((ocean_forced + ocean_update.astype(jnp.float32)) * sea_mask).astype(jnp.bfloat16)
    air_next = (air_forced + air_update.astype(jnp.float32)).astype(jnp.bfloat16)
    return (ocean_next, air_next)


def solution(mesh):
    in_specs = (
        P(None, "ch", ("comp", "lon"), None),
        P(("comp", "lon"), None),
        P(None, "ch", "lon", None, "comp"),
        P(("comp", "lon"), None),
        P(None, "lon", None, "comp"),
        P("ch", None, None, None),
        P(),
        P(),
        P(),
        P("ch", None, None, None),
        P(),
        P(),
        P(),
        P(None, "ch"),
        P("ch"),
    )
    out_specs = (P(None, "ch", ("comp", "lon"), None), P(None, "ch", "lon", None, "comp"))
    return jax.shard_map(
        per_device, mesh=mesh, in_specs=in_specs, out_specs=out_specs, check_vma=False
    )
```

profile of v0, /device:TPU:8, one launch (start us, length us, event | category | flops | bytes accessed | tf_op | source)
XLA Modules:
  0.0 261.5 jit_solution(11224694601812276739)
XLA Ops:
  8.5 3.6 %all-to-all-start.1 = ((f32[1,4,1,2,128]{4,1,2,0,3:T(4,128)}), f32[1,4,1,2,128]{4,1,2,0,3:T(4,128)S(1)}, u32[]{:S(2)}, u32[]{:S(2)}) async-start(f32[1,4,1,2,128]{4,1,2,0,3:T(4,128)} %multiply_bitcast_fusion), calls=%async_computation.2 | async-start | bytes 8192 | tf_op jit(solution)/shard_map/all_to_all | solution.py:102
  25.0 1.7 slice_bitcast_fusion.293
  30.0 1.7 slice_bitcast_fusion.290
  33.2 1.7 slice_bitcast_fusion.288
  42.8 4.8 %all-to-all-start = ((f32[4,4,1,2,128]{4,1,0,2,3:T(4,128)}), f32[4,4,1,2,128]{4,1,0,2,3:T(4,128)S(1)}, u32[]{:S(2)}, u32[]{:S(2)}) async-start(f32[4,4,1,2,128]{4,1,0,2,3:T(4,128)} %bitcast.641), calls=%async_computation | async-start | bytes 32768 | tf_op jit(solution)/shard_map/all_to_all | solution.py:103
  47.7 5.2 %all-to-all-done = f32[4,4,1,2,128]{4,1,0,2,3:T(4,128)S(1)} async-done(((f32[4,4,1,2,128]{4,1,0,2,3:T(4,128)}), f32[4,4,1,2,128]{4,1,0,2,3:T(4,128)S(1)}, u32[]{:S(2)}, u32[]{:S(2)}) %all-to-all-start) | async-done | bytes 16416 | tf_op jit(solution)/shard_map/all_to_all | solution.py:103
  54.7 7.5 %collective-permute-start.1 = (f32[3,64,3,256]{3,1,2,0:T(8,128)}, f32[3,64,3,256]{3,1,2,0:T(8,128)}, u32[]{:S(2)}, u32[]{:S(2)}) collective-permute-start(f32[3,64,3,256]{3,1,2,0:T(8,128)} %get-tuple-element.15), channel_id=1, source_target_pairs={{2,0},{4,2},{6,4},{8,6},{10,8},{12,10},{14,12},{16,14},{18,16},{20... | collective-permute-start | bytes 1769480 | tf_op jit(solution)/shard_map/ppermute | solution.py:16
  66.1 2.6 collective-permute-start.3
  72.5 1.8 fusion.482
  74.3 2.4 copy.36
  76.7 2.4 copy.37
  79.5 5.4 %collective-permute-start.5 = (f32[2,96,3,2,134]{1,3,4,2,0:T(2,128)}, f32[2,96,3,2,134]{1,3,4,2,0:T(2,128)}, u32[]{:S(2)}, u32[]{:S(2)}) collective-permute-start(f32[2,96,3,2,134]{1,3,4,2,0:T(2,128)} %copy.37), channel_id=1, source_target_pairs={{2,0},{4,2},{6,4},{8,6},{10,8},{12,10},{14,12},{16,14},{18,16},{20... | collective-permute-start | bytes 1852424 | tf_op jit(solution)/shard_map/ppermute | solution.py:16
  84.9 2.5 select_maximum_fusion
  87.7 32.2 %fusion.351 = bf16[3,64,4,256]{3,1,2,0:T(8,128)(2,1)S(1)} fusion(f32[5,64,10,262]{3,1,2,0:T(8,128)S(1)} %select_maximum_fusion, f32[3,64,3,256]{3,1,2,0:T(8,128)} %collective-permute-done.1, f32[3,64,4,256]{3,1,2,0:T(8,128)S(1)} %maximum_multiply_fusion, f32[3,64,3,256]{3,1,2,0:T(8,128)} %collective-permute-done, f32[64]{0:T(128)} %get-tuple-element.289, ...), kind=kLoop, calls=%fused_computation.524 | loop fusion | flops 58982400 | bytes 112497408 | tf_op jit(solution)/shard_map/convert_element_type | solution.py:119
  119.9 8.4 %all_gather.6 = bf16[3,128,4,256]{3,1,2,0:T(8,128)(2,1)S(1)} all-gather(bf16[3,64,4,256]{3,1,2,0:T(8,128)(2,1)S(1)} %fusion.351), channel_id=1, replica_groups=mesh['comp'=2,'lon'=64,'ch'=2] {'ch'}, dimensions={1}, use_global_device_ids=true | all-gather | bytes 1179648 | tf_op jit(solution)/shard_map/all_gather | solution.py:123
  128.8 3.8 %fusion.32 = f32[3,128,4,256]{3,1,2,0:T(8,128)} fusion(bf16[3,128,4,256]{3,1,2,0:T(8,128)(2,1)S(1)} %all_gather.6, f32[128]{0:T(128)} %param.21, f32[3,4,256]{2,1,0:T(4,128)S(1)} %add_rsqrt_fusion, f32[3,4,256]{2,1,0:T(4,128)S(1)} %broadcast_multiply_fusion, bf16[512,128]{1,0:T(8,128)(2,1)} %param.23, s32[]{:T(128)S(6)} %select_n.19, ...), kind=kOutput, calls=%fused_computation.153 | convolution fusion | flops 411697152 | bytes 2516480 | tf_op jit(solution)/shard_map/hc,lh...->lc.../dot_general | solution.py:54
  132.9 2.4 copy.38
  135.3 2.4 copy.39
  137.6 2.6 %maximum_select_fusion = f32[2,96,10,2,134]{4,1,3,2,0:T(8,128)S(1)} fusion(f32[2,96,3,2,134]{4,1,3,2,0:T(8,128)} %copy.39, f32[2,96,4,2,3]{4,1,3,2,0:T(8,128)S(1)} %copy.35, f32[1,96,4,2,128]{4,1,3,2,0:T(8,128)S(1)} %get-tuple-element.13, f32[1,96,4,2,128]{4,1,3,2,0:T(8,128)S(1)} %get-tuple-element.12, f32[2,96,4,2,3]{4,1,3,2,0:T(8,128)S(1)} %copy.34, ...), kind=kLoop, calls=%fused_computation.110 | loop fusion | flops 3087360 | bytes 4116614 | tf_op jit(solution)/shard_map/jit(_where)/select_n | solution.py:63
  141.1 3.5 %select_select_fusion = f32[2,96,10,2,134]{4,1,3,2,0:T(8,128)} fusion(f32[2,96,10,2,134]{4,1,3,2,0:T(8,128)S(1)} %maximum_select_fusion, f32[2,96,10,1,134]{4,1,3,2,0:T(8,128)S(1)} %get-tuple-element.7, f32[2,96,10,1,134]{4,1,3,2,0:T(8,128)S(1)} %get-tuple-element.6, pred[10]{0:T(512)(128)(4,1)} %compare_and_fusion, pred[10]{0:T(512)(128)(4,1)} %compare_and_fusion.1), kind=kLoop, calls=%fused_computation.102 | loop fusion | flops 1543680 | bytes 6174740 | tf_op jit(solution)/shard_map/jit(_where)/select_n | solution.py:69
  145.0 63.5 %fusion.455 = bf16[2,96,4,2,128]{4,1,3,2,0:T(8,128)(2,1)S(1)} fusion(f32[2,96,10,2,134]{4,1,3,2,0:T(8,128)} %select_select_fusion, f32[96]{0:T(128)} %get-tuple-element.142, f32[96]{0:T(128)} %get-tuple-element.143, f32[96]{0:T(128)S(1)} %copy-done.28, f32[96]{0:T(128)S(1)} %copy-done.29, f32[96]{0:T(128)S(1)} %copy-done.30, f32[96]{0:T(128)S(1)} %copy-done.31, ...), kind=kLoop, calls=%fused_computation.765 | loop fusion | flops 57802752 | bytes 42928512 | tf_op jit(solution)/shard_map/convert_element_type | solution.py:121
  208.5 8.4 %all_gather.7 = bf16[2,192,4,2,128]{4,1,3,2,0:T(8,128)(2,1)S(1)} all-gather(bf16[2,96,4,2,128]{4,1,3,2,0:T(8,128)(2,1)S(1)} %fusion.455), channel_id=1, replica_groups=mesh['comp'=2,'lon'=64,'ch'=2] {'ch'}, dimensions={1}, use_global_device_ids=true | all-gather | bytes 1179648 | tf_op jit(solution)/shard_map/all_gather | solution.py:124
  217.4 3.8 %fusion.30 = f32[2,192,4,2,128]{4,1,3,2,0:T(8,128)} fusion(bf16[2,192,4,2,128]{4,1,3,2,0:T(8,128)(2,1)S(1)} %all_gather.7, f32[192]{0:T(256)} %param.25, f32[2,4,2,128]{3,2,1,0:T(2,128)S(1)} %add_rsqrt_fusion.1, f32[2,4,2,128]{3,2,1,0:T(2,128)S(1)} %broadcast_multiply_fusion.1, bf16[768,192]{0,1:T(8,128)(2,1)S(1)} %copy-done, s32[]{:T(128)S(6)} %select_n.23, ...), kind=kOutput, calls=%fused_computation.151 | convolution fusion | flops 613023744 | bytes 2672640 | tf_op jit(solution)/shard_map/hc,lh...->lc.../dot_general | solution.py:54
  223.6 28.8 %reduce-scatter.5.cloned.1.call-done = f32[2,96,4,2,128]{4,1,3,2,0:T(8,128)} async-done(((f32[2,192,4,2,128]{4,1,3,2,0:T(8,128)}), f32[2,96,4,2,128]{4,1,3,2,0:T(8,128)}) %reduce-scatter.5.cloned.1.call-update) | async-done | bytes 786448 | tf_op jit(solution)/shard_map/reduce_scatter | solution.py:142
  (237 shorter events, 42.9 us)
Async XLA Ops:
  7.2 210.2 %copy-start = (bf16[768,192]{0,1:T(8,128)(2,1)S(1)}, bf16[768,192]{0,1:T(8,128)(2,1)}, u32[]{:S(2)}) copy-start(bf16[768,192]{0,1:T(8,128)(2,1)} %param.27) | copy-start | bytes 884740
  7.2 34.9 %copy-start.5 = (f32[4,4,2,128]{3,2,1,0:T(2,128)S(1)}, f32[4,4,2,128]{3,2,1,0:T(2,128)}, u32[]{:S(2)}) copy-start(f32[4,4,2,128]{3,2,1,0:T(2,128)} %param.19) | copy-start | bytes 49156
  7.2 40.4 %copy-start.85 = (f32[96]{0:T(128)S(1)}, f32[96]{0:T(128)}, u32[]{:S(2)}) copy-start(f32[96]{0:T(128)} %param.29) | copy-start | bytes 1156
  7.2 45.8 %copy-start.6 = (f32[4,64]{1,0:T(4,128)S(1)}, f32[4,64]{1,0:T(4,128)}, u32[]{:S(2)}) copy-start(f32[4,64]{1,0:T(4,128)} %param.28) | copy-start | bytes 3076
  8.5 34.2 %all-to-all-start.1 = ((f32[1,4,1,2,128]{4,1,2,0,3:T(4,128)}), f32[1,4,1,2,128]{4,1,2,0,3:T(4,128)S(1)}, u32[]{:S(2)}, u32[]{:S(2)}) async-start(f32[1,4,1,2,128]{4,1,2,0,3:T(4,128)} %multiply_bitcast_fusion), calls=%async_computation.2 | async-start | bytes 8192 | tf_op jit(solution)/shard_map/all_to_all | solution.py:102
  42.1 21.3 %copy-start.1 = (f32[2,64,4,256]{3,1,2,0:T(8,128)}, f32[2,64,4,256]{3,1,2,0:T(8,128)S(1)}, u32[]{:S(2)}) copy-start(f32[2,64,4,256]{3,1,2,0:T(8,128)S(1)} %slice.3334) | copy-start | bytes 1572868
  42.8 10.2 %all-to-all-start = ((f32[4,4,1,2,128]{4,1,0,2,3:T(4,128)}), f32[4,4,1,2,128]{4,1,0,2,3:T(4,128)S(1)}, u32[]{:S(2)}, u32[]{:S(2)}) async-start(f32[4,4,1,2,128]{4,1,0,2,3:T(4,128)} %bitcast.641), calls=%async_computation | async-start | bytes 32768 | tf_op jit(solution)/shard_map/all_to_all | solution.py:103
  47.6 173.6 %reduce-scatter.3.cloned.1.call-start = ((), (), s32[]{:S(2)}) async-start(), calls=%async_computation.4 | async-start | bytes 2359296 | tf_op jit(solution)/shard_map/reduce_scatter | solution.py:141
  53.4 8.7 %copy-start.3 = (f32[1,64,4,256]{3,1,2,0:T(8,128)}, f32[1,64,4,256]{3,1,2,0:T(8,128)S(1)}, u32[]{:S(2)}) copy-start(f32[1,64,4,256]{3,1,2,0:T(8,128)S(1)} %fusion.33) | copy-start | bytes 786436
  54.6 30.2 %collective-permute-start = (f32[3,64,3,256]{3,1,2,0:T(8,128)}, f32[3,64,3,256]{3,1,2,0:T(8,128)}, u32[]{:S(2)}, u32[]{:S(2)}) collective-permute-start(f32[3,64,3,256]{3,1,2,0:T(8,128)} %get-tuple-element.14), channel_id=1, source_target_pairs={{0,2},{2,4},{4,6},{6,8},{8,10},{10,12},{12,14},{14,16},{16,18},{18... | collective-permute-start | bytes 1769480 | tf_op jit(solution)/shard_map/ppermute | solution.py:13
  54.7 30.2 %collective-permute-start.1 = (f32[3,64,3,256]{3,1,2,0:T(8,128)}, f32[3,64,3,256]{3,1,2,0:T(8,128)}, u32[]{:S(2)}, u32[]{:S(2)}) collective-permute-start(f32[3,64,3,256]{3,1,2,0:T(8,128)} %get-tuple-element.15), channel_id=1, source_target_pairs={{2,0},{4,2},{6,4},{8,6},{10,8},{12,10},{14,12},{16,14},{18,16},{20... | collective-permute-start | bytes 1769480 | tf_op jit(solution)/shard_map/ppermute | solution.py:16
  64.8 5.5 %collective-permute-start.2 = (f32[2,96,4,2,3]{1,2,4,3,0:T(4,128)S(1)}, f32[2,96,4,2,3]{1,2,4,3,0:T(4,128)S(1)}, u32[]{:S(2)}, u32[]{:S(2)}) collective-permute-start(f32[2,96,4,2,3]{1,2,4,3,0:T(4,128)S(1)} %copy.32), channel_id=1, source_target_pairs={{0,128},{128,0},{1,129},{129,1},{2,130},{130,2},{3,131},{131,3},{4... | collective-permute-start | bytes 55304 | tf_op jit(solution)/shard_map/ppermute | solution.py:13
  66.1 5.4 %collective-permute-start.3 = (f32[2,96,4,2,3]{1,2,4,3,0:T(4,128)S(1)}, f32[2,96,4,2,3]{1,2,4,3,0:T(4,128)S(1)}, u32[]{:S(2)}, u32[]{:S(2)}) collective-permute-start(f32[2,96,4,2,3]{1,2,4,3,0:T(4,128)S(1)} %copy.33), channel_id=1, source_target_pairs={{128,0},{0,128},{129,1},{1,129},{130,2},{2,130},{131,3},{3,131},{1... | collective-permute-start | bytes 55304 | tf_op jit(solution)/shard_map/ppermute | solution.py:16
  76.7 56.2 %collective-permute-start.4 = (f32[2,96,3,2,134]{1,3,4,2,0:T(2,128)}, f32[2,96,3,2,134]{1,3,4,2,0:T(2,128)}, u32[]{:S(2)}, u32[]{:S(2)}) collective-permute-start(f32[2,96,3,2,134]{1,3,4,2,0:T(2,128)} %copy.36), channel_id=1, source_target_pairs={{0,2},{2,4},{4,6},{6,8},{8,10},{10,12},{12,14},{14,16},{16,18},{18... | collective-permute-start | bytes 1852424 | tf_op jit(solution)/shard_map/ppermute | solution.py:13
  79.1 8.3 %copy-start.50 = (f32[64]{0:T(128)S(1)}, f32[64]{0:T(128)}, u32[]{:S(2)}) copy-start(f32[64]{0:T(128)} %get-tuple-element.170) | copy-start | bytes 772
  79.1 8.3 %copy-start.51 = (f32[64]{0:T(128)S(1)}, f32[64]{0:T(128)}, u32[]{:S(2)}) copy-start(f32[64]{0:T(128)} %get-tuple-element.171) | copy-start | bytes 772
  79.1 8.3 %copy-start.52 = (f32[64]{0:T(128)S(1)}, f32[64]{0:T(128)}, u32[]{:S(2)}) copy-start(f32[64]{0:T(128)} %get-tuple-element.172) | copy-start | bytes 772
  79.2 8.3 %copy-start.53 = (f32[64]{0:T(128)S(1)}, f32[64]{0:T(128)}, u32[]{:S(2)}) copy-start(f32[64]{0:T(128)} %get-tuple-element.173) | copy-start | bytes 772
  79.2 8.3 %copy-start.54 = (f32[64]{0:T(128)S(1)}, f32[64]{0:T(128)}, u32[]{:S(2)}) copy-start(f32[64]{0:T(128)} %get-tuple-element.174) | copy-start | bytes 772
  79.2 8.3 %copy-start.55 = (f32[64]{0:T(128)S(1)}, f32[64]{0:T(128)}, u32[]{:S(2)}) copy-start(f32[64]{0:T(128)} %get-tuple-element.175) | copy-start | bytes 772
  79.2 8.3 %copy-start.56 = (f32[64]{0:T(128)S(1)}, f32[64]{0:T(128)}, u32[]{:S(2)}) copy-start(f32[64]{0:T(128)} %get-tuple-element.176) | copy-start | bytes 772
  79.2 8.3 %copy-start.57 = (f32[64]{0:T(128)S(1)}, f32[64]{0:T(128)}, u32[]{:S(2)}) copy-start(f32[64]{0:T(128)} %get-tuple-element.177) | copy-start | bytes 772
  79.5 55.8 %collective-permute-start.5 = (f32[2,96,3,2,134]{1,3,4,2,0:T(2,128)}, f32[2,96,3,2,134]{1,3,4,2,0:T(2,128)}, u32[]{:S(2)}, u32[]{:S(2)}) collective-permute-start(f32[2,96,3,2,134]{1,3,4,2,0:T(2,128)} %copy.37), channel_id=1, source_target_pairs={{2,0},{4,2},{6,4},{8,6},{10,8},{12,10},{14,12},{16,14},{18,16},{20... | collective-permute-start | bytes 1852424 | tf_op jit(solution)/shard_map/ppermute | solution.py:16
  132.6 119.8 %reduce-scatter.5.cloned.1.call-start = ((), (), s32[]{:S(2)}) async-start(), calls=%async_computation.5 | async-start | bytes 2359296 | tf_op jit(solution)/shard_map/reduce_scatter | solution.py:142
  (73 other events, 419.8 us)
Sparse Core Ops, SparseCore 0:
  132.7 28.2 reduce-scatter.2
  221.3 31.0 reduce-scatter.4
where the time goes:
time: 265 us; the launch traced here: 262 us
  other arithmetic  115 us (43%)
  local copies, waits for them, and re-layouts  44.3 us (17%)
  waiting for transfers between devices  36.1 us (14%)
  starting transfers between devices  25.1 us (9%)
  blocking collectives  16.9 us (6%)
  between operations  15.6 us (6%)
  matrix products  8.05 us (3%)
    convert_element_type x1, other arithmetic, per_device(): depthwise(edged, air_kernel, air_forced.shape).astype(jnp.bfloat16)  63.5 us
    convert_element_type x1, other arithmetic, per_device(): depthwise(rimmed, ocean_kernel, ocean_forced.shape).astype(jnp.bfloat16)  32.2 us
    reduce_scatter x1, waiting for transfers between devices, per_device(): lax.psum_scatter(air_part, 'ch', scatter_dimension=1, tiled=True)  28.8 us
    mul x16, local copies, waits for them, and re-layouts, depthwise(): summed = summed + weight * window  25.9 us
    ppermute x3, starting transfers between devices, padded_2(): lax.ppermute(lax.slice_in_dim(block, 0, width, axis=dim), axis, backward)  15.5 us
    all_gather x1, blocking collectives, per_device(): lax.all_gather(ocean_conv, 'ch', axis=1, tiled=True)  8.45 us
    all_gather x1, blocking collectives, per_device(): lax.all_gather(air_conv, 'ch', axis=1, tiled=True)  8.45 us
    dot_general x2, matrix products, feed_forward(): jnp.einsum('hc,lh...->lc...', down_proj, hidden, preferred_element_type=j...  7.63 us
  transfers between devices with their start and end apart: 10, of which 4 were waited for; matrix products, arithmetic and copies ran while one was open for 62% of the time, Pallas kernels for 0%

commit v1 on v0

v1 whole, which is shorter than its diff:
```python
import functools

import jax
import jax.numpy as jnp
from jax import lax
from jax.experimental import pallas as pl
from jax.experimental.pallas import tpu as pltpu
from jax.sharding import PartitionSpec as P

F32 = jnp.float32
BF16 = jnp.bfloat16
LANES = 128
VMEM = pl.BlockSpec(memory_space=pltpu.VMEM)


def lane_ids(rows):
    return lax.broadcasted_iota(jnp.int32, (rows, LANES), 1)


def call(kernel, out_shape, scratch, name, flops, moved, *args):
    return pl.pallas_call(
        kernel,
        out_shape=out_shape,
        in_specs=[VMEM] * len(args),
        out_specs=jax.tree.map(lambda _: VMEM, out_shape),
        scratch_shapes=scratch,
        name=name,
        cost_estimate=pl.CostEstimate(flops=flops, bytes_accessed=moved, transcendentals=0),
    )(*args)


def pack_kernel(mask_ref, temp_ref, flux_ref, air_ref, out_ref):
    comp = lax.axis_index("comp")
    band = mask_ref.shape[0]
    fields = flux_ref.shape[0]
    for k in range(fields):
        for j in range(band):
            out_ref[k * band + j : k * band + j + 1, :] = flux_ref[k, j, pl.ds(1 - comp, 1), :]
    temp = temp_ref[...] * mask_ref[...].astype(F32)
    base = fields * band
    for s in range(2):
        out_ref[base + s * band : base + (s + 1) * band, :] = temp[:, s * LANES : (s + 1) * LANES]
    base += 2 * band
    levels, channels = air_ref.shape[1], air_ref.shape[3]
    start = jnp.where(comp == 0, LANES - 8, 0)
    lane = lane_ids(channels)
    packed = jnp.zeros((channels, LANES), F32)
    for level in range(levels):
        for h in range(2):
            for j in range(band):
                idx = (level * 2 + h) * band + j
                rolled = pltpu.roll(
                    air_ref[h, level, j].astype(F32), lax.rem(8 * idx - start + LANES, LANES), 1
                )
                packed = jnp.where(lane // 8 == idx, rolled, packed)
    out_ref[base : base + channels, :] = packed


def force_kernel(
    mask_ref, temp_ref, flux_ref, got_ref, ocean_ref, air_ref, fw_ref, tw_ref,
    fo_ref, fa_ref, edge_ref, ow_ref, oe_ref, aw_ref, ae_ref,
):
    comp = lax.axis_index("comp")
    band = mask_ref.shape[0]
    fields = flux_ref.shape[0]
    o_levels, a_levels = ocean_ref.shape[1], air_ref.shape[1]
    channels = air_ref.shape[3]
    sea = mask_ref[...].astype(F32)
    temp = temp_ref[...] * sea
    weights = fw_ref[...]
    for s in range(2):
        for i in range(band):
            sea_row = sea[i : i + 1, s * LANES : (s + 1) * LANES]
            inject = None
            for k in range(fields):
                mine = flux_ref[k, i, pl.ds(comp, 1), :]
                row = jnp.where(comp == s, mine, got_ref[k * band + i : k * band + i + 1, :])
                term = weights[:, k : k + 1] * row
                inject = term if inject is None else inject + term
            for level in range(o_levels):
                value = ocean_ref[s, level, i].astype(F32)
                if level == 0:
                    value = value + inject
                value = value * sea_row
                fo_ref[s, level, i] = value
                small = value.astype(BF16)
                at = (s * o_levels + level) * (band - 1)
                if i < band - 1:
                    ow_ref[at + i] = small
                if i > 0:
                    oe_ref[at + i - 1] = small
    base = fields * band
    heat = tw_ref[...]
    start = jnp.where(comp == 0, 0, LANES - 8)
    lane = lane_ids(8)
    edge_temp = jnp.zeros((8, LANES), F32)
    for h in range(2):
        for j in range(band):
            mine = [temp[j : j + 1, s * LANES : (s + 1) * LANES] for s in range(2)]
            here = jnp.where(comp == 0, mine[0], mine[1])
            there = jnp.where(comp == 0, mine[1], mine[0])
            got_here = got_ref[pl.ds(base + comp * band + j, 1), :]
            got_there = got_ref[pl.ds(base + (1 - comp) * band + j, 1), :]
            row = jnp.where(comp == h, here, got_here)
            beyond = jnp.where(comp == h, there, got_there)
            idx = h * band + j
            rolled = pltpu.roll(
                jnp.broadcast_to(beyond, (8, LANES)), lax.rem(8 * idx - start + LANES, LANES), 1
            )
            edge_temp = jnp.where(lane // 8 == idx, rolled, edge_temp)
            for level in range(a_levels):
                value = air_ref[h, level, j].astype(F32)
                if level == 0:
                    value = value + heat * row
                fa_ref[h, level, j] = value
                small = value.astype(BF16)
                at = (h * a_levels + level) * (band - 1)
                if j < band - 1:
                    aw_ref[at + j] = small
                if j > 0:
                    ae_ref[at + j - 1] = small
    base += 2 * band
    edge = got_ref[base : base + channels, :] + heat * edge_temp[0:1, :]
    edge_ref[...] = edge
    last = 2 * a_levels * (band - 1)
    aw_ref[last] = edge.astype(BF16)
    ae_ref[last] = edge.astype(BF16)


def lat_swap(data_ref, edge_ref, count):
    levels, channels = data_ref.shape[1], data_ref.shape[3]
    lane = lane_ids(channels)
    for level in range(levels):
        for i in range(count):
            edge_ref[0, level, i] = jnp.where(lane < 64, data_ref[1, level, i], 0.0)
            edge_ref[1, level, i] = jnp.where(lane >= 64, data_ref[0, level, i], 0.0)


def unpack_edge(packed, idx, channels):
    comp = lax.axis_index("comp")
    start = jnp.where(comp == 0, 0, LANES - 8)
    rolled = pltpu.roll(packed, lax.rem(start - 8 * idx + 2 * LANES, LANES), 1)
    return jnp.where(lane_ids(channels) // 8 == start // 8, rolled, 0.0)


def convolve(data_ref, edge_ref, weight_ref, start_ref, out_ref, columns, band):
    levels, channels = data_ref.shape[1], data_ref.shape[3]
    lane = lane_ids(8)

    def step(at, carry):
        half = lax.rem(at, 2)
        rows = pl.ds(pl.multiple_of(at // 2 * 8, 8), 8)
        weight = weight_ref[rows, :]
        acc = [
            [None if start_ref is None else start_ref[half, level, i, rows] for i in range(band)]
            for level in range(levels)
        ]
        for d in range(7):
            off = d - 3
            shifted = {}
            for level in range(levels):
                for slot, x in enumerate(columns):
                    value = data_ref[half, level, slot, rows]
                    if off > 0:
                        beyond = edge_ref[half, level, slot, rows]
                        value = pltpu.roll(jnp.where(lane < off, beyond, value), LANES - off, 1)
                    elif off < 0:
                        beyond = edge_ref[half, level, slot, rows]
                        value = pltpu.roll(
                            jnp.where(lane >= LANES + off, beyond, value), -off, 1
                        )
                    shifted[level, x] = value
            for a in range(3):
                for b in range(7):
                    pairs = [
                        (level, i)
                        for level in range(levels)
                        for i in range(band)
                        if (level + a - 1, i + b - 3) in shifted
                    ]
                    if not pairs:
                        continue
                    tap = a * 49 + b * 7 + d
                    scale = jnp.broadcast_to(weight[:, tap : tap + 1], (8, LANES))
                    for level, i in pairs:
                        term = scale * shifted[level + a - 1, i + b - 3]
                        old = acc[level][i]
                        acc[level][i] = term if old is None else old + term
        for level in range(levels):
            for i in range(band):
                out_ref[half, level, i, rows] = acc[level][i]
        return carry

    lax.fori_loop(0, channels // 8 * 2, step, 0)


def own_ocean_kernel(data_ref, weight_ref, out_ref, edge_ref):
    band = data_ref.shape[2]
    lat_swap(data_ref, edge_ref, band)
    convolve(data_ref, edge_ref, weight_ref, None, out_ref, range(band), band)


def own_air_kernel(data_ref, packed_ref, weight_ref, out_ref, edge_ref):
    _, levels, band, channels, _ = data_ref.shape
    for h in range(2):
        for level in range(levels):
            for j in range(band):
                idx = (level * 2 + h) * band + j
                edge_ref[h, level, j] = unpack_edge(packed_ref[...], idx, channels)
    convolve(data_ref, edge_ref, weight_ref, None, out_ref, range(band), band)


def halo_columns(band):
    return [-3, -2, -1] + [band, band + 1, band + 2]


def halo_ocean_kernel(west_ref, east_ref, weight_ref, start_ref, out_ref, data_ref, edge_ref, acc_ref):
    _, levels, band, _, _ = start_ref.shape
    for s in range(2):
        for level in range(levels):
            for i in range(3):
                at = (s * levels + level) * 3 + i
                data_ref[s, level, i] = west_ref[at].astype(F32)
                data_ref[s, level, 3 + i] = east_ref[at].astype(F32)
    lat_swap(data_ref, edge_ref, 6)
    convolve(data_ref, edge_ref, weight_ref, start_ref, acc_ref, halo_columns(band), band)
    out_ref[...] = acc_ref[...].astype(BF16)


def halo_air_kernel(west_ref, east_ref, weight_ref, start_ref, out_ref, data_ref, edge_ref, acc_ref):
    _, levels, band, channels, _ = start_ref.shape
    lon = lax.axis_index("lon")
    swap_west = jnp.where(lon == 0, 1, 0)
    swap_east = jnp.where(lon == lax.axis_size("lon") - 1, 1, 0)
    last = 2 * levels * 3
    west_edge = west_ref[last].astype(F32)
    east_edge = east_ref[last].astype(F32)
    for h in range(2):
        west_h = jnp.abs(h - swap_west)
        east_h = jnp.abs(h - swap_east)
        for level in range(levels):
            for i in range(3):
                data_ref[h, level, i] = west_ref[(west_h * levels + level) * 3 + i].astype(F32)
                data_ref[h, level, 3 + i] = east_ref[(east_h * levels + level) * 3 + i].astype(F32)
                edge_ref[h, level, i] = unpack_edge(
                    west_edge, (level * 2 + west_h) * band + i + band - 3, channels
                )
                edge_ref[h, level, 3 + i] = unpack_edge(
                    east_edge, (level * 2 + east_h) * band + i, channels
                )
    convolve(data_ref, edge_ref, weight_ref, start_ref, acc_ref, halo_columns(band), band)
    out_ref[...] = acc_ref[...].astype(BF16)


def mlp_kernel(masked, *refs):
    own_ref, other_ref, gain_ref, up_ref, down_ref, forced_ref = refs[:6]
    mask_ref = refs[6] if masked else None
    out_ref, values_ref = refs[-2:]
    _, levels, band, channels, _ = own_ref.shape
    ch = lax.axis_index("ch")
    total = 2 * channels

    def step(at, carry):
        level = at // band
        i = lax.rem(at, band)
        mine = pl.ds(pl.multiple_of(ch * channels, channels), channels)
        theirs = pl.ds(pl.multiple_of((1 - ch) * channels, channels), channels)
        for s in range(2):
            lanes = slice(s * LANES, (s + 1) * LANES)
            values_ref[mine, lanes] = own_ref[s, level, i].astype(F32)
            values_ref[theirs, lanes] = other_ref[s, level, i].astype(F32)
        values = values_ref[...]
        center = jnp.sum(values, axis=0, keepdims=True) * (1.0 / total)
        values = values - center
        spread = jnp.sum(values * values, axis=0, keepdims=True) * (1.0 / total)
        normed = (values * lax.rsqrt(spread + 1e-06) * gain_ref[...]).astype(BF16)
        raw = jnp.dot(up_ref[...], normed, preferred_element_type=F32)
        inner = raw * (0.7978845608028654 + 0.035677408136300125 * (raw * raw))
        half = 0.5 * raw
        hidden = (half + half * jnp.tanh(inner)).astype(BF16)
        down = down_ref[mine, :]
        if masked:
            mask = mask_ref[...]
            picked = lax.broadcasted_iota(jnp.int32, mask.shape, 0) == i
            sea = jnp.sum(jnp.where(picked, mask.astype(F32), 0.0), axis=0, keepdims=True)
        update = jnp.dot(down, hidden, preferred_element_type=F32).astype(BF16).astype(F32)
        for s in range(2):
            lanes = slice(s * LANES, (s + 1) * LANES)
            result = forced_ref[s, level, i] + update[:, lanes]
            if masked:
                result = result * sea[:, lanes]
            out_ref[s, level, i] = result.astype(BF16)
        return carry

    lax.fori_loop(0, levels * band, step, 0)


def ring(count, step):
    return [(i, (i + step) % count) for i in range(count)]


def per_device(
    ocean_state, ocean_mask, air_state, surface_temp, air_fluxes, ocean_kernel, ocean_gain, ocean_up,
    ocean_down, air_kernel, air_gain, air_up, air_down, flux_weight, temp_weight,
):
    o_levels, o_ch, band, lats = ocean_state.shape
    a_levels, a_ch = air_state.shape[:2]
    fields = air_fluxes.shape[0]
    shape = jax.ShapeDtypeStruct

    ocean_grid = jnp.transpose(
        ocean_state.reshape(o_levels, o_ch, band, 2, LANES), (3, 0, 2, 1, 4)
    )
    air_grid = jnp.transpose(air_state, (3, 0, 2, 1, 4))
    o_grid = (2, o_levels, band, o_ch, LANES)
    a_grid = (2, a_levels, band, a_ch, LANES)

    rows = fields * band + 2 * band + a_ch
    packed = call(
        pack_kernel, shape((rows, LANES), F32), [], "pack", 10**5, 10**6,
        ocean_mask, surface_temp, air_fluxes, air_grid,
    )
    got = lax.ppermute(packed, "comp", ring(2, 1))
    o_rim = (2 * o_levels * 3, o_ch, LANES)
    a_rim = (2 * a_levels * 3 + 1, a_ch, LANES)
    ocean_forced, air_forced, edge, o_west, o_east, a_west, a_east = call(
        force_kernel,
        (
            shape(o_grid, F32), shape(a_grid, F32), shape((a_ch, LANES), F32),
            shape(o_rim, BF16), shape(o_rim, BF16), shape(a_rim, BF16), shape(a_rim, BF16),
        ),
        [], "force", 10**6, 4 * 10**6,
        ocean_mask, surface_temp, air_fluxes, got, ocean_grid, air_grid,
        flux_weight.T, temp_weight[:, None],
    )
    bands = lax.axis_size("comp") * lax.axis_size("lon")
    lons = lax.axis_size("lon")
    from_west_o = lax.ppermute(o_east, ("comp", "lon"), ring(bands, 1))
    from_east_o = lax.ppermute(o_west, ("comp", "lon"), ring(bands, -1))
    from_west_a = lax.ppermute(a_east, "lon", ring(lons, 1))
    from_east_a = lax.ppermute(a_west, "lon", ring(lons, -1))

    o_weight = ocean_kernel.reshape(o_ch, -1)
    a_weight = air_kernel.reshape(a_ch, -1)
    o_own = call(
        own_ocean_kernel, shape(o_grid, F32), [pltpu.VMEM(o_grid, F32)], "own_ocean",
        3 * 10**9, 10**6, ocean_forced, o_weight,
    )
    a_own = call(
        own_air_kernel, shape(a_grid, F32), [pltpu.VMEM(a_grid, F32)], "own_air",
        3 * 10**9, 10**6, air_forced, edge, a_weight,
    )
    o_six = (2, o_levels, 6, o_ch, LANES)
    a_six = (2, a_levels, 6, a_ch, LANES)
    o_conv = call(
        halo_ocean_kernel, shape(o_grid, BF16),
        [pltpu.VMEM(o_six, F32), pltpu.VMEM(o_six, F32), pltpu.VMEM(o_grid, F32)], "halo_ocean",
        2 * 10**9, 10**6, from_west_o, from_east_o, o_weight, o_own,
    )
    o_other = lax.ppermute(o_conv, "ch", ring(2, 1))
    a_conv = call(
        halo_air_kernel, shape(a_grid, BF16),
        [pltpu.VMEM(a_six, F32), pltpu.VMEM(a_six, F32), pltpu.VMEM(a_grid, F32)], "halo_air",
        2 * 10**9, 10**6, from_west_a, from_east_a, a_weight, a_own,
    )
    a_other = lax.ppermute(a_conv, "ch", ring(2, 1))

    o_next = call(
        functools.partial(mlp_kernel, True), shape(o_grid, BF16),
        [pltpu.VMEM((2 * o_ch, 2 * LANES), F32)], "mlp_ocean", 10**9, 3 * 10**6,
        o_conv, o_other, ocean_gain[:, None], ocean_up.T, ocean_down.T, ocean_forced, ocean_mask,
    )
    a_next = call(
        functools.partial(mlp_kernel, False), shape(a_grid, BF16),
        [pltpu.VMEM((2 * a_ch, 2 * LANES), F32)], "mlp_air", 10**9, 3 * 10**6,
        a_conv, a_other, air_gain[:, None], air_up.T, air_down.T, air_forced,
    )
    ocean_next = jnp.transpose(o_next, (1, 3, 2, 0, 4)).reshape(ocean_state.shape)
    air_next = jnp.transpose(a_next, (1, 3, 2, 0, 4))
    return (ocean_next, air_next)


def solution(mesh):
    in_specs = (
        P(None, "ch", ("comp", "lon"), None),
        P(("comp", "lon"), None),
        P(None, "ch", "lon", None, "comp"),
        P(("comp", "lon"), None),
        P(None, "lon", None, "comp"),
        P("ch", None, None, None),
        P(),
        P(),
        P(),
        P("ch", None, None, None),
        P(),
        P(),
        P(),
        P(None, "ch"),
        P("ch"),
    )
    out_specs = (P(None, "ch", ("comp", "lon"), None), P(None, "ch", "lon", None, "comp"))
    return jax.shard_map(
        per_device, mesh=mesh, in_specs=in_specs, out_specs=out_specs, check_vma=False
    )
```

time: 265 us -> 104 us (0.39); the launches traced: 262 us -> 103 us
  other arithmetic: 115 us -> 0 us
  Pallas kernels: 0 us -> 62.7 us
  waiting for transfers between devices: 36.1 us -> 0.02 us
  local copies, waits for them, and re-layouts: 44.3 us -> 20.8 us
  blocking collectives: 16.9 us -> 0 us
  between operations: 15.6 us -> 0.71 us
  matrix products: 8.05 us -> 0 us
  starting transfers between devices: 25.1 us -> 19 us
    convert_element_type x7 -> x0, other arithmetic: 101 us -> none  [the longest x1 63.5 us: per_device(): depthwise(edged, air_kernel, air_forced.shape).astype(jnp.bfloat16)]
    pallas_call x0 -> x8, Pallas kernels: none -> 62.7 us  [call(): pl.pallas_call(kernel, out_shape=out_shape, in_specs=[VMEM] * len(args),...]
    reduce_scatter x2 -> x0, waiting for transfers between devices: 28.9 us -> none  [the longest x1 28.8 us: per_device(): lax.psum_scatter(air_part, 'ch', scatter_dimension=1, tiled=True)]
    mul x17 -> x0, local copies, waits for them, and re-layouts: 25.9 us -> none  [the longest x16 25.9 us: depthwise(): summed = summed + weight * window]
    all_gather x2 -> x0, blocking collectives: 16.9 us -> none  [the longest x1 8.45 us: per_device(): lax.all_gather(ocean_conv, 'ch', axis=1, tiled=True)]
    unnamed x177 -> x42, local copies, waits for them, and re-layouts: 3.13 us -> 16.1 us
    slice x8 -> x0, local copies, waits for them, and re-layouts: 9.89 us -> none  [the longest x4 6.71 us: padded_2(): lax.slice_in_dim(block, block.shape[dim] - width, None, axis=dim)]
    all_to_all x2 -> x0, starting transfers between devices: 8.36 us -> none  [the longest x1 4.8 us: per_device(): lax.all_to_all(sent_flux, 'comp', split_axis=3, concat_axis=2, tiled=True)]
  transfers between devices with their start and end apart: 10 -> 7, of which waited for: 4 -> 0; matrix products, arithmetic and copies ran while one was open for 62% -> 10% of each run, Pallas kernels for 0% -> 49%
where the time goes in v1:
time: 104 us; the launch traced here: 103 us
  Pallas kernels  62.7 us (60%)
  local copies, waits for them, and re-layouts  20.8 us (20%)
  starting transfers between devices  19 us (18%)
    pallas_call x8, Pallas kernels, call(): pl.pallas_call(kernel, out_shape=out_shape, in_specs=[VMEM] * len(args),...  62.7 us
    unnamed x42, local copies, waits for them, and re-layouts  16.1 us
    ppermute x1, starting transfers between devices, per_device(): from_east_o = lax.ppermute(o_west, ('comp', 'lon'), ring(bands, -1))  7.47 us
    ppermute x1, starting transfers between devices, per_device(): from_east_a = lax.ppermute(a_west, 'lon', ring(lons, -1))  7.25 us
    ppermute x1, starting transfers between devices, per_device(): got = lax.ppermute(packed, 'comp', ring(2, 1))  2.3 us
  transfers between devices with their start and end apart: 7, of which 0 were waited for; matrix products, arithmetic and copies ran while one was open for 10% of the time, Pallas kernels for 49%

profile of v1, /device:TPU:8, one launch (start us, length us, event | category | flops | bytes accessed | tf_op | source)
XLA Modules:
  0.0 103.3 jit_solution(2987011848108123514)
XLA Ops:
  0.6 1.8 %copy.51 = bf16[2,96,4,2,128]{4,1,2,0,3:T(8,128)(2,1)} copy(bf16[2,96,4,2,128]{4,3,2,1,0:T(2,128)(2,1)} %param.17) | data formatting | bytes 786432 | tf_op args[2]
  2.4 1.9 %pack.1 = f32[120,128]{1,0:T(8,128)} custom-call(s32[4,256]{1,0:T(4,128)} %refs_6_.1, f32[4,256]{1,0:T(4,128)} %temp_ref.3, f32[4,4,2,128]{3,2,1,0:T(2,128)} %flux_ref.3, bf16[2,2,4,96,128]{4,3,2,1,0:T(8,128)(2,1)} %bitcast.20), custom_call_target="tpu_custom_call" | custom-call | flops 100000 | bytes 1000000 | tf_op jit(solution)/shard_map/pack/pallas_call | solution.py:21
  4.3 2.3 %collective-permute-start = (f32[120,128]{1,0:T(8,128)}, f32[120,128]{1,0:T(8,128)S(1)}, u32[]{:S(2)}, u32[]{:S(2)}) collective-permute-start(f32[120,128]{1,0:T(8,128)} %pack.1), channel_id=1, source_target_pairs={{0,128},{128,0},{1,129},{129,1},{2,130},{130,2},{3,131},{131,3},{4... | collective-permute-start | bytes 184328 | tf_op jit(solution)/shard_map/ppermute | solution.py:323
  6.8 0.8 copy.50
  11.3 3.1 %force.1 = (f32[2,3,4,64,128]{4,3,2,1,0:T(8,128)}, f32[2,2,4,96,128]{4,3,2,1,0:T(8,128)}, f32[96,128]{1,0:T(8,128)}, bf16[18,64,128]{2,1,0:T(8,128)(2,1)}, bf16[...) custom-call(s32[4,256]{1,0:T(4,128)} %refs_6_.1, f32[4,256]{1,0:T(4,128)} %temp_ref.3, ...), custom_call_target="tpu_custom_call" | custom-call | flops 1000000 | bytes 4000000 | tf_op jit(solution)/shard_map/force/pallas_call | solution.py:21
  14.4 7.3 %collective-permute-start.5 = (bf16[13,96,128]{2,1,0:T(8,128)(2,1)}, bf16[13,96,128]{2,1,0:T(8,128)(2,1)S(1)}, u32[]{:S(2)}, u32[]{:S(2)}) collective-permute-start(bf16[13,96,128]{2,1,0:T(8,128)(2,1)} %get-tuple-element.13), channel_id=1, source_target_pairs={{0,126},{2,0},{4,2},{6,4},{8,6},{10,8},{12,10},{14,12},{16,14},{18... | collective-permute-start | bytes 958472 | tf_op jit(solution)/shard_map/ppermute | solution.py:341
  21.7 7.5 %collective-permute-start.2 = (bf16[18,64,128]{2,1,0:T(8,128)(2,1)}, bf16[18,64,128]{2,1,0:T(8,128)(2,1)S(1)}, u32[]{:S(2)}, u32[]{:S(2)}) collective-permute-start(bf16[18,64,128]{2,1,0:T(8,128)(2,1)} %get-tuple-element.10), channel_id=1, source_target_pairs={{0,254},{2,0},{4,2},{6,4},{8,6},{10,8},{12,10},{14,12},{16,14},{18... | collective-permute-start | bytes 884744 | tf_op jit(solution)/shard_map/ppermute | solution.py:339
  29.1 8.9 %own_ocean.1.start_ref = f32[2,3,4,64,128]{4,3,2,1,0:T(8,128)} custom-call(f32[2,3,4,64,128]{4,3,2,1,0:T(8,128)} %get-tuple-element.11.data_ref.refs_5_, f32[64,147]{1,0:T(8,128)} %copy.33.weight_ref), custom_call_target="tpu_custom_call" | custom-call | flops 3000000000 | bytes 1000000 | tf_op jit(solution)/shard_map/own_ocean/pallas_call | solution.py:21
  38.1 11.8 %own_air.1.start_ref = f32[2,2,4,96,128]{4,3,2,1,0:T(8,128)} custom-call(f32[2,2,4,96,128]{4,3,2,1,0:T(8,128)} %get-tuple-element.14.data_ref.refs_5_, f32[96,128]{1,0:T(8,128)} %get-tuple-element.15.packed_ref, f32[96,147]{1,0:T(8,128)} %copy.39.weight_ref), custom_call_target="tpu_custom_call" | custom-call | flops 3000000000 | bytes 1000000 | tf_op jit(solution)/shard_map/own_air/pallas_call | solution.py:21
  51.3 9.2 %halo_ocean.1.refs_0_ = bf16[2,3,4,64,128]{4,3,2,1,0:T(8,128)(2,1)} custom-call(bf16[18,64,128]{2,1,0:T(8,128)(2,1)} %copy-done.15, bf16[18,64,128]{2,1,0:T(8,128)(2,1)} %copy-done.16, f32[64,147]{1,0:T(8,128)} %copy.33.weight_ref, f32[2,3,4,64,128]{4,3,2,1,0:T(8,128)} %own_ocean.1.start_ref), custom_call_target="tpu_custom_call" | custom-call | flops 2000000000 | bytes 1000000 | tf_op jit(solution)/shard_map/halo_ocean/pallas_call | solution.py:21
  60.5 1.3 %collective-permute-start.3 = (bf16[2,3,4,64,128]{4,3,2,1,0:T(8,128)(2,1)}, bf16[2,3,4,64,128]{4,3,2,1,0:T(8,128)(2,1)S(1)}, u32[]{:S(2)}, u32[]{:S(2)}) collective-permute-start(bf16[2,3,4,64,128]{4,3,2,1,0:T(8,128)(2,1)} %halo_ocean.1.refs_0_), channel_id=1, source_target_pairs={{0,1},{1,0},{2,3},{3,2},{4,5},{5,4},{6,7},{7,6},{8,9},{9,8},{10,11... | collective-permute-start | bytes 1179656 | tf_op jit(solution)/shard_map/ppermute | solution.py:360
  63.3 11.6 %halo_air.1.refs_0_ = bf16[2,2,4,96,128]{4,3,2,1,0:T(8,128)(2,1)} custom-call(bf16[13,96,128]{2,1,0:T(8,128)(2,1)} %copy-done.13, bf16[13,96,128]{2,1,0:T(8,128)(2,1)} %copy-done.14, f32[96,147]{1,0:T(8,128)} %copy.39.weight_ref, f32[2,2,4,96,128]{4,3,2,1,0:T(8,128)} %own_air.1.start_ref), custom_call_target="tpu_custom_call" | custom-call | flops 2000000000 | bytes 1000000 | tf_op jit(solution)/shard_map/halo_air/pallas_call | solution.py:21
  75.6 1.0 copy.40
  77.2 0.8 copy.41.refs_2_
  78.0 0.8 copy.34
  78.9 0.8 copy.35
  80.3 0.7 copy.36.refs_2_
  81.1 0.7 copy-done.11
  81.8 8.6 %mlp_ocean.1 = bf16[2,3,4,64,128]{4,3,2,1,0:T(8,128)(2,1)} custom-call(bf16[2,3,4,64,128]{4,3,2,1,0:T(8,128)(2,1)} %halo_ocean.1.refs_0_, bf16[2,3,4,64,128]{4,3,2,1,0:T(8,128)(2,1)} %copy-done.11, f32[128,1]{1,0:T(8,128)} %copy.36.refs_2_, bf16[512,128]{1,0:T(8,128)(2,1)} %bitcast.26, bf16[128,512]{1,0:T(8,128)(2,1)} %bitcast.27, ...), custom_call_target="tpu_custom_call" | custom-call | flops 1000000000 | bytes 3000000 | tf_op jit(solution)/shard_map/mlp_ocean/pallas_call | solution.py:21
  90.4 1.4 %copy.46 = bf16[3,64,4,2,128]{4,3,2,1,0:T(2,128)(2,1)S(1)} copy(bf16[3,64,4,2,128]{4,1,2,0,3:T(8,128)(2,1)} %bitcast.23) | data formatting | bytes 786432
  91.8 1.0 reshape.21
  92.8 0.7 copy-done.12
  93.6 7.6 %mlp_air.1 = bf16[2,2,4,96,128]{4,3,2,1,0:T(8,128)(2,1)} custom-call(bf16[2,2,4,96,128]{4,3,2,1,0:T(8,128)(2,1)} %halo_air.1.refs_0_, bf16[2,2,4,96,128]{4,3,2,1,0:T(8,128)(2,1)} %copy-done.12, f32[192,1]{1,0:T(8,128)} %copy.41.refs_2_, bf16[768,192]{1,0:T(8,128)(2,1)} %bitcast.25, bf16[192,768]{1,0:T(8,128)(2,1)} %bitcast.32, ...), custom_call_target="tpu_custom_call" | custom-call | flops 1000000000 | bytes 3000000 | tf_op jit(solution)/shard_map/mlp_air/pallas_call | solution.py:21
  101.2 2.1 %copy.43 = bf16[2,96,4,2,128]{4,3,2,1,0:T(2,128)(2,1)} copy(bf16[2,96,4,2,128]{4,1,2,0,3:T(8,128)(2,1)} %bitcast.24) | data formatting | bytes 786432
  (49 shorter events, 8.9 us)
Async XLA Ops:
  2.4 4.2 %copy-start = (bf16[3,64,4,256]{3,2,1,0:T(4,128)(2,1)S(1)}, bf16[3,64,4,256]{3,2,1,0:T(4,128)(2,1)}, u32[]{:S(2)}) copy-start(bf16[3,64,4,256]{3,2,1,0:T(4,128)(2,1)} %param.15) | copy-start | bytes 1179652
  4.3 6.4 %collective-permute-start = (f32[120,128]{1,0:T(8,128)}, f32[120,128]{1,0:T(8,128)S(1)}, u32[]{:S(2)}, u32[]{:S(2)}) collective-permute-start(f32[120,128]{1,0:T(8,128)} %pack.1), channel_id=1, source_target_pairs={{0,128},{128,0},{1,129},{129,1},{2,130},{130,2},{3,131},{131,3},{4... | collective-permute-start | bytes 184328 | tf_op jit(solution)/shard_map/ppermute | solution.py:323
  6.8 0.9 copy-start.9
  6.8 1.6 %copy-start.7 = (f32[4,64]{1,0:T(4,128)S(1)}, f32[4,64]{1,0:T(4,128)}, u32[]{:S(2)}) copy-start(f32[4,64]{1,0:T(4,128)} %param.28) | copy-start | bytes 3076
  7.6 1.4 %copy-start.4 = (f32[96,3,7,7]{0,3,2,1:T(8,128)S(1)}, f32[96,3,7,7]{0,3,2,1:T(8,128)}, u32[]{:S(2)}) copy-start(f32[96,3,7,7]{0,3,2,1:T(8,128)} %param.24) | copy-start | bytes 169348
  9.1 0.9 copy-start.5
  10.7 0.6 copy-start.6
  14.4 47.4 %collective-permute-start.4 = (bf16[13,96,128]{2,1,0:T(8,128)(2,1)}, bf16[13,96,128]{2,1,0:T(8,128)(2,1)S(1)}, u32[]{:S(2)}, u32[]{:S(2)}) collective-permute-start(bf16[13,96,128]{2,1,0:T(8,128)(2,1)} %get-tuple-element.12), channel_id=1, source_target_pairs={{0,2},{2,4},{4,6},{6,8},{8,10},{10,12},{12,14},{14,16},{16,18},{18... | collective-permute-start | bytes 958472 | tf_op jit(solution)/shard_map/ppermute | solution.py:340
  14.4 47.4 %collective-permute-start.5 = (bf16[13,96,128]{2,1,0:T(8,128)(2,1)}, bf16[13,96,128]{2,1,0:T(8,128)(2,1)S(1)}, u32[]{:S(2)}, u32[]{:S(2)}) collective-permute-start(bf16[13,96,128]{2,1,0:T(8,128)(2,1)} %get-tuple-element.13), channel_id=1, source_target_pairs={{0,126},{2,0},{4,2},{6,4},{8,6},{10,8},{12,10},{14,12},{16,14},{18... | collective-permute-start | bytes 958472 | tf_op jit(solution)/shard_map/ppermute | solution.py:341
  21.7 28.2 %collective-permute-start.1 = (bf16[18,64,128]{2,1,0:T(8,128)(2,1)}, bf16[18,64,128]{2,1,0:T(8,128)(2,1)S(1)}, u32[]{:S(2)}, u32[]{:S(2)}) collective-permute-start(bf16[18,64,128]{2,1,0:T(8,128)(2,1)} %get-tuple-element.9), channel_id=1, source_target_pairs={{0,2},{2,4},{4,6},{6,8},{8,10},{10,12},{12,14},{14,16},{16,18},{18... | collective-permute-start | bytes 884744 | tf_op jit(solution)/shard_map/ppermute | solution.py:338
  21.7 28.2 %collective-permute-start.2 = (bf16[18,64,128]{2,1,0:T(8,128)(2,1)}, bf16[18,64,128]{2,1,0:T(8,128)(2,1)S(1)}, u32[]{:S(2)}, u32[]{:S(2)}) collective-permute-start(bf16[18,64,128]{2,1,0:T(8,128)(2,1)} %get-tuple-element.10), channel_id=1, source_target_pairs={{0,254},{2,0},{4,2},{6,4},{8,6},{10,8},{12,10},{14,12},{16,14},{18... | collective-permute-start | bytes 884744 | tf_op jit(solution)/shard_map/ppermute | solution.py:339
  49.9 0.7 copy-start.15
  50.6 0.7 copy-start.16
  60.5 15.1 %copy-start.1 = (bf16[192,768]{1,0:T(8,128)(2,1)S(1)}, bf16[192,768]{1,0:T(8,128)(2,1)}, u32[]{:S(2)}) copy-start(bf16[192,768]{1,0:T(8,128)(2,1)} %param.26) | copy-start | bytes 884740
  60.5 20.6 %collective-permute-start.3 = (bf16[2,3,4,64,128]{4,3,2,1,0:T(8,128)(2,1)}, bf16[2,3,4,64,128]{4,3,2,1,0:T(8,128)(2,1)S(1)}, u32[]{:S(2)}, u32[]{:S(2)}) collective-permute-start(bf16[2,3,4,64,128]{4,3,2,1,0:T(8,128)(2,1)} %halo_ocean.1.refs_0_), channel_id=1, source_target_pairs={{0,1},{1,0},{2,3},{3,2},{4,5},{5,4},{6,7},{7,6},{8,9},{9,8},{10,11... | collective-permute-start | bytes 1179656 | tf_op jit(solution)/shard_map/ppermute | solution.py:360
  61.8 0.7 copy-start.13
  62.5 0.7 copy-start.14
  74.9 17.9 %collective-permute-start.6 = (bf16[2,2,4,96,128]{4,3,2,1,0:T(8,128)(2,1)}, bf16[2,2,4,96,128]{4,3,2,1,0:T(8,128)(2,1)S(1)}, u32[]{:S(2)}, u32[]{:S(2)}) collective-permute-start(bf16[2,2,4,96,128]{4,3,2,1,0:T(8,128)(2,1)} %halo_air.1.refs_0_), channel_id=1, source_target_pairs={{0,1},{1,0},{2,3},{3,2},{4,5},{5,4},{6,7},{7,6},{8,9},{9,8},{10,11... | collective-permute-start | bytes 1179656 | tf_op jit(solution)/shard_map/ppermute | solution.py:366
  75.6 2.4 %copy-start.2 = (bf16[128,512]{1,0:T(8,128)(2,1)S(1)}, bf16[128,512]{1,0:T(8,128)(2,1)}, u32[]{:S(2)}) copy-start(bf16[128,512]{1,0:T(8,128)(2,1)} %param.22) | copy-start | bytes 393220
  76.5 0.7 copy-start.8
  78.0 0.9 copy-start.3
  79.7 0.7 copy-start.10
  81.1 0.7 copy-start.11
  92.8 0.7 copy-start.12

commit v2 on v1

--- a/solution.py
+++ b/solution.py
@@ -58,7 +58,7 @@
 
 def force_kernel(
     mask_ref, temp_ref, flux_ref, got_ref, ocean_ref, air_ref, fw_ref, tw_ref,
-    fo_ref, fa_ref, edge_ref, ow_ref, oe_ref, aw_ref, ae_ref,
+    fo_ref, fa_ref, ob_ref, ab_ref, edge_ref, ow_ref, oe_ref, aw_ref, ae_ref,
 ):
     comp = lax.axis_index("comp")
     band = mask_ref.shape[0]
@@ -82,8 +82,10 @@
                 if level == 0:
                     value = value + inject
                 value = value * sea_row
-                fo_ref[s, level, i] = value
+                if level == 0:
+                    fo_ref[s, i] = value
                 small = value.astype(BF16)
+                ob_ref[s, level, i] = small
                 at = (s * o_levels + level) * (band - 1)
                 if i < band - 1:
                     ow_ref[at + i] = small
@@ -112,8 +114,10 @@
                 value = air_ref[h, level, j].astype(F32)
                 if level == 0:
                     value = value + heat * row
-                fa_ref[h, level, j] = value
+                if level == 0:
+                    fa_ref[h, j] = value
                 small = value.astype(BF16)
+                ab_ref[h, level, j] = small
                 at = (h * a_levels + level) * (band - 1)
                 if j < band - 1:
                     aw_ref[at + j] = small
@@ -127,134 +131,188 @@
     ae_ref[last] = edge.astype(BF16)
 
 
-def lat_swap(data_ref, edge_ref, count):
-    levels, channels = data_ref.shape[1], data_ref.shape[3]
-    lane = lane_ids(channels)
-    for level in range(levels):
-        for i in range(count):
-            edge_ref[0, level, i] = jnp.where(lane < 64, data_ref[1, level, i], 0.0)
-            edge_ref[1, level, i] = jnp.where(lane >= 64, data_ref[0, level, i], 0.0)
-
-
-def unpack_edge(packed, idx, channels):
+def unpack_edge(packed, idx, shift, lane):
     comp = lax.axis_index("comp")
-    start = jnp.where(comp == 0, 0, LANES - 8)
+    start = lax.rem(jnp.where(comp == 0, 0, LANES - 8) + shift, LANES)
     rolled = pltpu.roll(packed, lax.rem(start - 8 * idx + 2 * LANES, LANES), 1)
-    return jnp.where(lane_ids(channels) // 8 == start // 8, rolled, 0.0)
-
-
-def convolve(data_ref, edge_ref, weight_ref, start_ref, out_ref, columns, band):
-    levels, channels = data_ref.shape[1], data_ref.shape[3]
+    return jnp.where(lane // 8 == start // 8, rolled, 0.0)
+
+
+TAPS = 7
+
+
+def toeplitz_kernel(taps_ref, out_ref):
+    groups, pairs, rows, depth = out_ref.shape
+    channels = groups * 8
+    levels = pairs // 2
+    window = taps_ref.shape[1]
+    taps = taps_ref[...].astype(BF16)
+    row = lax.broadcasted_iota(jnp.int32, (window, depth), 0)
+    lane = lax.broadcasted_iota(jnp.int32, (window, depth), 1)
+    from_level = lane // 80
+    from_lon = lane // 8 - from_level * 10
+    same = (lax.broadcasted_iota(jnp.int32, (8, depth), 1) & 7) == lax.broadcasted_iota(
+        jnp.int32, (8, depth), 0
+    )
+
+    def step(pair, carry):
+        level = pair // 2
+        parts = []
+        for side in range(2):
+            a = from_level - level + 1
+            b = from_lon - (lax.rem(pair, 2) * 2 + side)
+            hit = (
+                (from_level < levels)
+                & (a >= 0) & (a <= 2) & (b >= 0) & (b < TAPS) & (a * TAPS + b == row)
+            )
+            choose = jnp.where(hit, 1.0, 0.0).astype(BF16)
+            parts.append(jnp.dot(taps, choose, preferred_element_type=F32))
+        for g in range(groups):
+            tiles = [
+                jnp.where(same, part[d * channels + g * 8 : d * channels + g * 8 + 8], 0.0)
+                for part in parts
+                for d in range(TAPS)
+            ]
+            out_ref[g, pair] = jnp.concatenate(tiles, axis=0).astype(BF16)
+        return carry
+
+    lax.fori_loop(0, pairs, step, 0)
+
+
+def conv_ocean_kernel(own_ref, west_ref, east_ref, matrix_ref, out_ref, product_ref):
+    _, levels, band, count, _ = own_ref.shape
+    depth = matrix_ref.shape[-1]
     lane = lane_ids(8)
-
-    def step(at, carry):
-        half = lax.rem(at, 2)
-        rows = pl.ds(pl.multiple_of(at // 2 * 8, 8), 8)
-        weight = weight_ref[rows, :]
-        acc = [
-            [None if start_ref is None else start_ref[half, level, i, rows] for i in range(band)]
-            for level in range(levels)
-        ]
-        for d in range(7):
-            off = d - 3
-            shifted = {}
+    for sub in range(count // 8):
+        rows = slice(sub * 8, sub * 8 + 8)
+        halves = []
+        for s in range(2):
+            tiles = []
             for level in range(levels):
-                for slot, x in enumerate(columns):
-                    value = data_ref[half, level, slot, rows]
-                    if off > 0:
-                        beyond = edge_ref[half, level, slot, rows]
-                        value = pltpu.roll(jnp.where(lane < off, beyond, value), LANES - off, 1)
-                    elif off < 0:
-                        beyond = edge_ref[half, level, slot, rows]
-                        value = pltpu.roll(
-                            jnp.where(lane >= LANES + off, beyond, value), -off, 1
-                        )
-                    shifted[level, x] = value
-            for a in range(3):
-                for b in range(7):
-                    pairs = [
-                        (level, i)
-                        for level in range(levels)
-                        for i in range(band)
-                        if (level + a - 1, i + b - 3) in shifted
-                    ]
-                    if not pairs:
-                        continue
-                    tap = a * 49 + b * 7 + d
-                    scale = jnp.broadcast_to(weight[:, tap : tap + 1], (8, LANES))
-                    for level, i in pairs:
-                        term = scale * shifted[level + a - 1, i + b - 3]
-                        old = acc[level][i]
-                        acc[level][i] = term if old is None else old + term
+                at = (s * levels + level) * 3
+                tiles += [west_ref[at + i, rows].astype(F32) for i in range(3)]
+                tiles += [own_ref[s, level, i, rows].astype(F32) for i in range(band)]
+                tiles += [east_ref[at + i, rows].astype(F32) for i in range(3)]
+            if depth > len(tiles) * 8:
+                tiles.append(jnp.zeros((depth - len(tiles) * 8, LANES), F32))
+            halves.append(jnp.concatenate(tiles, axis=0))
+        data = jnp.concatenate(halves, axis=1).astype(BF16)
+        matrix = matrix_ref[sub].reshape(-1, depth)
+        product_ref[...] = jnp.dot(matrix, data, preferred_element_type=F32)
         for level in range(levels):
             for i in range(band):
-                out_ref[half, level, i, rows] = acc[level][i]
-        return carry
-
-    lax.fori_loop(0, channels // 8 * 2, step, 0)
-
-
-def own_ocean_kernel(data_ref, weight_ref, out_ref, edge_ref):
-    band = data_ref.shape[2]
-    lat_swap(data_ref, edge_ref, band)
-    convolve(data_ref, edge_ref, weight_ref, None, out_ref, range(band), band)
-
-
-def own_air_kernel(data_ref, packed_ref, weight_ref, out_ref, edge_ref):
-    _, levels, band, channels, _ = data_ref.shape
-    for h in range(2):
-        for level in range(levels):
-            for j in range(band):
-                idx = (level * 2 + h) * band + j
-                edge_ref[h, level, j] = unpack_edge(packed_ref[...], idx, channels)
-    convolve(data_ref, edge_ref, weight_ref, None, out_ref, range(band), band)
-
-
-def halo_columns(band):
-    return [-3, -2, -1] + [band, band + 1, band + 2]
-
-
-def halo_ocean_kernel(west_ref, east_ref, weight_ref, start_ref, out_ref, data_ref, edge_ref, acc_ref):
-    _, levels, band, _, _ = start_ref.shape
-    for s in range(2):
-        for level in range(levels):
-            for i in range(3):
-                at = (s * levels + level) * 3 + i
-                data_ref[s, level, i] = west_ref[at].astype(F32)
-                data_ref[s, level, 3 + i] = east_ref[at].astype(F32)
-    lat_swap(data_ref, edge_ref, 6)
-    convolve(data_ref, edge_ref, weight_ref, start_ref, acc_ref, halo_columns(band), band)
-    out_ref[...] = acc_ref[...].astype(BF16)
-
-
-def halo_air_kernel(west_ref, east_ref, weight_ref, start_ref, out_ref, data_ref, edge_ref, acc_ref):
-    _, levels, band, channels, _ = start_ref.shape
+                base = (level * band + i) * TAPS
+                sums = [None, None]
+                for d in range(TAPS):
+                    at = slice((base + d) * 8, (base + d) * 8 + 8)
+                    first = product_ref[at, :LANES]
+                    second = product_ref[at, LANES:]
+                    off = d - 3
+                    if off > 0:
+                        first, second = (
+                            pltpu.roll(jnp.where(lane < off, second, first), LANES - off, 1),
+                            pltpu.roll(jnp.where(lane < off, 0.0, second), LANES - off, 1),
+                        )
+                    elif off < 0:
+                        first, second = (
+                            pltpu.roll(jnp.where(lane >= LANES + off, 0.0, first), -off, 1),
+                            pltpu.roll(jnp.where(lane >= LANES + off, first, second), -off, 1),
+                        )
+                    sums = [
+                        part if old is None else old + part
+                        for old, part in zip(sums, (first, second))
+                    ]
+                for s in range(2):
+                    out_ref[s, level, i, rows] = sums[s].astype(BF16)
+
+
+def conv_air_kernel(own_ref, west_ref, east_ref, packed_ref, matrix_ref, out_ref, product_ref):
+    _, levels, band, count, _ = own_ref.shape
+    depth = matrix_ref.shape[-1]
     lon = lax.axis_index("lon")
     swap_west = jnp.where(lon == 0, 1, 0)
     swap_east = jnp.where(lon == lax.axis_size("lon") - 1, 1, 0)
     last = 2 * levels * 3
-    west_edge = west_ref[last].astype(F32)
-    east_edge = east_ref[last].astype(F32)
-    for h in range(2):
-        west_h = jnp.abs(h - swap_west)
-        east_h = jnp.abs(h - swap_east)
+    lane = lane_ids(8)
+    for sub in range(count // 8):
+        rows = slice(sub * 8, sub * 8 + 8)
+        packed = [packed_ref[rows], west_ref[last, rows].astype(F32), east_ref[last, rows].astype(F32)]
+        columns = []
+        edges = []
+        for h in range(2):
+            west_h = jnp.abs(h - swap_west)
+            east_h = jnp.abs(h - swap_east)
+            tiles = []
+            beyond = []
+            for level in range(levels):
+                for i in range(3):
+                    tiles.append(west_ref[(west_h * levels + level) * 3 + i, rows].astype(F32))
+                    beyond.append((1, (level * 2 + west_h) * band + i + band - 3))
+                for i in range(band):
+                    tiles.append(own_ref[h, level, i, rows].astype(F32))
+                    beyond.append((0, (level * 2 + h) * band + i))
+                for i in range(3):
+                    tiles.append(east_ref[(east_h * levels + level) * 3 + i, rows].astype(F32))
+                    beyond.append((2, (level * 2 + east_h) * band + i))
+            edges.append([unpack_edge(packed[who], idx, h * 64, lane) for who, idx in beyond])
+            columns.append(tiles)
+        columns.append([first + second for first, second in zip(*edges)])
+        pad = depth - len(columns[0]) * 8
+        if pad:
+            columns = [tiles + [jnp.zeros((pad, LANES), F32)] for tiles in columns]
+        data = jnp.concatenate(
+            [jnp.concatenate(tiles, axis=0) for tiles in columns], axis=1
+        ).astype(BF16)
+        matrix = matrix_ref[sub].reshape(-1, depth)
+        product_ref[...] = jnp.dot(matrix, data, preferred_element_type=F32)
         for level in range(levels):
-            for i in range(3):
-                data_ref[h, level, i] = west_ref[(west_h * levels + level) * 3 + i].astype(F32)
-                data_ref[h, level, 3 + i] = east_ref[(east_h * levels + level) * 3 + i].astype(F32)
-                edge_ref[h, level, i] = unpack_edge(
-                    west_edge, (level * 2 + west_h) * band + i + band - 3, channels
-                )
-                edge_ref[h, level, 3 + i] = unpack_edge(
-                    east_edge, (level * 2 + east_h) * band + i, channels
-                )
-    convolve(data_ref, edge_ref, weight_ref, start_ref, acc_ref, halo_columns(band), band)
-    out_ref[...] = acc_ref[...].astype(BF16)
+            for i in range(band):
+                base = (level * band + i) * TAPS
+                sums = [None, None]
+                for d in range(TAPS):
+                    at = slice((base + d) * 8, (base + d) * 8 + 8)
+                    off = d - 3
+                    edge = product_ref[at, 2 * LANES :] if off else None
+                    for h in range(2):
+                        part = product_ref[at, h * LANES : (h + 1) * LANES]
+                        if off:
+                            here = edge if h == 0 else pltpu.roll(edge, 64, 1)
+                            inside = lane < off if off > 0 else lane >= LANES + off
+                            part = pltpu.roll(jnp.where(inside, here, part), (LANES - off) % LANES, 1)
+                        sums[h] = part if sums[h] is None else sums[h] + part
+                for h in range(2):
+                    out_ref[h, level, i, rows] = sums[h].astype(BF16)
+
+
+def convolution(kernel, name, own, west, east, packed, matrix):
+    _, levels, band, channels, _ = own.shape
+    groups, pairs, rows, depth = matrix.shape
+    count = 16
+    lane_tiles = 2 if packed is None else 3
+    grid_spec = pl.BlockSpec((2, levels, band, count, LANES), lambda g: (0, 0, 0, g, 0))
+    rim_spec = pl.BlockSpec((west.shape[0], count, LANES), lambda g: (0, g, 0))
+    args = [own, west, east]
+    specs = [grid_spec, rim_spec, rim_spec]
+    if packed is not None:
+        args.append(packed)
+        specs.append(pl.BlockSpec((count, LANES), lambda g: (g, 0)))
+    args.append(matrix)
+    specs.append(pl.BlockSpec((count // 8, pairs, rows, depth), lambda g: (g, 0, 0, 0)))
+    return pl.pallas_call(
+        kernel,
+        grid=(channels // count,),
+        out_shape=jax.ShapeDtypeStruct(own.shape, BF16),
+        in_specs=specs,
+        out_specs=grid_spec,
+        scratch_shapes=[pltpu.VMEM((pairs * rows, lane_tiles * LANES), F32)],
+        name=name,
+        cost_estimate=pl.CostEstimate(flops=2 * 10**9, bytes_accessed=4 * 10**6, transcendentals=0),
+    )(*args)
 
 
 def mlp_kernel(masked, *refs):
-    own_ref, other_ref, gain_ref, up_ref, down_ref, forced_ref = refs[:6]
-    mask_ref = refs[6] if masked else None
+    own_ref, other_ref, gain_ref, up_ref, down_ref, top_ref, forced_ref = refs[:7]
+    mask_ref = refs[7] if masked else None
     out_ref, values_ref = refs[-2:]
     _, levels, band, channels, _ = own_ref.shape
     ch = lax.axis_index("ch")
@@ -286,13 +344,23 @@
         update = jnp.dot(down, hidden, preferred_element_type=F32).astype(BF16).astype(F32)
         for s in range(2):
             lanes = slice(s * LANES, (s + 1) * LANES)
-            result = forced_ref[s, level, i] + update[:, lanes]
+            forced = jnp.where(level == 0, top_ref[s, i], forced_ref[s, level, i].astype(F32))
+            result = forced + update[:, lanes]
             if masked:
                 result = result * sea[:, lanes]
             out_ref[s, level, i] = result.astype(BF16)
         return carry
 
     lax.fori_loop(0, levels * band, step, 0)
+
+
+def toeplitz(kernel, levels, name):
+    channels = kernel.shape[0]
+    taps = jnp.transpose(kernel, (3, 0, 1, 2)).reshape(TAPS * channels, 3 * TAPS)
+    return call(
+        toeplitz_kernel, jax.ShapeDtypeStruct((channels // 8, levels * 2, 2 * TAPS * 8, 256), BF16),
+        [], name, 10**9, 3 * 10**6, taps,
+    )
 
 
 def ring(count, step):
@@ -323,10 +391,11 @@
     got = lax.ppermute(packed, "comp", ring(2, 1))
     o_rim = (2 * o_levels * 3, o_ch, LANES)
     a_rim = (2 * a_levels * 3 + 1, a_ch, LANES)
-    ocean_forced, air_forced, edge, o_west, o_east, a_west, a_east = call(
+    ocean_top, air_top, ocean_forced, air_forced, edge, o_west, o_east, a_west, a_east = call(
         force_kernel,
         (
-            shape(o_grid, F32), shape(a_grid, F32), shape((a_ch, LANES), F32),
+            shape((2, band, o_ch, LANES), F32), shape((2, band, a_ch, LANES), F32),
+            shape(o_grid, BF16), shape(a_grid, BF16), shape((a_ch, LANES), F32),
             shape(o_rim, BF16), shape(o_rim, BF16), shape(a_rim, BF16), shape(a_rim, BF16),
         ),
         [], "force", 10**6, 4 * 10**6,
@@ -340,40 +409,27 @@
     from_west_a = lax.ppermute(a_east, "lon", ring(lons, 1))
     from_east_a = lax.ppermute(a_west, "lon", ring(lons, -1))
 
-    o_weight = ocean_kernel.reshape(o_ch, -1)
-    a_weight = air_kernel.reshape(a_ch, -1)
-    o_own = call(
-        own_ocean_kernel, shape(o_grid, F32), [pltpu.VMEM(o_grid, F32)], "own_ocean",
-        3 * 10**9, 10**6, ocean_forced, o_weight,
-    )
-    a_own = call(
-        own_air_kernel, shape(a_grid, F32), [pltpu.VMEM(a_grid, F32)], "own_air",
-        3 * 10**9, 10**6, air_forced, edge, a_weight,
-    )
-    o_six = (2, o_levels, 6, o_ch, LANES)
-    a_six = (2, a_levels, 6, a_ch, LANES)
-    o_conv = call(
-        halo_ocean_kernel, shape(o_grid, BF16),
-        [pltpu.VMEM(o_six, F32), pltpu.VMEM(o_six, F32), pltpu.VMEM(o_grid, F32)], "halo_ocean",
-        2 * 10**9, 10**6, from_west_o, from_east_o, o_weight, o_own,
+    o_matrix = toeplitz(ocean_kernel, o_levels, "matrix_ocean")
+    a_matrix = toeplitz(air_kernel, a_levels, "matrix_air")
+    o_conv = convolution(
+        conv_ocean_kernel, "conv_ocean", ocean_forced, from_west_o, from_east_o, None, o_matrix
     )
     o_other = lax.ppermute(o_conv, "ch", ring(2, 1))
-    a_conv = call(
-        halo_air_kernel, shape(a_grid, BF16),
-        [pltpu.VMEM(a_six, F32), pltpu.VMEM(a_six, F32), pltpu.VMEM(a_grid, F32)], "halo_air",
-        2 * 10**9, 10**6, from_west_a, from_east_a, a_weight, a_own,
+    a_conv = convolution(
+        conv_air_kernel, "conv_air", air_forced, from_west_a, from_east_a, edge, a_matrix
     )
     a_other = lax.ppermute(a_conv, "ch", ring(2, 1))
 
     o_next = call(
         functools.partial(mlp_kernel, True), shape(o_grid, BF16),
         [pltpu.VMEM((2 * o_ch, 2 * LANES), F32)], "mlp_ocean", 10**9, 3 * 10**6,
-        o_conv, o_other, ocean_gain[:, None], ocean_up.T, ocean_down.T, ocean_forced, ocean_mask,
+        o_conv, o_other, ocean_gain[:, None], ocean_up.T, ocean_down.T, ocean_top, ocean_forced,
+        ocean_mask,
     )
     a_next = call(
         functools.partial(mlp_kernel, False), shape(a_grid, BF16),
         [pltpu.VMEM((2 * a_ch, 2 * LANES), F32)], "mlp_air", 10**9, 3 * 10**6,
-        a_conv, a_other, air_gain[:, None], air_up.T, air_down.T, air_forced,
+        a_conv, a_other, air_gain[:, None], air_up.T, air_down.T, air_top, air_forced,
     )
     ocean_next = jnp.transpose(o_next, (1, 3, 2, 0, 4)).reshape(ocean_state.shape)
     air_next = jnp.transpose(a_next, (1, 3, 2, 0, 4))

time: 104 us -> 79.4 us (0.76)
  Pallas kernels: 62.7 us -> 40.9 us
  local copies, waits for them, and re-layouts: 20.8 us -> 19.3 us
  starting transfers between devices: 19 us -> 17.5 us
    pallas_call x8 -> x6, Pallas kernels: 62.7 us -> 29 us  [call(): pl.pallas_call(kernel, out_shape=out_shape, in_specs=[VMEM] * len(args),...]
    pallas_call x0 -> x2, Pallas kernels: none -> 11.9 us  [convolution(): pl.pallas_call(kernel, grid=(channels // count,), out_shape=jax.ShapeDtyp...]
    unnamed x42 -> x40, local copies, waits for them, and re-layouts: 16.1 us -> 13.2 us
    ppermute x1, starting transfers between devices: 7.25 us -> 5.06 us  [per_device(): from_east_a = lax.ppermute(a_west, 'lon', ring(lons, -1))]
  transfers between devices with their start and end apart: 7 -> 7, of which waited for: 0 -> 1; matrix products, arithmetic and copies ran while one was open for 10% -> 15% of each run, Pallas kernels for 49% -> 36%
where the time goes in v2:
time: 79.4 us; the launch traced here: 78.8 us
  Pallas kernels  40.9 us (52%)
  local copies, waits for them, and re-layouts  19.3 us (24%)
  starting transfers between devices  17.5 us (22%)
    pallas_call x6, Pallas kernels, call(): pl.pallas_call(kernel, out_shape=out_shape, in_specs=[VMEM] * len(args),...  29 us
    unnamed x40, local copies, waits for them, and re-layouts  13.2 us
    pallas_call x2, Pallas kernels, convolution(): pl.pallas_call(kernel, grid=(channels // count,), out_shape=jax.ShapeDtyp...  11.9 us
    ppermute x1, starting transfers between devices, per_device(): from_east_o = lax.ppermute(o_west, ('comp', 'lon'), ring(bands, -1))  8.15 us
    ppermute x1, starting transfers between devices, per_device(): from_east_a = lax.ppermute(a_west, 'lon', ring(lons, -1))  5.06 us
    ppermute x1, starting transfers between devices, per_device(): got = lax.ppermute(packed, 'comp', ring(2, 1))  2.3 us
    reshape x2, local copies, waits for them, and re-layouts, per_device(): ocean_state.reshape(o_levels, o_ch, band, 2, LANES)  1.98 us
    reshape x4, local copies, waits for them, and re-layouts, toeplitz(): jnp.transpose(kernel, (3, 0, 1, 2)).reshape(TAPS * channels, 3 * TAPS)  1.91 us
  transfers between devices with their start and end apart: 7, of which 1 were waited for; matrix products, arithmetic and copies ran while one was open for 15% of the time, Pallas kernels for 36%

profile of v2, /device:TPU:8, one launch (start us, length us, event | category | flops | bytes accessed | tf_op | source)
XLA Modules:
  0.0 78.8 jit_solution(450818923561616130)
XLA Ops:
  0.7 1.8 %copy.49 = bf16[2,96,4,2,128]{4,1,2,0,3:T(8,128)(2,1)} copy(bf16[2,96,4,2,128]{4,3,2,1,0:T(2,128)(2,1)} %param.17) | data formatting | bytes 786432 | tf_op args[2]
  2.5 1.8 %pack.1 = f32[120,128]{1,0:T(8,128)} custom-call(s32[4,256]{1,0:T(4,128)} %refs_7_.1, f32[4,256]{1,0:T(4,128)} %temp_ref.3, f32[4,4,2,128]{3,2,1,0:T(2,128)} %flux_ref.3, bf16[2,2,4,96,128]{4,3,2,1,0:T(8,128)(2,1)} %bitcast.22), custom_call_target="tpu_custom_call" | custom-call | flops 100000 | bytes 1000000 | tf_op jit(solution)/shard_map/pack/pallas_call | solution.py:21
  4.3 2.3 %collective-permute-start = (f32[120,128]{1,0:T(8,128)}, f32[120,128]{1,0:T(8,128)S(1)}, u32[]{:S(2)}, u32[]{:S(2)}) collective-permute-start(f32[120,128]{1,0:T(8,128)} %pack.1), channel_id=1, source_target_pairs={{0,128},{128,0},{1,129},{129,1},{2,130},{130,2},{3,131},{131,3},{4... | collective-permute-start | bytes 184328 | tf_op jit(solution)/shard_map/ppermute | solution.py:391
  6.6 1.1 %reshape.20 = bf16[3,64,4,2,128]{4,3,2,1,0:T(2,128)(2,1)S(1)} reshape(bf16[3,64,4,256]{3,2,1,0:T(4,128)(2,1)} %param.15) | data formatting | bytes 786432 | tf_op jit(solution)/shard_map/reshape | solution.py:380
  7.8 0.8 %copy.48 = bf16[3,64,4,2,128]{4,1,2,0,3:T(8,128)(2,1)} copy(bf16[3,64,4,2,128]{4,3,2,1,0:T(2,128)(2,1)S(1)} %reshape.20) | data formatting | bytes 786432 | tf_op jit(solution)/shard_map/reshape | solution.py:380
  10.9 3.0 %force.1 = (f32[2,4,64,128]{3,2,1,0:T(8,128)}, f32[2,4,96,128]{3,2,1,0:T(8,128)}, bf16[2,3,4,64,128]{4,3,2,1,0:T(8,128)(2,1)}, bf16[2,2,4,96,128]{4,3,2,1,0:T(8,...) custom-call(s32[4,256]{1,0:T(4,128)} %refs_7_.1, ...), custom_call_target="tpu_custom_call" | custom-call | flops 1000000 | bytes 4000000 | tf_op jit(solution)/shard_map/force/pallas_call | solution.py:21
  13.9 8.1 %collective-permute-start.2 = (bf16[18,64,128]{2,1,0:T(8,128)(2,1)}, bf16[18,64,128]{2,1,0:T(8,128)(2,1)S(1)}, u32[]{:S(2)}, u32[]{:S(2)}) collective-permute-start(bf16[18,64,128]{2,1,0:T(8,128)(2,1)} %get-tuple-element.13), channel_id=1, source_target_pairs={{0,254},{2,0},{4,2},{6,4},{8,6},{10,8},{12,10},{14,12},{16,14},{18... | collective-permute-start | bytes 884744 | tf_op jit(solution)/shard_map/ppermute | solution.py:408
  22.2 0.9 %copy.37.taps_ref = f32[672,21]{1,0:T(8,128)} copy(f32[672,21]{0,1:T(8,128)S(1)} %reshape.19) | data formatting | bytes 112896 | tf_op jit(solution)/shard_map/reshape | solution.py:359
  23.1 5.1 %collective-permute-start.5 = (bf16[13,96,128]{2,1,0:T(8,128)(2,1)}, bf16[13,96,128]{2,1,0:T(8,128)(2,1)S(1)}, u32[]{:S(2)}, u32[]{:S(2)}) collective-permute-start(bf16[13,96,128]{2,1,0:T(8,128)(2,1)} %get-tuple-element.17), channel_id=1, source_target_pairs={{0,126},{2,0},{4,2},{6,4},{8,6},{10,8},{12,10},{14,12},{16,14},{18... | collective-permute-start | bytes 958472 | tf_op jit(solution)/shard_map/ppermute | solution.py:410
  28.1 3.9 %matrix_air.1.matrix_ref = bf16[12,4,112,256]{3,2,1,0:T(8,128)(2,1)} custom-call(f32[672,21]{1,0:T(8,128)} %copy.37.taps_ref), custom_call_target="tpu_custom_call" | custom-call | flops 1000000000 | bytes 3000000 | tf_op jit(solution)/shard_map/matrix_air/pallas_call | solution.py:21
  32.1 0.8 %copy.32.taps_ref = f32[448,21]{1,0:T(8,128)} copy(f32[448,21]{0,1:T(8,128)S(1)} %reshape.17) | data formatting | bytes 75264 | tf_op jit(solution)/shard_map/reshape | solution.py:359
  32.9 4.1 %matrix_ocean.1.matrix_ref = bf16[8,6,112,256]{3,2,1,0:T(8,128)(2,1)} custom-call(f32[448,21]{1,0:T(8,128)} %copy.32.taps_ref), custom_call_target="tpu_custom_call" | custom-call | flops 1000000000 | bytes 3000000 | tf_op jit(solution)/shard_map/matrix_ocean/pallas_call | solution.py:21
  37.8 4.8 %conv_ocean.1.refs_0_ = bf16[2,3,4,64,128]{4,3,2,1,0:T(8,128)(2,1)} custom-call(bf16[2,3,4,64,128]{4,3,2,1,0:T(8,128)(2,1)} %get-tuple-element.11.own_ref.refs_6_, bf16[18,64,128]{2,1,0:T(8,128)(2,1)} %copy-done.14, bf16[18,64,128]{2,1,0:T(8,128)(2,1)} %copy-done.15, bf16[8,6,112,256]{3,2,1,0:T(8,128)(2,1)} %matrix_ocean.1.matrix_ref), custom_call_target="tpu_custom_call" | custom-call | flops 2000000000 | bytes 4000000 | tf_op jit(solution)/shard_map/conv_ocean/pallas_call | solution.py:301
  42.7 1.5 %collective-permute-start.3 = (bf16[2,3,4,64,128]{4,3,2,1,0:T(8,128)(2,1)}, bf16[2,3,4,64,128]{4,3,2,1,0:T(8,128)(2,1)S(1)}, u32[]{:S(2)}, u32[]{:S(2)}) collective-permute-start(bf16[2,3,4,64,128]{4,3,2,1,0:T(8,128)(2,1)} %conv_ocean.1.refs_0_), channel_id=1, source_target_pairs={{0,1},{1,0},{2,3},{3,2},{4,5},{5,4},{6,7},{7,6},{8,9},{9,8},{10,11... | collective-permute-start | bytes 1179656 | tf_op jit(solution)/shard_map/ppermute | solution.py:417
  45.0 7.1 %conv_air.1.refs_0_ = bf16[2,2,4,96,128]{4,3,2,1,0:T(8,128)(2,1)} custom-call(bf16[2,2,4,96,128]{4,3,2,1,0:T(8,128)(2,1)} %get-tuple-element.15.own_ref.refs_6_, bf16[13,96,128]{2,1,0:T(8,128)(2,1)} %copy-done.12, bf16[13,96,128]{2,1,0:T(8,128)(2,1)} %copy-done.13, f32[96,128]{1,0:T(8,128)} %get-tuple-element.18.packed_ref, ...), custom_call_target="tpu_custom_call" | custom-call | flops 2000000000 | bytes 4000000 | tf_op jit(solution)/shard_map/conv_air/pallas_call | solution.py:301
  52.6 0.9 %copy.38 = bf16[192,768]{0,1:T(8,128)(2,1)} copy(bf16[192,768]{1,0:T(8,128)(2,1)S(1)} %copy-done) | data formatting | bytes 589824 | tf_op args[11]
  53.6 0.8 copy.39.refs_2_
  54.3 0.7 copy.33
  55.1 0.8 copy.34
  57.3 8.6 %mlp_ocean.1 = bf16[2,3,4,64,128]{4,3,2,1,0:T(8,128)(2,1)} custom-call(bf16[2,3,4,64,128]{4,3,2,1,0:T(8,128)(2,1)} %conv_ocean.1.refs_0_, bf16[2,3,4,64,128]{4,3,2,1,0:T(8,128)(2,1)} %copy-done.10, f32[128,1]{1,0:T(8,128)} %copy.35.refs_2_, bf16[512,128]{1,0:T(8,128)(2,1)} %bitcast.28, bf16[128,512]{1,0:T(8,128)(2,1)} %bitcast.29, ...), custom_call_target="tpu_custom_call" | custom-call | flops 1000000000 | bytes 3000000 | tf_op jit(solution)/shard_map/mlp_ocean/pallas_call | solution.py:21
  65.9 1.4 %copy.44 = bf16[3,64,4,2,128]{4,3,2,1,0:T(2,128)(2,1)S(1)} copy(bf16[3,64,4,2,128]{4,1,2,0,3:T(8,128)(2,1)} %bitcast.25) | data formatting | bytes 786432
  67.3 1.0 %reshape.21 = bf16[3,64,4,256]{3,2,1,0:T(4,128)(2,1)} reshape(bf16[3,64,4,2,128]{4,3,2,1,0:T(2,128)(2,1)S(1)} %copy.44) | data formatting | bytes 786432
  69.1 7.6 %mlp_air.1 = bf16[2,2,4,96,128]{4,3,2,1,0:T(8,128)(2,1)} custom-call(bf16[2,2,4,96,128]{4,3,2,1,0:T(8,128)(2,1)} %conv_air.1.refs_0_, bf16[2,2,4,96,128]{4,3,2,1,0:T(8,128)(2,1)} %copy-done.11, f32[192,1]{1,0:T(8,128)} %copy.39.refs_2_, bf16[768,192]{1,0:T(8,128)(2,1)} %bitcast.27, bf16[192,768]{1,0:T(8,128)(2,1)} %bitcast.36, ...), custom_call_target="tpu_custom_call" | custom-call | flops 1000000000 | bytes 3000000 | tf_op jit(solution)/shard_map/mlp_air/pallas_call | solution.py:21
  76.6 2.1 %copy.41 = bf16[2,96,4,2,128]{4,3,2,1,0:T(2,128)(2,1)} copy(bf16[2,96,4,2,128]{4,1,2,0,3:T(8,128)(2,1)} %bitcast.26) | data formatting | bytes 786432
  (47 shorter events, 6.9 us)
Async XLA Ops:
  0.6 8.0 %copy-start.8 = (f32[96]{0:T(128)S(1)}, f32[96]{0:T(128)}, u32[]{:S(2)}) copy-start(f32[96]{0:T(128)} %param.29) | copy-start | bytes 1156
  0.6 8.7 %copy-start.6 = (f32[4,64]{1,0:T(4,128)S(1)}, f32[4,64]{1,0:T(4,128)}, u32[]{:S(2)}) copy-start(f32[4,64]{1,0:T(4,128)} %param.28) | copy-start | bytes 3076
  0.7 21.4 %copy-start.3 = (f32[96,3,7,7]{0,3,2,1:T(8,128)S(1)}, f32[96,3,7,7]{0,3,2,1:T(8,128)}, u32[]{:S(2)}) copy-start(f32[96,3,7,7]{0,3,2,1:T(8,128)} %param.24) | copy-start | bytes 169348
  4.3 5.9 %collective-permute-start = (f32[120,128]{1,0:T(8,128)}, f32[120,128]{1,0:T(8,128)S(1)}, u32[]{:S(2)}, u32[]{:S(2)}) collective-permute-start(f32[120,128]{1,0:T(8,128)} %pack.1), channel_id=1, source_target_pairs={{0,128},{128,0},{1,129},{129,1},{2,130},{130,2},{3,131},{131,3},{4... | collective-permute-start | bytes 184328 | tf_op jit(solution)/shard_map/ppermute | solution.py:391
  8.6 23.4 %copy-start.4 = (f32[64,3,7,7]{0,3,2,1:T(8,128)S(1)}, f32[64,3,7,7]{0,3,2,1:T(8,128)}, u32[]{:S(2)}) copy-start(f32[64,3,7,7]{0,3,2,1:T(8,128)} %param.20) | copy-start | bytes 112900
  10.3 0.6 copy-start.5
  13.9 23.1 %collective-permute-start.1 = (bf16[18,64,128]{2,1,0:T(8,128)(2,1)}, bf16[18,64,128]{2,1,0:T(8,128)(2,1)S(1)}, u32[]{:S(2)}, u32[]{:S(2)}) collective-permute-start(bf16[18,64,128]{2,1,0:T(8,128)(2,1)} %get-tuple-element.12), channel_id=1, source_target_pairs={{0,2},{2,4},{4,6},{6,8},{8,10},{10,12},{12,14},{14,16},{16,18},{18... | collective-permute-start | bytes 884744 | tf_op jit(solution)/shard_map/ppermute | solution.py:407
  13.9 23.1 %collective-permute-start.2 = (bf16[18,64,128]{2,1,0:T(8,128)(2,1)}, bf16[18,64,128]{2,1,0:T(8,128)(2,1)S(1)}, u32[]{:S(2)}, u32[]{:S(2)}) collective-permute-start(bf16[18,64,128]{2,1,0:T(8,128)(2,1)} %get-tuple-element.13), channel_id=1, source_target_pairs={{0,254},{2,0},{4,2},{6,4},{8,6},{10,8},{12,10},{14,12},{16,14},{18... | collective-permute-start | bytes 884744 | tf_op jit(solution)/shard_map/ppermute | solution.py:408
  23.1 21.1 %collective-permute-start.4 = (bf16[13,96,128]{2,1,0:T(8,128)(2,1)}, bf16[13,96,128]{2,1,0:T(8,128)(2,1)S(1)}, u32[]{:S(2)}, u32[]{:S(2)}) collective-permute-start(bf16[13,96,128]{2,1,0:T(8,128)(2,1)} %get-tuple-element.16), channel_id=1, source_target_pairs={{0,2},{2,4},{4,6},{6,8},{8,10},{10,12},{12,14},{14,16},{16,18},{18... | collective-permute-start | bytes 958472 | tf_op jit(solution)/shard_map/ppermute | solution.py:409
  23.1 21.1 %collective-permute-start.5 = (bf16[13,96,128]{2,1,0:T(8,128)(2,1)}, bf16[13,96,128]{2,1,0:T(8,128)(2,1)S(1)}, u32[]{:S(2)}, u32[]{:S(2)}) collective-permute-start(bf16[13,96,128]{2,1,0:T(8,128)(2,1)} %get-tuple-element.17), channel_id=1, source_target_pairs={{0,126},{2,0},{4,2},{6,4},{8,6},{10,8},{12,10},{14,12},{16,14},{18... | collective-permute-start | bytes 958472 | tf_op jit(solution)/shard_map/ppermute | solution.py:410
  37.0 0.7 copy-start.14
  37.0 0.8 %copy-start.15 = (bf16[18,64,128]{2,1,0:T(8,128)(2,1)}, bf16[18,64,128]{2,1,0:T(8,128)(2,1)S(1)}, u32[]{:S(2)}) copy-start(bf16[18,64,128]{2,1,0:T(8,128)(2,1)S(1)} %collective-permute-done.2.east_ref) | copy-start | bytes 884740
  42.7 13.9 %collective-permute-start.3 = (bf16[2,3,4,64,128]{4,3,2,1,0:T(8,128)(2,1)}, bf16[2,3,4,64,128]{4,3,2,1,0:T(8,128)(2,1)S(1)}, u32[]{:S(2)}, u32[]{:S(2)}) collective-permute-start(bf16[2,3,4,64,128]{4,3,2,1,0:T(8,128)(2,1)} %conv_ocean.1.refs_0_), channel_id=1, source_target_pairs={{0,1},{1,0},{2,3},{3,2},{4,5},{5,4},{6,7},{7,6},{8,9},{9,8},{10,11... | collective-permute-start | bytes 1179656 | tf_op jit(solution)/shard_map/ppermute | solution.py:417
  44.2 0.7 copy-start.12
  44.2 0.8 %copy-start.13 = (bf16[13,96,128]{2,1,0:T(8,128)(2,1)}, bf16[13,96,128]{2,1,0:T(8,128)(2,1)S(1)}, u32[]{:S(2)}) copy-start(bf16[13,96,128]{2,1,0:T(8,128)(2,1)S(1)} %collective-permute-done.5.east_ref) | copy-start | bytes 958468
  45.0 7.7 %copy-start = (bf16[192,768]{1,0:T(8,128)(2,1)S(1)}, bf16[192,768]{1,0:T(8,128)(2,1)}, u32[]{:S(2)}) copy-start(bf16[192,768]{1,0:T(8,128)(2,1)} %param.26) | copy-start | bytes 884740
  45.0 8.6 %copy-start.7 = (f32[192]{0:T(256)S(1)}, f32[192]{0:T(256)}, u32[]{:S(2)}) copy-start(f32[192]{0:T(256)} %param.25) | copy-start | bytes 2308
  45.0 9.3 %copy-start.1 = (bf16[128,512]{1,0:T(8,128)(2,1)S(1)}, bf16[128,512]{1,0:T(8,128)(2,1)}, u32[]{:S(2)}) copy-start(bf16[128,512]{1,0:T(8,128)(2,1)} %param.22) | copy-start | bytes 393220
  45.0 10.1 %copy-start.2 = (bf16[512,128]{1,0:T(8,128)(2,1)S(1)}, bf16[512,128]{1,0:T(8,128)(2,1)}, u32[]{:S(2)}) copy-start(bf16[512,128]{1,0:T(8,128)(2,1)} %param.23) | copy-start | bytes 393220
  45.0 10.9 %copy-start.9 = (f32[128]{0:T(128)S(1)}, f32[128]{0:T(128)}, u32[]{:S(2)}) copy-start(f32[128]{0:T(128)} %param.21) | copy-start | bytes 1540
  52.1 16.2 %collective-permute-start.6 = (bf16[2,2,4,96,128]{4,3,2,1,0:T(8,128)(2,1)}, bf16[2,2,4,96,128]{4,3,2,1,0:T(8,128)(2,1)S(1)}, u32[]{:S(2)}, u32[]{:S(2)}) collective-permute-start(bf16[2,2,4,96,128]{4,3,2,1,0:T(8,128)(2,1)} %conv_air.1.refs_0_), channel_id=1, source_target_pairs={{0,1},{1,0},{2,3},{3,2},{4,5},{5,4},{6,7},{7,6},{8,9},{9,8},{10,11... | collective-permute-start | bytes 1179656 | tf_op jit(solution)/shard_map/ppermute | solution.py:421
  56.6 0.7 copy-start.10
  68.3 0.7 copy-start.11

commit v3 on v2

v3 whole, which is shorter than its diff:
```python
import functools

import jax
import jax.numpy as jnp
from jax import lax
from jax.experimental import pallas as pl
from jax.experimental.pallas import tpu as pltpu
from jax.sharding import PartitionSpec as P

F32 = jnp.float32
BF16 = jnp.bfloat16
LANES = 128
VMEM = pl.BlockSpec(memory_space=pltpu.VMEM)


def lane_ids(rows):
    return lax.broadcasted_iota(jnp.int32, (rows, LANES), 1)


def call(kernel, out_shape, scratch, name, flops, moved, *args):
    return pl.pallas_call(
        kernel,
        out_shape=out_shape,
        in_specs=[VMEM] * len(args),
        out_specs=jax.tree.map(lambda _: VMEM, out_shape),
        scratch_shapes=scratch,
        name=name,
        cost_estimate=pl.CostEstimate(flops=flops, bytes_accessed=moved, transcendentals=0),
    )(*args)


def rows_of(fields, band):
    temp = fields * band * 2
    return temp, temp + 2 * band, temp + 4 * band


def pack_kernel(mask_ref, temp_ref, flux_ref, air_ref, out_ref):
    comp = lax.axis_index("comp")
    fields, band = flux_ref.shape[:2]
    temp_row, sea_row, edge_row = rows_of(fields, band)
    for k in range(fields):
        for j in range(band):
            at = (k * band + j) * 2
            out_ref[at : at + 2, :] = flux_ref[k, j]
    sea = mask_ref[...].astype(F32)
    temp = temp_ref[...] * sea
    for s in range(2):
        lanes = slice(s * LANES, (s + 1) * LANES)
        out_ref[temp_row + s * band : temp_row + (s + 1) * band, :] = temp[:, lanes]
        out_ref[sea_row + s * band : sea_row + (s + 1) * band, :] = sea[:, lanes]
    levels, channels = air_ref.shape[1], air_ref.shape[3]
    start = jnp.where(comp == 0, LANES - 8, 0)
    lane = lane_ids(channels)
    packed = jnp.zeros((channels, LANES), F32)
    for level in range(levels):
        for h in range(2):
            for j in range(band):
                idx = (level * 2 + h) * band + j
                rolled = pltpu.roll(
                    air_ref[h, level, j].astype(F32), lax.rem(8 * idx - start + LANES, LANES), 1
                )
                packed = jnp.where(lane // 8 == idx, rolled, packed)
    out_ref[edge_row : edge_row + channels, :] = packed


def fill_surface(mask_ref, temp_ref, surface_ref):
    band = mask_ref.shape[0]
    sea = mask_ref[...].astype(F32)
    temp = temp_ref[...] * sea
    for s in range(2):
        lanes = slice(s * LANES, (s + 1) * LANES)
        surface_ref[s * band : (s + 1) * band, :] = temp[:, lanes]
        surface_ref[(2 + s) * band : (3 + s) * band, :] = sea[:, lanes]


def inject_of(flux_ref, got_ref, fw_ref, half, s, i):
    comp = lax.axis_index("comp")
    fields, band = flux_ref.shape[:2]
    total = None
    for k in range(fields):
        mine = flux_ref[k, i, pl.ds(half, 1), :]
        theirs = got_ref[pl.ds((k * band + i) * 2 + half, 1), :]
        term = fw_ref[:, k : k + 1] * jnp.where(comp == s, mine, theirs)
        total = term if total is None else total + term
    return total


def temp_of(surface_ref, got_ref, fields, band, h, s, j):
    comp = lax.axis_index("comp")
    temp_row = rows_of(fields, band)[0]
    mine = surface_ref[pl.ds(s * band + j, 1), :]
    theirs = got_ref[pl.ds(temp_row + s * band + j, 1), :]
    return jnp.where(comp == h, mine, theirs)


def force_halo_kernel(
    mask_ref, temp_ref, flux_ref, got_ref, ocean_ref, swapped_ref, air_ref, fw_ref, tw_ref,
    even_ref, odd_ref, edge_ref, surface_ref,
):
    comp = lax.axis_index("comp")
    lon = lax.axis_index("lon")
    parity = lax.rem(lon, 2)
    at_end = (lon == 0) | (lon == lax.axis_size("lon") - 1)
    fields, band = flux_ref.shape[:2]
    o_levels, o_ch = ocean_ref.shape[1], ocean_ref.shape[3]
    a_levels, a_ch = air_ref.shape[1], air_ref.shape[3]
    temp_row, sea_row, edge_row = rows_of(fields, band)
    fill_surface(mask_ref, temp_ref, surface_ref)
    heat = tw_ref[...]

    start = jnp.where(comp == 0, 0, LANES - 8)
    lane = lane_ids(8)
    edge_temp = jnp.zeros((8, LANES), F32)
    for h in range(2):
        for j in range(band):
            idx = h * band + j
            row = temp_of(surface_ref, got_ref, fields, band, h, 1 - comp, j)
            rolled = pltpu.roll(
                jnp.broadcast_to(row, (8, LANES)), lax.rem(8 * idx - start + LANES, LANES), 1
            )
            edge_temp = jnp.where(lane // 8 == idx, rolled, edge_temp)
    edge = got_ref[edge_row : edge_row + a_ch, :] + heat * edge_temp[0:1, :]
    edge_ref[...] = edge

    first_air = 2 * o_levels * 3 * o_ch
    for out_ref, offset, outer in ((even_ref, 1 - parity, None), (odd_ref, parity, at_end)):
        for j in range(3):
            col = j + offset
            half = comp if outer is None else jnp.where(outer, 1 - comp, comp)
            for s in range(2):
                inject = inject_of(flux_ref, got_ref, fw_ref, half, s, col)
                sea = surface_ref[pl.ds((2 + s) * band + col, 1), :]
                if outer is not None:
                    sea = jnp.where(outer, got_ref[pl.ds(sea_row + s * band + col, 1), :], sea)
                for level in range(o_levels):
                    tile = (s * o_levels + level) * 3 + j
                    value = ocean_ref[s, level, col].astype(F32)
                    if outer is not None:
                        value = jnp.where(outer, swapped_ref[tile].astype(F32), value)
                    if level == 0:
                        value = value + inject
                    out_ref[tile * o_ch : (tile + 1) * o_ch, :] = (value * sea).astype(BF16)
            for h in range(2):
                row = temp_of(surface_ref, got_ref, fields, band, h, comp, col)
                for level in range(a_levels):
                    value = air_ref[h, level, col].astype(F32)
                    if level == 0:
                        value = value + heat * row
                    at = first_air + ((h * a_levels + level) * 3 + j) * a_ch
                    out_ref[at : at + a_ch, :] = value.astype(BF16)
        at = first_air + 2 * a_levels * 3 * a_ch
        out_ref[at : at + a_ch, :] = edge.astype(BF16)


def force_own_kernel(
    mask_ref, temp_ref, flux_ref, got_ref, ocean_ref, air_ref, fw_ref, tw_ref,
    fo_ref, fa_ref, ob_ref, ab_ref, surface_ref,
):
    comp = lax.axis_index("comp")
    fields, band = flux_ref.shape[:2]
    o_levels, a_levels = ocean_ref.shape[1], air_ref.shape[1]
    fill_surface(mask_ref, temp_ref, surface_ref)
    heat = tw_ref[...]
    for s in range(2):
        for i in range(band):
            inject = inject_of(flux_ref, got_ref, fw_ref, comp, s, i)
            at = (2 + s) * band + i
            sea = surface_ref[at : at + 1, :]
            row = temp_of(surface_ref, got_ref, fields, band, s, comp, i)
            for level in range(o_levels):
                value = ocean_ref[s, level, i].astype(F32)
                if level == 0:
                    value = (value + inject) * sea
                    fo_ref[s, i] = value
                else:
                    value = value * sea
                ob_ref[s, level, i] = value.astype(BF16)
            for level in range(a_levels):
                value = air_ref[s, level, i].astype(F32)
                if level == 0:
                    value = value + heat * row
                    fa_ref[s, i] = value
                ab_ref[s, level, i] = value.astype(BF16)


def unpack_edge(packed, idx, shift, lane):
    comp = lax.axis_index("comp")
    start = lax.rem(jnp.where(comp == 0, 0, LANES - 8) + shift, LANES)
    rolled = pltpu.roll(packed, lax.rem(start - 8 * idx + 2 * LANES, LANES), 1)
    return jnp.where(lane // 8 == start // 8, rolled, 0.0)


TAPS = 7


def toeplitz_kernel(levels, taps_ref, out_ref):
    groups, _, rows, depth = out_ref.shape
    channels = groups * 8
    pair = pl.program_id(0)
    window = taps_ref.shape[1]
    taps = taps_ref[...].astype(BF16)
    row = lax.broadcasted_iota(jnp.int32, (window, depth), 0)
    lane = lax.broadcasted_iota(jnp.int32, (window, depth), 1)
    from_level = lane // 80
    from_lon = lane // 8 - from_level * 10
    same = (lax.broadcasted_iota(jnp.int32, (8, depth), 1) & 7) == lax.broadcasted_iota(
        jnp.int32, (8, depth), 0
    )
    level = pair // 2
    parts = []
    for side in range(2):
        a = from_level - level + 1
        b = from_lon - (lax.rem(pair, 2) * 2 + side)
        hit = (
            (from_level < levels)
            & (a >= 0) & (a <= 2) & (b >= 0) & (b < TAPS) & (a * TAPS + b == row)
        )
        choose = jnp.where(hit, 1.0, 0.0).astype(BF16)
        parts.append(jnp.dot(taps, choose, preferred_element_type=F32))
    for g in range(groups):
        tiles = [
            jnp.where(same, part[d * channels + g * 8 : d * channels + g * 8 + 8], 0.0)
            for part in parts
            for d in range(TAPS)
        ]
        out_ref[g, 0] = jnp.concatenate(tiles, axis=0).astype(BF16)


def rim_tile(even_ref, odd_ref, at, count):
    rows = pl.ds(pl.multiple_of(at, 16), count)
    return even_ref[rows, :].astype(F32), odd_ref[rows, :].astype(F32)


def conv_ocean_kernel(own_ref, even_ref, odd_ref, matrix_ref, out_ref, product_ref):
    _, levels, band, count, _ = own_ref.shape
    depth = matrix_ref.shape[-1]
    lane = lane_ids(8)
    channels = pl.num_programs(0) * count
    first = pl.program_id(0) * count
    inner = lax.rem(lax.axis_index("lon"), 2) == 1
    columns = []
    for s in range(2):
        tiles = []
        for level in range(levels):
            west, east = [], []
            for i in range(3):
                at = ((s * levels + level) * 3 + i) * channels + first
                even, odd = rim_tile(even_ref, odd_ref, at, count)
                west.append(jnp.where(inner, even, odd))
                east.append(jnp.where(inner, odd, even))
            own = [own_ref[s, level, i].astype(F32) for i in range(band)]
            tiles += west + own + east
        columns.append(tiles)
    for sub in range(count // 8):
        rows = slice(sub * 8, sub * 8 + 8)
        halves = []
        for tiles in columns:
            tiles = [tile[rows] for tile in tiles]
            if depth > len(tiles) * 8:
                tiles.append(jnp.zeros((depth - len(tiles) * 8, LANES), F32))
            halves.append(jnp.concatenate(tiles, axis=0))
        data = jnp.concatenate(halves, axis=1).astype(BF16)
        matrix = matrix_ref[sub].reshape(-1, depth)
        product_ref[...] = jnp.dot(matrix, data, preferred_element_type=F32)
        for level in range(levels):
            for i in range(band):
                base = (level * band + i) * TAPS
                sums = [None, None]
                for d in range(TAPS):
                    at = slice((base + d) * 8, (base + d) * 8 + 8)
                    first = product_ref[at, :LANES]
                    second = product_ref[at, LANES:]
                    off = d - 3
                    if off > 0:
                        first, second = (
                            pltpu.roll(jnp.where(lane < off, second, first), LANES - off, 1),
                            pltpu.roll(jnp.where(lane < off, 0.0, second), LANES - off, 1),
                        )
                    elif off < 0:
                        first, second = (
                            pltpu.roll(jnp.where(lane >= LANES + off, 0.0, first), -off, 1),
                            pltpu.roll(jnp.where(lane >= LANES + off, first, second), -off, 1),
                        )
                    sums = [
                        part if old is None else old + part
                        for old, part in zip(sums, (first, second))
                    ]
                for s in range(2):
                    out_ref[s, level, i, rows] = sums[s].astype(BF16)


def conv_air_kernel(own_ref, even_ref, odd_ref, packed_ref, matrix_ref, out_ref, product_ref):
    _, levels, band, count, _ = own_ref.shape
    depth = matrix_ref.shape[-1]
    lon = lax.axis_index("lon")
    inner = lax.rem(lon, 2) == 1
    swap_west = jnp.where(lon == 0, 1, 0)
    swap_east = jnp.where(lon == lax.axis_size("lon") - 1, 1, 0)
    channels = pl.num_programs(0) * count
    first = pl.program_id(0) * count + even_ref.shape[0] - (2 * levels * 3 + 1) * channels
    lane = lane_ids(8)
    even, odd = rim_tile(even_ref, odd_ref, first + 2 * levels * 3 * channels, count)
    edge_tiles = [packed_ref[...], jnp.where(inner, even, odd), jnp.where(inner, odd, even)]
    all_tiles = []
    beyond = []
    for h in range(2):
        west_h = jnp.abs(h - swap_west)
        east_h = jnp.abs(h - swap_east)
        tiles = []
        for level in range(levels):
            west, east = [], []
            for i in range(3):
                at = first + ((west_h * levels + level) * 3 + i) * channels
                even, odd = rim_tile(even_ref, odd_ref, at, count)
                west.append(jnp.where(inner, even, odd))
                at = first + ((east_h * levels + level) * 3 + i) * channels
                even, odd = rim_tile(even_ref, odd_ref, at, count)
                east.append(jnp.where(inner, odd, even))
            tiles += west + [own_ref[h, level, i].astype(F32) for i in range(band)] + east
            beyond += [(h, 1, (level * 2 + west_h) * band + i + band - 3) for i in range(3)]
            beyond += [(h, 0, (level * 2 + h) * band + i) for i in range(band)]
            beyond += [(h, 2, (level * 2 + east_h) * band + i) for i in range(3)]
        all_tiles.append(tiles)
    for sub in range(count // 8):
        rows = slice(sub * 8, sub * 8 + 8)
        columns = [[tile[rows] for tile in tiles] for tiles in all_tiles]
        packed = [tile[rows] for tile in edge_tiles]
        edges = [
            [unpack_edge(packed[who], idx, h * 64, lane) for at_h, who, idx in beyond if at_h == h]
            for h in range(2)
        ]
        columns.append([one + two for one, two in zip(*edges)])
        pad = depth - len(columns[0]) * 8
        if pad:
            columns = [tiles + [jnp.zeros((pad, LANES), F32)] for tiles in columns]
        data = jnp.concatenate(
            [jnp.concatenate(tiles, axis=0) for tiles in columns], axis=1
        ).astype(BF16)
        matrix = matrix_ref[sub].reshape(-1, depth)
        product_ref[...] = jnp.dot(matrix, data, preferred_element_type=F32)
        for level in range(levels):
            for i in range(band):
                base = (level * band + i) * TAPS
                sums = [None, None]
                for d in range(TAPS):
                    at = slice((base + d) * 8, (base + d) * 8 + 8)
                    off = d - 3
                    edge = product_ref[at, 2 * LANES :] if off else None
                    for h in range(2):
                        part = product_ref[at, h * LANES : (h + 1) * LANES]
                        if off:
                            here = edge if h == 0 else pltpu.roll(edge, 64, 1)
                            inside = lane < off if off > 0 else lane >= LANES + off
                            part = pltpu.roll(jnp.where(inside, here, part), (LANES - off) % LANES, 1)
                        sums[h] = part if sums[h] is None else sums[h] + part
                for h in range(2):
                    out_ref[h, level, i, rows] = sums[h].astype(BF16)


def convolution(kernel, name, own, even, odd, packed, matrix):
    _, levels, band, channels, _ = own.shape
    groups, pairs, rows, depth = matrix.shape
    count = 16
    lane_tiles = 2 if packed is None else 3
    grid_spec = pl.BlockSpec((2, levels, band, count, LANES), lambda g: (0, 0, 0, g, 0))
    rim_spec = pl.BlockSpec(even.shape, lambda g: (0, 0))
    args = [own, even, odd]
    specs = [grid_spec, rim_spec, rim_spec]
    if packed is not None:
        args.append(packed)
        specs.append(pl.BlockSpec((count, LANES), lambda g: (g, 0)))
    args.append(matrix)
    specs.append(pl.BlockSpec((count // 8, pairs, rows, depth), lambda g: (g, 0, 0, 0)))
    return pl.pallas_call(
        kernel,
        grid=(channels // count,),
        out_shape=jax.ShapeDtypeStruct(own.shape, BF16),
        in_specs=specs,
        out_specs=grid_spec,
        scratch_shapes=[pltpu.VMEM((pairs * rows, lane_tiles * LANES), F32)],
        name=name,
        cost_estimate=pl.CostEstimate(flops=2 * 10**9, bytes_accessed=4 * 10**6, transcendentals=0),
    )(*args)


def mlp_kernel(masked, *refs):
    own_ref, other_ref, gain_ref, up_ref, down_ref, top_ref, forced_ref = refs[:7]
    mask_ref = refs[7] if masked else None
    out_ref, values_ref = refs[-2:]
    _, levels, band, channels, _ = own_ref.shape
    ch = lax.axis_index("ch")
    total = 2 * channels

    def row(at, slot):
        level = at // band
        i = lax.rem(at, band)
        mine = pl.ds(pl.multiple_of(ch * channels, channels), channels)
        theirs = pl.ds(pl.multiple_of((1 - ch) * channels, channels), channels)
        for s in range(2):
            lanes = slice(s * LANES, (s + 1) * LANES)
            values_ref[slot, mine, lanes] = own_ref[s, level, i].astype(F32)
            values_ref[slot, theirs, lanes] = other_ref[s, level, i].astype(F32)
        values = values_ref[slot]
        center = jnp.sum(values, axis=0, keepdims=True) * (1.0 / total)
        values = values - center
        spread = jnp.sum(values * values, axis=0, keepdims=True) * (1.0 / total)
        normed = (values * lax.rsqrt(spread + 1e-06) * gain_ref[...]).astype(BF16)
        raw = jnp.dot(up_ref[...], normed, preferred_element_type=F32)
        inner = raw * (0.7978845608028654 + 0.035677408136300125 * (raw * raw))
        doubled = (raw + raw * jnp.tanh(inner)).astype(BF16)
        update = jnp.dot(down_ref[mine, :], doubled, preferred_element_type=F32) * 0.5
        update = update.astype(BF16).astype(F32)
        if masked:
            mask = mask_ref[...]
            picked = lax.broadcasted_iota(jnp.int32, mask.shape, 0) == i
            sea = jnp.sum(jnp.where(picked, mask.astype(F32), 0.0), axis=0, keepdims=True)
        for s in range(2):
            lanes = slice(s * LANES, (s + 1) * LANES)
            forced = jnp.where(level == 0, top_ref[s, i], forced_ref[s, level, i].astype(F32))
            result = forced + update[:, lanes]
            if masked:
                result = result * sea[:, lanes]
            out_ref[s, level, i] = result.astype(BF16)

    def step(at, carry):
        row(at * 2, 0)
        row(at * 2 + 1, 1)
        return carry

    lax.fori_loop(0, levels * band // 2, step, 0)


def taps_of(kernel):
    return jnp.transpose(kernel, (3, 0, 1, 2)).reshape(TAPS * kernel.shape[0], 3 * TAPS)


def toeplitz(taps, levels, name):
    groups = taps.shape[0] // TAPS // 8
    block = (groups, 1, 2 * TAPS * 8, 256)
    return pl.pallas_call(
        functools.partial(toeplitz_kernel, levels),
        grid=(levels * 2,),
        out_shape=jax.ShapeDtypeStruct((groups, levels * 2) + block[2:], BF16),
        in_specs=[pl.BlockSpec(taps.shape, lambda p: (0, 0))],
        out_specs=pl.BlockSpec(block, lambda p: (0, p, 0, 0)),
        name=name,
        cost_estimate=pl.CostEstimate(flops=10**9, bytes_accessed=3 * 10**6, transcendentals=0),
    )(taps)


def pairs_of(count, first):
    pairs = []
    for i in range(first, count + first, 2):
        pairs += [(i % count, (i + 1) % count), ((i + 1) % count, i % count)]
    return pairs


def ring(count, step):
    return [(i, (i + step) % count) for i in range(count)]


def per_device(
    ocean_state, ocean_mask, air_state, surface_temp, air_fluxes, ocean_kernel, ocean_gain, ocean_up,
    ocean_down, air_kernel, air_gain, air_up, air_down, flux_weight, temp_weight,
):
    o_levels, o_ch, band, lats = ocean_state.shape
    a_levels, a_ch = air_state.shape[:2]
    fields = air_fluxes.shape[0]
    shape = jax.ShapeDtypeStruct

    ocean_grid = jnp.transpose(
        ocean_state.reshape(o_levels, o_ch, band, 2, LANES), (3, 0, 2, 1, 4)
    )
    air_grid = jnp.transpose(air_state, (3, 0, 2, 1, 4))
    o_grid = (2, o_levels, band, o_ch, LANES)
    a_grid = (2, a_levels, band, a_ch, LANES)

    lons = lax.axis_size("lon")
    bands = lax.axis_size("comp") * lons
    lon = lax.axis_index("lon")
    outward = lax.dynamic_slice_in_dim(ocean_grid, jnp.where(lon == 0, 0, band - 3), 3, 2)
    swaps = [(i, (i + lons) % bands) for i in (0, lons - 1, lons, bands - 1)]
    rows = rows_of(fields, band)[-1] + a_ch
    packed = call(
        pack_kernel, shape((rows, LANES), F32), [], "pack", 10**5, 10**6,
        ocean_mask, surface_temp, air_fluxes, air_grid,
    )
    got = lax.ppermute(packed, "comp", ring(2, 1))
    o_tiles = 2 * o_levels * 3
    swapped = lax.ppermute(outward.reshape(o_tiles, o_ch, LANES), ("comp", "lon"), swaps)
    rim = (o_tiles * o_ch + (2 * a_levels * 3 + 1) * a_ch, LANES)
    surface = pltpu.VMEM((4 * band, LANES), F32)
    weights = (flux_weight.T, temp_weight[:, None])
    even_out, odd_out, edge = call(
        force_halo_kernel,
        (shape(rim, BF16), shape(rim, BF16), shape((a_ch, LANES), F32)),
        [surface], "force_halo", 10**6, 4 * 10**6,
        ocean_mask, surface_temp, air_fluxes, got, ocean_grid, swapped, air_grid, *weights,
    )
    even = lax.ppermute(even_out, "lon", pairs_of(lons, 0))
    odd = lax.ppermute(odd_out, "lon", pairs_of(lons, 1))
    ocean_top, air_top, ocean_forced, air_forced = call(
        force_own_kernel,
        (
            shape((2, band, o_ch, LANES), F32), shape((2, band, a_ch, LANES), F32),
            shape(o_grid, BF16), shape(a_grid, BF16),
        ),
        [surface], "force_own", 10**6, 4 * 10**6,
        ocean_mask, surface_temp, air_fluxes, got, ocean_grid, air_grid, *weights,
    )

    o_taps, a_taps, o_gain, a_gain, o_up, a_up, o_down, a_down = lax.optimization_barrier(
        (
            taps_of(ocean_kernel), taps_of(air_kernel), ocean_gain[:, None], air_gain[:, None],
            ocean_up.T, air_up.T, ocean_down.T, air_down.T,
        )
    )
    o_matrix = toeplitz(o_taps, o_levels, "matrix_ocean")
    a_matrix = toeplitz(a_taps, a_levels, "matrix_air")
    a_conv = convolution(conv_air_kernel, "conv_air", air_forced, even, odd, edge, a_matrix)
    a_other = lax.ppermute(a_conv, "ch", ring(2, 1))
    o_conv = convolution(conv_ocean_kernel, "conv_ocean", ocean_forced, even, odd, None, o_matrix)
    o_other = lax.ppermute(o_conv, "ch", ring(2, 1))

    a_next = call(
        functools.partial(mlp_kernel, False), shape(a_grid, BF16),
        [pltpu.VMEM((2, 2 * a_ch, 2 * LANES), F32)], "mlp_air", 10**9, 3 * 10**6,
        a_conv, a_other, a_gain, a_up, a_down, air_top, air_forced,
    )
    o_next = call(
        functools.partial(mlp_kernel, True), shape(o_grid, BF16),
        [pltpu.VMEM((2, 2 * o_ch, 2 * LANES), F32)], "mlp_ocean", 10**9, 3 * 10**6,
        o_conv, o_other, o_gain, o_up, o_down, ocean_top, ocean_forced, ocean_mask,
    )
    ocean_next = jnp.transpose(o_next, (1, 3, 2, 0, 4)).reshape(ocean_state.shape)
    air_next = jnp.transpose(a_next, (1, 3, 2, 0, 4))
    return (ocean_next, air_next)


def solution(mesh):
    in_specs = (
        P(None, "ch", ("comp", "lon"), None),
        P(("comp", "lon"), None),
        P(None, "ch", "lon", None, "comp"),
        P(("comp", "lon"), None),
        P(None, "lon", None, "comp"),
        P("ch", None, None, None),
        P(),
        P(),
        P(),
        P("ch", None, None, None),
        P(),
        P(),
        P(),
        P(None, "ch"),
        P("ch"),
    )
    out_specs = (P(None, "ch", ("comp", "lon"), None), P(None, "ch", "lon", None, "comp"))
    return jax.shard_map(
        per_device, mesh=mesh, in_specs=in_specs, out_specs=out_specs, check_vma=False
    )
```

time: 79.4 us -> 81.4 us (1.025)
  waiting for transfers between devices: 0.25 us -> 5.77 us
  starting transfers between devices: 17.5 us -> 13.5 us
    pallas_call x6 -> x5, Pallas kernels: 29 us -> 20.8 us  [call(): pl.pallas_call(kernel, out_shape=out_shape, in_specs=[VMEM] * len(args),...]
    pallas_call x0 -> x2, Pallas kernels: none -> 8.11 us  [toeplitz(): pl.pallas_call(functools.partial(toeplitz_kernel, levels), grid=(levels *...]
    optimization_barrier x0 -> x4, local copies, waits for them, and re-layouts: none -> 3.25 us  [per_device(): lax.optimization_barrier((taps_of(ocean_kernel), taps_of(air_kernel), oce...]
    ppermute x1, waiting for transfers between devices: 0.01 us -> 3.19 us  [per_device(): a_other = lax.ppermute(a_conv, 'ch', ring(2, 1))]
    ppermute x4 -> x3, starting transfers between devices: 13.2 us -> 10.3 us  [the longest x1 6.06 us: per_device(): odd = lax.ppermute(odd_out, 'lon', pairs_of(lons, 1))]
    ppermute x1, waiting for transfers between devices: 0.23 us -> 2.57 us  [per_device(): got = lax.ppermute(packed, 'comp', ring(2, 1))]
    reshape x4 -> x2, local copies, waits for them, and re-layouts: 1.91 us -> 0.17 us  [taps_of(): jnp.transpose(kernel, (3, 0, 1, 2))]
    broadcast_in_dim x3 -> x1, local copies, waits for them, and re-layouts: 2.2 us -> 0.72 us  [per_device(): weights = (flux_weight.T, temp_weight[:, None])]
  transfers between devices with their start and end apart: 7 -> 6, of which waited for: 1 -> 2; matrix products, arithmetic and copies ran while one was open for 15% -> 15% of each run, Pallas kernels for 36% -> 30%
where the time goes in v3:
time: 81.4 us; the launch traced here: 80.7 us
  Pallas kernels  41.4 us (51%)
  local copies, waits for them, and re-layouts  19.2 us (24%)
  starting transfers between devices  13.5 us (17%)
  waiting for transfers between devices  5.77 us (7%)
    pallas_call x5, Pallas kernels, call(): pl.pallas_call(kernel, out_shape=out_shape, in_specs=[VMEM] * len(args),...  20.8 us
    unnamed x38, local copies, waits for them, and re-layouts  12.8 us
    pallas_call x2, Pallas kernels, convolution(): pl.pallas_call(kernel, grid=(channels // count,), out_shape=jax.ShapeDtyp...  12.5 us
    pallas_call x2, Pallas kernels, toeplitz(): pl.pallas_call(functools.partial(toeplitz_kernel, levels), grid=(levels *...  8.11 us
    ppermute x1, starting transfers between devices, per_device(): odd = lax.ppermute(odd_out, 'lon', pairs_of(lons, 1))  6.06 us
    ppermute x1, starting transfers between devices, per_device(): lax.ppermute(outward.reshape(o_tiles, o_ch, LANES), ('comp', 'lon'), swaps)  4.2 us
    optimization_barrier x4, local copies, waits for them, and re-layouts, per_device(): lax.optimization_barrier((taps_of(ocean_kernel), taps_of(air_kernel), oce...  3.25 us
    ppermute x1, waiting for transfers between devices, per_device(): a_other = lax.ppermute(a_conv, 'ch', ring(2, 1))  3.19 us
  transfers between devices with their start and end apart: 6, of which 2 were waited for; matrix products, arithmetic and copies ran while one was open for 15% of the time, Pallas kernels for 30%

profile of v3, /device:TPU:8, one launch (start us, length us, event | category | flops | bytes accessed | tf_op | source)
XLA Modules:
  0.0 80.7 jit_solution(17011907035062759762)
XLA Ops:
  0.7 1.2 %reshape.24 = bf16[3,64,4,2,128]{4,3,2,1,0:T(2,128)(2,1)S(1)} reshape(bf16[3,64,4,256]{3,2,1,0:T(4,128)(2,1)} %param.15) | data formatting | bytes 786432 | tf_op jit(solution)/shard_map/reshape | solution.py:472
  2.2 4.2 %collective-permute-start.1 = (bf16[18,64,128]{2,1,0:T(8,128)(2,1)S(1)}, bf16[18,64,128]{2,1,0:T(8,128)(2,1)S(1)}, u32[]{:S(2)}, u32[]{:S(2)}) collective-permute-start(bf16[18,64,128]{2,1,0:T(8,128)(2,1)S(1)} %bitcast.34), channel_id=1, source_target_pairs={{0,128},{126,254},{128,0},{254,126},{1,129},{127,255},{129,1},{255... | collective-permute-start | bytes 884744 | tf_op jit(solution)/shard_map/ppermute | solution.py:490
  6.4 1.8 %copy.54 = bf16[2,96,4,2,128]{4,1,2,0,3:T(8,128)(2,1)} copy(bf16[2,96,4,2,128]{4,3,2,1,0:T(2,128)(2,1)} %param.17) | data formatting | bytes 786432 | tf_op args[2]
  8.2 1.8 %pack.1 = f32[144,128]{1,0:T(8,128)} custom-call(s32[4,256]{1,0:T(4,128)} %refs_7_.1, f32[4,256]{1,0:T(4,128)} %temp_ref.5, f32[4,4,2,128]{3,2,1,0:T(2,128)} %flux_ref.5, bf16[2,2,4,96,128]{4,3,2,1,0:T(8,128)(2,1)} %bitcast.26), custom_call_target="tpu_custom_call" | custom-call | flops 100000 | bytes 1000000 | tf_op jit(solution)/shard_map/pack/pallas_call | solution.py:21
  10.0 1.2 %collective-permute-start = (f32[144,128]{1,0:T(8,128)}, f32[144,128]{1,0:T(8,128)S(1)}, u32[]{:S(2)}, u32[]{:S(2)}) collective-permute-start(f32[144,128]{1,0:T(8,128)} %pack.1), channel_id=1, source_target_pairs={{0,128},{128,0},{1,129},{129,1},{2,130},{130,2},{3,131},{131,3},{4... | collective-permute-start | bytes 221192 | tf_op jit(solution)/shard_map/ppermute | solution.py:488
  11.3 0.8 %copy.53 = bf16[3,64,4,2,128]{4,1,2,0,3:T(8,128)(2,1)} copy(bf16[3,64,4,2,128]{4,3,2,1,0:T(2,128)(2,1)S(1)} %reshape.24) | data formatting | bytes 786432 | tf_op jit(solution)/shard_map/reshape | solution.py:472
  13.5 2.6 %collective-permute-done.got_ref = f32[144,128]{1,0:T(8,128)S(1)} collective-permute-done((f32[144,128]{1,0:T(8,128)}, f32[144,128]{1,0:T(8,128)S(1)}, u32[]{:S(2)}, u32[]{:S(2)}) %collective-permute-start) | collective-permute-done | bytes 73760 | tf_op jit(solution)/shard_map/ppermute | solution.py:488
  16.9 3.0 %force_halo.1 = (bf16[2400,128]{1,0:T(8,128)(2,1)}, bf16[2400,128]{1,0:T(8,128)(2,1)}, f32[96,128]{1,0:T(8,128)}) custom-call(s32[4,256]{1,0:T(4,128)} %refs_7_.1, f32[4,256]{1,0:T(4,128)} %temp_ref.5, f32[4,4,2,128]{3,2,1,0:T(2,128)} %flux_ref.5, f32[144,128]{1,0:T(8,128)} %copy-done.2, bf16[2,3,4,64,128]{4,3,2,1,0:T(8,128)(2,1)} %bitcast.29, ...), custom_call_target="tpu_custom_call" | custom-call | flops 1000000 | bytes 4000000 | tf_op jit(solution)/shard_map/force_halo/pallas_call | solution.py:21
  19.9 6.1 %collective-permute-start.3 = (bf16[2400,128]{1,0:T(8,128)(2,1)}, bf16[2400,128]{1,0:T(8,128)(2,1)S(1)}, u32[]{:S(2)}, u32[]{:S(2)}) collective-permute-start(bf16[2400,128]{1,0:T(8,128)(2,1)} %get-tuple-element.19), channel_id=1, source_target_pairs={{2,4},{4,2},{6,8},{8,6},{10,12},{12,10},{14,16},{16,14},{18,20},{2... | collective-permute-start | bytes 1843208 | tf_op jit(solution)/shard_map/ppermute | solution.py:501
  26.0 0.9 %copy.36 = bf16[192,768]{0,1:T(8,128)(2,1)} copy(bf16[192,768]{1,0:T(8,128)(2,1)S(1)} %copy-done.1) | data formatting | bytes 589824 | tf_op args[11]
  28.6 0.9 %copy.41.taps_ref = f32[672,21]{1,0:T(8,128)} copy(f32[672,21]{0,1:T(8,128)S(1)} %reshape.22) | data formatting | bytes 112896 | tf_op jit(solution)/shard_map/optimization_barrier | solution.py:512
  29.5 0.8 %copy.38.taps_ref = f32[448,21]{1,0:T(8,128)} copy(f32[448,21]{0,1:T(8,128)S(1)} %reshape.21) | data formatting | bytes 75264 | tf_op jit(solution)/shard_map/optimization_barrier | solution.py:512
  30.3 3.8 %matrix_air.1.matrix_ref = bf16[12,4,112,256]{3,2,1,0:T(8,128)(2,1)} custom-call(f32[672,21]{1,0:T(8,128)} %copy.41.taps_ref), custom_call_target="tpu_custom_call" | custom-call | flops 1000000000 | bytes 3000000 | tf_op jit(solution)/shard_map/matrix_air/pallas_call | solution.py:440
  34.1 4.4 %matrix_ocean.1.matrix_ref = bf16[8,6,112,256]{3,2,1,0:T(8,128)(2,1)} custom-call(f32[448,21]{1,0:T(8,128)} %copy.38.taps_ref), custom_call_target="tpu_custom_call" | custom-call | flops 1000000000 | bytes 3000000 | tf_op jit(solution)/shard_map/matrix_ocean/pallas_call | solution.py:440
  38.5 2.6 %force_own.1 = (f32[2,4,64,128]{3,2,1,0:T(8,128)}, f32[2,4,96,128]{3,2,1,0:T(8,128)}, bf16[2,3,4,64,128]{4,3,2,1,0:T(8,128)(2,1)}, bf16[2,2,4,96,128]{4,3,2,1,0:T(8,128)(2,1)}) custom-call(s32[4,256]{1,0:T(4,128)} %refs_7_.1, f32[4,256]{1,0:T(4,128)} %temp_ref.5, f32[4,4,2,128]{3,2,1,0:T(2,128)} %flux_ref.5, f32[144,128]{1,0:T(8,128)} %copy-done.2, ...), custom_call_target="tpu_custom_call" | custom-call | flops 1000000 | bytes 4000000 | tf_op jit(solution)/shard_map/force_own/pallas_call | solution.py:21
  42.1 7.4 %conv_air.1.refs_0_ = bf16[2,2,4,96,128]{4,3,2,1,0:T(8,128)(2,1)} custom-call(bf16[2,2,4,96,128]{4,3,2,1,0:T(8,128)(2,1)} %get-tuple-element.25.own_ref.refs_6_, bf16[2400,128]{1,0:T(8,128)(2,1)} %copy-done.11, bf16[2400,128]{1,0:T(8,128)(2,1)} %copy-done.12, f32[96,128]{1,0:T(8,128)} %get-tuple-element.26.packed_ref, ...), custom_call_target="tpu_custom_call" | custom-call | flops 2000000000 | bytes 4000000 | tf_op jit(solution)/shard_map/conv_air/pallas_call | solution.py:374
  49.5 1.3 %collective-permute-start.5 = (bf16[2,2,4,96,128]{4,3,2,1,0:T(8,128)(2,1)}, bf16[2,2,4,96,128]{4,3,2,1,0:T(8,128)(2,1)S(1)}, u32[]{:S(2)}, u32[]{:S(2)}) collective-permute-start(bf16[2,2,4,96,128]{4,3,2,1,0:T(8,128)(2,1)} %conv_air.1.refs_0_), channel_id=1, source_target_pairs={{0,1},{1,0},{2,3},{3,2},{4,5},{5,4},{6,7},{7,6},{8,9},{9,8},{10,11... | collective-permute-start | bytes 1179656 | tf_op jit(solution)/shard_map/ppermute | solution.py:521
  50.9 5.2 %conv_ocean.1.refs_0_ = bf16[2,3,4,64,128]{4,3,2,1,0:T(8,128)(2,1)} custom-call(bf16[2,3,4,64,128]{4,3,2,1,0:T(8,128)(2,1)} %get-tuple-element.17.own_ref.refs_6_, bf16[2400,128]{1,0:T(8,128)(2,1)} %copy-done.11, bf16[2400,128]{1,0:T(8,128)(2,1)} %copy-done.12, bf16[8,6,112,256]{3,2,1,0:T(8,128)(2,1)} %matrix_ocean.1.matrix_ref), custom_call_target="tpu_custom_call" | custom-call | flops 2000000000 | bytes 4000000 | tf_op jit(solution)/shard_map/conv_ocean/pallas_call | solution.py:374
  58.2 3.2 %collective-permute-done.5.refs_1_ = bf16[2,2,4,96,128]{4,3,2,1,0:T(8,128)(2,1)S(1)} collective-permute-done((bf16[2,2,4,96,128]{4,3,2,1,0:T(8,128)(2,1)}, bf16[2,2,4,96,128]{4,3,2,1,0:T(8,128)(2,1)S(1)}, u32[]{:S(2)}, u32[]{:S(2)}) %collective-permute-start.5) | collective-permute-done | bytes 393248 | tf_op jit(solution)/shard_map/ppermute | solution.py:521
  62.1 6.3 %mlp_air.1 = bf16[2,2,4,96,128]{4,3,2,1,0:T(8,128)(2,1)} custom-call(bf16[2,2,4,96,128]{4,3,2,1,0:T(8,128)(2,1)} %conv_air.1.refs_0_, bf16[2,2,4,96,128]{4,3,2,1,0:T(8,128)(2,1)} %copy-done.14, f32[192,1]{1,0:T(8,128)} %copy.42.refs_2_, bf16[768,192]{1,0:T(8,128)(2,1)} %bitcast.33, bf16[192,768]{1,0:T(8,128)(2,1)} %bitcast.44, ...), custom_call_target="tpu_custom_call" | custom-call | flops 1000000000 | bytes 3000000 | tf_op jit(solution)/shard_map/mlp_air/pallas_call | solution.py:21
  68.5 2.1 %copy.44 = bf16[2,96,4,2,128]{4,3,2,1,0:T(2,128)(2,1)} copy(bf16[2,96,4,2,128]{4,1,2,0,3:T(8,128)(2,1)} %bitcast.32) | data formatting | bytes 786432
  71.4 6.9 %mlp_ocean.1 = bf16[2,3,4,64,128]{4,3,2,1,0:T(8,128)(2,1)} custom-call(bf16[2,3,4,64,128]{4,3,2,1,0:T(8,128)(2,1)} %conv_ocean.1.refs_0_, bf16[2,3,4,64,128]{4,3,2,1,0:T(8,128)(2,1)} %copy-done.13, f32[128,1]{1,0:T(8,128)} %copy.39.refs_2_, bf16[512,128]{1,0:T(8,128)(2,1)} %bitcast.37, bf16[128,512]{1,0:T(8,128)(2,1)} %bitcast.38, ...), custom_call_target="tpu_custom_call" | custom-call | flops 1000000000 | bytes 3000000 | tf_op jit(solution)/shard_map/mlp_ocean/pallas_call | solution.py:21
  78.3 1.4 %copy.47 = bf16[3,64,4,2,128]{4,3,2,1,0:T(2,128)(2,1)S(1)} copy(bf16[3,64,4,2,128]{4,1,2,0,3:T(8,128)(2,1)} %bitcast.31) | data formatting | bytes 786432
  79.7 1.0 %reshape.25 = bf16[3,64,4,256]{3,2,1,0:T(4,128)(2,1)} reshape(bf16[3,64,4,2,128]{4,3,2,1,0:T(2,128)(2,1)S(1)} %copy.47) | data formatting | bytes 786432
  (46 shorter events, 8.9 us)
Async XLA Ops:
  0.6 11.5 %copy-start.9 = (f32[96]{0:T(128)S(1)}, f32[96]{0:T(128)}, u32[]{:S(2)}) copy-start(f32[96]{0:T(128)} %param.29) | copy-start | bytes 1156
  0.6 12.2 %copy-start.7 = (f32[4,64]{1,0:T(4,128)S(1)}, f32[4,64]{1,0:T(4,128)}, u32[]{:S(2)}) copy-start(f32[4,64]{1,0:T(4,128)} %param.28) | copy-start | bytes 3076
  0.7 25.3 %copy-start.1 = (bf16[192,768]{1,0:T(8,128)(2,1)S(1)}, bf16[192,768]{1,0:T(8,128)(2,1)}, u32[]{:S(2)}) copy-start(bf16[192,768]{1,0:T(8,128)(2,1)} %param.26) | copy-start | bytes 884740
  1.9 25.0 %copy-start.3 = (bf16[128,512]{1,0:T(8,128)(2,1)S(1)}, bf16[128,512]{1,0:T(8,128)(2,1)}, u32[]{:S(2)}) copy-start(bf16[128,512]{1,0:T(8,128)(2,1)} %param.22) | copy-start | bytes 393220
  1.9 25.8 %copy-start.4 = (bf16[512,128]{1,0:T(8,128)(2,1)S(1)}, bf16[512,128]{1,0:T(8,128)(2,1)}, u32[]{:S(2)}) copy-start(bf16[512,128]{1,0:T(8,128)(2,1)} %param.23) | copy-start | bytes 393220
  2.1 26.3 %copy-start.5 = (f32[96,3,7,7]{0,3,2,1:T(8,128)S(1)}, f32[96,3,7,7]{0,3,2,1:T(8,128)}, u32[]{:S(2)}) copy-start(f32[96,3,7,7]{0,3,2,1:T(8,128)} %param.24) | copy-start | bytes 169348
  2.1 26.4 %copy-start.6 = (f32[64,3,7,7]{0,3,2,1:T(8,128)S(1)}, f32[64,3,7,7]{0,3,2,1:T(8,128)}, u32[]{:S(2)}) copy-start(f32[64,3,7,7]{0,3,2,1:T(8,128)} %param.20) | copy-start | bytes 112900
  2.2 13.9 %collective-permute-start.1 = (bf16[18,64,128]{2,1,0:T(8,128)(2,1)S(1)}, bf16[18,64,128]{2,1,0:T(8,128)(2,1)S(1)}, u32[]{:S(2)}, u32[]{:S(2)}) collective-permute-start(bf16[18,64,128]{2,1,0:T(8,128)(2,1)S(1)} %bitcast.34), channel_id=1, source_target_pairs={{0,128},{126,254},{128,0},{254,126},{1,129},{127,255},{129,1},{255... | collective-permute-start | bytes 884744 | tf_op jit(solution)/shard_map/ppermute | solution.py:490
  10.0 6.1 %collective-permute-start = (f32[144,128]{1,0:T(8,128)}, f32[144,128]{1,0:T(8,128)S(1)}, u32[]{:S(2)}, u32[]{:S(2)}) collective-permute-start(f32[144,128]{1,0:T(8,128)} %pack.1), channel_id=1, source_target_pairs={{0,128},{128,0},{1,129},{129,1},{2,130},{130,2},{3,131},{131,3},{4... | collective-permute-start | bytes 221192 | tf_op jit(solution)/shard_map/ppermute | solution.py:488
  16.1 0.6 copy-start.2
  16.1 0.7 copy-start
  19.9 21.2 %collective-permute-start.2 = (bf16[2400,128]{1,0:T(8,128)(2,1)}, bf16[2400,128]{1,0:T(8,128)(2,1)S(1)}, u32[]{:S(2)}, u32[]{:S(2)}) collective-permute-start(bf16[2400,128]{1,0:T(8,128)(2,1)} %get-tuple-element.18), channel_id=1, source_target_pairs={{0,2},{2,0},{4,6},{6,4},{8,10},{10,8},{12,14},{14,12},{16,18},{18,... | collective-permute-start | bytes 1843208 | tf_op jit(solution)/shard_map/ppermute | solution.py:500
  19.9 21.2 %collective-permute-start.3 = (bf16[2400,128]{1,0:T(8,128)(2,1)}, bf16[2400,128]{1,0:T(8,128)(2,1)S(1)}, u32[]{:S(2)}, u32[]{:S(2)}) collective-permute-start(bf16[2400,128]{1,0:T(8,128)(2,1)} %get-tuple-element.19), channel_id=1, source_target_pairs={{2,4},{4,2},{6,8},{8,6},{10,12},{12,10},{14,16},{16,14},{18,20},{2... | collective-permute-start | bytes 1843208 | tf_op jit(solution)/shard_map/ppermute | solution.py:501
  41.1 0.8 %copy-start.11 = (bf16[2400,128]{1,0:T(8,128)(2,1)}, bf16[2400,128]{1,0:T(8,128)(2,1)S(1)}, u32[]{:S(2)}) copy-start(bf16[2400,128]{1,0:T(8,128)(2,1)S(1)} %collective-permute-done.2.even_ref) | copy-start | bytes 1843204
  41.1 1.0 %copy-start.12 = (bf16[2400,128]{1,0:T(8,128)(2,1)}, bf16[2400,128]{1,0:T(8,128)(2,1)S(1)}, u32[]{:S(2)}) copy-start(bf16[2400,128]{1,0:T(8,128)(2,1)S(1)} %collective-permute-done.3.odd_ref) | copy-start | bytes 1843204
  49.5 11.9 %collective-permute-start.5 = (bf16[2,2,4,96,128]{4,3,2,1,0:T(8,128)(2,1)}, bf16[2,2,4,96,128]{4,3,2,1,0:T(8,128)(2,1)S(1)}, u32[]{:S(2)}, u32[]{:S(2)}) collective-permute-start(bf16[2,2,4,96,128]{4,3,2,1,0:T(8,128)(2,1)} %conv_air.1.refs_0_), channel_id=1, source_target_pairs={{0,1},{1,0},{2,3},{3,2},{4,5},{5,4},{6,7},{7,6},{8,9},{9,8},{10,11... | collective-permute-start | bytes 1179656 | tf_op jit(solution)/shard_map/ppermute | solution.py:521
  50.9 5.8 %copy-start.8 = (f32[192]{0:T(256)S(1)}, f32[192]{0:T(256)}, u32[]{:S(2)}) copy-start(f32[192]{0:T(256)} %param.25) | copy-start | bytes 2308
  50.9 6.6 %copy-start.10 = (f32[128]{0:T(128)S(1)}, f32[128]{0:T(128)}, u32[]{:S(2)}) copy-start(f32[128]{0:T(128)} %param.21) | copy-start | bytes 1540
  56.0 14.6 %collective-permute-start.4 = (bf16[2,3,4,64,128]{4,3,2,1,0:T(8,128)(2,1)}, bf16[2,3,4,64,128]{4,3,2,1,0:T(8,128)(2,1)S(1)}, u32[]{:S(2)}, u32[]{:S(2)}) collective-permute-start(bf16[2,3,4,64,128]{4,3,2,1,0:T(8,128)(2,1)} %conv_ocean.1.refs_0_), channel_id=1, source_target_pairs={{0,1},{1,0},{2,3},{3,2},{4,5},{5,4},{6,7},{7,6},{8,9},{9,8},{10,11... | collective-permute-start | bytes 1179656 | tf_op jit(solution)/shard_map/ppermute | solution.py:523
  61.4 0.8 copy-start.14
  70.6 0.8 copy-start.13

commit v4 on v3

--- a/solution.py
+++ b/solution.py
@@ -10,11 +10,18 @@
 F32 = jnp.float32
 BF16 = jnp.bfloat16
 LANES = 128
+PARAMS = pltpu.CompilerParams(vmem_limit_bytes=24 * 2**20)
 VMEM = pl.BlockSpec(memory_space=pltpu.VMEM)
 
 
 def lane_ids(rows):
     return lax.broadcasted_iota(jnp.int32, (rows, LANES), 1)
+
+
+def column(row):
+    n = row.shape[1]
+    same = lax.broadcasted_iota(jnp.int32, (n, n), 0) == lax.broadcasted_iota(jnp.int32, (n, n), 1)
+    return jnp.sum(jnp.where(same, row, 0.0), axis=1, keepdims=True)
 
 
 def call(kernel, out_shape, scratch, name, flops, moved, *args):
@@ -25,6 +32,7 @@
         out_specs=jax.tree.map(lambda _: VMEM, out_shape),
         scratch_shapes=scratch,
         name=name,
+        compiler_params=PARAMS,
         cost_estimate=pl.CostEstimate(flops=flops, bytes_accessed=moved, transcendentals=0),
     )(*args)
 
@@ -57,9 +65,9 @@
             for j in range(band):
                 idx = (level * 2 + h) * band + j
                 rolled = pltpu.roll(
-                    air_ref[h, level, j].astype(F32), lax.rem(8 * idx - start + LANES, LANES), 1
+                    air_ref[h, level, j].astype(F32), (8 * idx - start + LANES) & (LANES - 1), 1
                 )
-                packed = jnp.where(lane // 8 == idx, rolled, packed)
+                packed = jnp.where((lane >> 3) == idx, rolled, packed)
     out_ref[edge_row : edge_row + channels, :] = packed
 
 
@@ -73,14 +81,14 @@
         surface_ref[(2 + s) * band : (3 + s) * band, :] = sea[:, lanes]
 
 
-def inject_of(flux_ref, got_ref, fw_ref, half, s, i):
+def inject_of(flux_ref, got_ref, fw, half, s, i):
     comp = lax.axis_index("comp")
     fields, band = flux_ref.shape[:2]
     total = None
     for k in range(fields):
         mine = flux_ref[k, i, pl.ds(half, 1), :]
         theirs = got_ref[pl.ds((k * band + i) * 2 + half, 1), :]
-        term = fw_ref[:, k : k + 1] * jnp.where(comp == s, mine, theirs)
+        term = fw[k] * jnp.where(comp == s, mine, theirs)
         total = term if total is None else total + term
     return total
 
@@ -99,14 +107,15 @@
 ):
     comp = lax.axis_index("comp")
     lon = lax.axis_index("lon")
-    parity = lax.rem(lon, 2)
+    parity = (lon & 1)
     at_end = (lon == 0) | (lon == lax.axis_size("lon") - 1)
     fields, band = flux_ref.shape[:2]
     o_levels, o_ch = ocean_ref.shape[1], ocean_ref.shape[3]
     a_levels, a_ch = air_ref.shape[1], air_ref.shape[3]
     temp_row, sea_row, edge_row = rows_of(fields, band)
     fill_surface(mask_ref, temp_ref, surface_ref)
-    heat = tw_ref[...]
+    heat = column(tw_ref[...])
+    fw = [column(fw_ref[k : k + 1, :]) for k in range(fields)]
 
     start = jnp.where(comp == 0, 0, LANES - 8)
     lane = lane_ids(8)
@@ -116,9 +125,9 @@
             idx = h * band + j
             row = temp_of(surface_ref, got_ref, fields, band, h, 1 - comp, j)
             rolled = pltpu.roll(
-                jnp.broadcast_to(row, (8, LANES)), lax.rem(8 * idx - start + LANES, LANES), 1
+                jnp.broadcast_to(row, (8, LANES)), (8 * idx - start + LANES) & (LANES - 1), 1
             )
-            edge_temp = jnp.where(lane // 8 == idx, rolled, edge_temp)
+            edge_temp = jnp.where((lane >> 3) == idx, rolled, edge_temp)
     edge = got_ref[edge_row : edge_row + a_ch, :] + heat * edge_temp[0:1, :]
     edge_ref[...] = edge
 
@@ -128,7 +137,7 @@
             col = j + offset
             half = comp if outer is None else jnp.where(outer, 1 - comp, comp)
             for s in range(2):
-                inject = inject_of(flux_ref, got_ref, fw_ref, half, s, col)
+                inject = inject_of(flux_ref, got_ref, fw, half, s, col)
                 sea = surface_ref[pl.ds((2 + s) * band + col, 1), :]
                 if outer is not None:
                     sea = jnp.where(outer, got_ref[pl.ds(sea_row + s * band + col, 1), :], sea)
@@ -160,10 +169,11 @@
     fields, band = flux_ref.shape[:2]
     o_levels, a_levels = ocean_ref.shape[1], air_ref.shape[1]
     fill_surface(mask_ref, temp_ref, surface_ref)
-    heat = tw_ref[...]
+    heat = column(tw_ref[...])
+    fw = [column(fw_ref[k : k + 1, :]) for k in range(fields)]
     for s in range(2):
         for i in range(band):
-            inject = inject_of(flux_ref, got_ref, fw_ref, comp, s, i)
+            inject = inject_of(flux_ref, got_ref, fw, comp, s, i)
             at = (2 + s) * band + i
             sea = surface_ref[at : at + 1, :]
             row = temp_of(surface_ref, got_ref, fields, band, s, comp, i)
@@ -185,45 +195,56 @@
 
 def unpack_edge(packed, idx, shift, lane):
     comp = lax.axis_index("comp")
-    start = lax.rem(jnp.where(comp == 0, 0, LANES - 8) + shift, LANES)
-    rolled = pltpu.roll(packed, lax.rem(start - 8 * idx + 2 * LANES, LANES), 1)
-    return jnp.where(lane // 8 == start // 8, rolled, 0.0)
+    start = (jnp.where(comp == 0, 0, LANES - 8) + shift) & (LANES - 1)
+    rolled = pltpu.roll(packed, (start - 8 * idx + 2 * LANES) & (LANES - 1), 1)
+    return jnp.where((lane >> 3) == (start >> 3), rolled, 0.0)
 
 
 TAPS = 7
 
 
-def toeplitz_kernel(levels, taps_ref, out_ref):
-    groups, _, rows, depth = out_ref.shape
+def toeplitz_kernel(taps_ref, out_ref, rows_ref):
+    groups, levels, _, depth = out_ref.shape
     channels = groups * 8
-    pair = pl.program_id(0)
-    window = taps_ref.shape[1]
-    taps = taps_ref[...].astype(BF16)
+    for d in range(TAPS):
+        rows_ref[d] = jnp.zeros(rows_ref.shape[1:], F32)
+        for a in range(3):
+            for b in range(TAPS):
+                at = a * TAPS + b
+                rows_ref[d, at : at + 1, :channels] = taps_ref[a, b, d : d + 1, :]
+    window = rows_ref.shape[1]
+    taps = [rows_ref[d].T[:channels].astype(BF16) for d in range(TAPS)]
+    taps = jnp.concatenate(taps, axis=0)
     row = lax.broadcasted_iota(jnp.int32, (window, depth), 0)
     lane = lax.broadcasted_iota(jnp.int32, (window, depth), 1)
     from_level = lane // 80
-    from_lon = lane // 8 - from_level * 10
+    from_lon = (lane >> 3) - from_level * 10
     same = (lax.broadcasted_iota(jnp.int32, (8, depth), 1) & 7) == lax.broadcasted_iota(
         jnp.int32, (8, depth), 0
     )
-    level = pair // 2
-    parts = []
-    for side in range(2):
-        a = from_level - level + 1
-        b = from_lon - (lax.rem(pair, 2) * 2 + side)
-        hit = (
-            (from_level < levels)
-            & (a >= 0) & (a <= 2) & (b >= 0) & (b < TAPS) & (a * TAPS + b == row)
-        )
-        choose = jnp.where(hit, 1.0, 0.0).astype(BF16)
-        parts.append(jnp.dot(taps, choose, preferred_element_type=F32))
-    for g in range(groups):
-        tiles = [
-            jnp.where(same, part[d * channels + g * 8 : d * channels + g * 8 + 8], 0.0)
-            for part in parts
-            for d in range(TAPS)
-        ]
-        out_ref[g, 0] = jnp.concatenate(tiles, axis=0).astype(BF16)
+    for level in range(levels):
+        parts = []
+        for side in range(2):
+            a = from_level - level + 1
+            b = from_lon - (pl.program_id(0) * 2 + side)
+            hit = (
+                (from_level < levels)
+                & (a >= 0) & (a <= 2) & (b >= 0) & (b < TAPS) & (a * TAPS + b == row)
+            )
+            choose = jnp.where(hit, 1.0, 0.0).astype(BF16)
+            parts.append(jnp.dot(taps, choose, preferred_element_type=F32))
+        for g in range(groups):
+            tiles = [
+                jnp.where(same, part[d * channels + g * 8 : d * channels + g * 8 + 8], 0.0)
+                for part in parts
+                for d in range(TAPS)
+            ]
+            out_ref[g, level] = jnp.concatenate(tiles, axis=0).astype(BF16)
+
+
+def both_toeplitz_kernel(o_ref, a_ref, o_out, a_out, o_rows, a_rows):
+    toeplitz_kernel(a_ref, a_out, a_rows)
+    toeplitz_kernel(o_ref, o_out, o_rows)
 
 
 def rim_tile(even_ref, odd_ref, at, count):
@@ -237,7 +258,7 @@
     lane = lane_ids(8)
     channels = pl.num_programs(0) * count
     first = pl.program_id(0) * count
-    inner = lax.rem(lax.axis_index("lon"), 2) == 1
+    inner = (lax.axis_index("lon") & 1) == 1
     columns = []
     for s in range(2):
         tiles = []
@@ -264,7 +285,7 @@
         product_ref[...] = jnp.dot(matrix, data, preferred_element_type=F32)
         for level in range(levels):
             for i in range(band):
-                base = (level * band + i) * TAPS
+                base = ((i // 2 * levels + level) * 2 + i % 2) * TAPS
                 sums = [None, None]
                 for d in range(TAPS):
                     at = slice((base + d) * 8, (base + d) * 8 + 8)
@@ -293,7 +314,7 @@
     _, levels, band, count, _ = own_ref.shape
     depth = matrix_ref.shape[-1]
     lon = lax.axis_index("lon")
-    inner = lax.rem(lon, 2) == 1
+    inner = (lon & 1) == 1
     swap_west = jnp.where(lon == 0, 1, 0)
     swap_east = jnp.where(lon == lax.axis_size("lon") - 1, 1, 0)
     channels = pl.num_programs(0) * count
@@ -340,7 +361,7 @@
         product_ref[...] = jnp.dot(matrix, data, preferred_element_type=F32)
         for level in range(levels):
             for i in range(band):
-                base = (level * band + i) * TAPS
+                base = ((i // 2 * levels + level) * 2 + i % 2) * TAPS
                 sums = [None, None]
                 for d in range(TAPS):
                     at = slice((base + d) * 8, (base + d) * 8 + 8)
@@ -379,6 +400,7 @@
         out_specs=grid_spec,
         scratch_shapes=[pltpu.VMEM((pairs * rows, lane_tiles * LANES), F32)],
         name=name,
+        compiler_params=PARAMS,
         cost_estimate=pl.CostEstimate(flops=2 * 10**9, bytes_accessed=4 * 10**6, transcendentals=0),
     )(*args)
 
@@ -386,10 +408,18 @@
 def mlp_kernel(masked, *refs):
     own_ref, other_ref, gain_ref, up_ref, down_ref, top_ref, forced_ref = refs[:7]
     mask_ref = refs[7] if masked else None
-    out_ref, values_ref = refs[-2:]
+    out_ref, values_ref, wide_ref, narrow_ref = refs[-4:]
     _, levels, band, channels, _ = own_ref.shape
     ch = lax.axis_index("ch")
     total = 2 * channels
+    gain = column(gain_ref[...])
+    wide_ref[...] = up_ref[...].astype(F32).T.astype(BF16)
+    mine = pl.ds(pl.multiple_of(ch * channels, channels), channels)
+    if masked:
+        narrow_ref[...] = down_ref[...].astype(F32).T.astype(BF16)
+    else:
+        narrow_ref[: channels] = down_ref[mine, :]
+    down_rows = mine if masked else slice(0, channels)
 
     def row(at, slot):
         level = at // band
@@ -404,11 +434,11 @@
         center = jnp.sum(values, axis=0, keepdims=True) * (1.0 / total)
         values = values - center
         spread = jnp.sum(values * values, axis=0, keepdims=True) * (1.0 / total)
-        normed = (values * lax.rsqrt(spread + 1e-06) * gain_ref[...]).astype(BF16)
-        raw = jnp.dot(up_ref[...], normed, preferred_element_type=F32)
+        normed = (values * lax.rsqrt(spread + 1e-06) * gain).astype(BF16)
+        raw = jnp.dot(wide_ref[...], normed, preferred_element_type=F32)
         inner = raw * (0.7978845608028654 + 0.035677408136300125 * (raw * raw))
         doubled = (raw + raw * jnp.tanh(inner)).astype(BF16)
-        update = jnp.dot(down_ref[mine, :], doubled, preferred_element_type=F32) * 0.5
+        update = jnp.dot(narrow_ref[down_rows, :], doubled, preferred_element_type=F32) * 0.5
         update = update.astype(BF16).astype(F32)
         if masked:
             mask = mask_ref[...]
@@ -430,22 +460,26 @@
     lax.fori_loop(0, levels * band // 2, step, 0)
 
 
-def taps_of(kernel):
-    return jnp.transpose(kernel, (3, 0, 1, 2)).reshape(TAPS * kernel.shape[0], 3 * TAPS)
-
-
-def toeplitz(taps, levels, name):
-    groups = taps.shape[0] // TAPS // 8
-    block = (groups, 1, 2 * TAPS * 8, 256)
+def toeplitz(ocean_kernel, air_kernel, o_levels, a_levels):
+    taps = [jnp.transpose(kernel, (1, 2, 3, 0)) for kernel in (ocean_kernel, air_kernel)]
+    shapes = [
+        (part.shape[-1] // 8, levels, 2 * TAPS * 8, 256)
+        for part, levels in zip(taps, (o_levels, a_levels))
+    ]
     return pl.pallas_call(
-        functools.partial(toeplitz_kernel, levels),
-        grid=(levels * 2,),
-        out_shape=jax.ShapeDtypeStruct((groups, levels * 2) + block[2:], BF16),
-        in_specs=[pl.BlockSpec(taps.shape, lambda p: (0, 0))],
-        out_specs=pl.BlockSpec(block, lambda p: (0, p, 0, 0)),
-        name=name,
-        cost_estimate=pl.CostEstimate(flops=10**9, bytes_accessed=3 * 10**6, transcendentals=0),
-    )(taps)
+        both_toeplitz_kernel,
+        grid=(2,),
+        out_shape=[
+            jax.ShapeDtypeStruct((g, 2 * levels, rows, depth), BF16)
+            for g, levels, rows, depth in shapes
+        ],
+        in_specs=[pl.BlockSpec(part.shape, lambda p: (0, 0, 0, 0)) for part in taps],
+        out_specs=[pl.BlockSpec(block, lambda p: (0, p, 0, 0)) for block in shapes],
+        scratch_shapes=[pltpu.VMEM((TAPS, LANES, LANES), F32)] * 2,
+        name="matrix",
+        compiler_params=PARAMS,
+        cost_estimate=pl.CostEstimate(flops=2 * 10**9, bytes_accessed=6 * 10**6, transcendentals=0),
+    )(*taps)
 
 
 def pairs_of(count, first):
@@ -487,10 +521,13 @@
     )
     got = lax.ppermute(packed, "comp", ring(2, 1))
     o_tiles = 2 * o_levels * 3
+    outward, _ = lax.optimization_barrier((outward, packed))
     swapped = lax.ppermute(outward.reshape(o_tiles, o_ch, LANES), ("comp", "lon"), swaps)
+    o_matrix, a_matrix = toeplitz(ocean_kernel, air_kernel, o_levels, a_levels)
+    o_matrix, a_matrix, got, swapped = lax.optimization_barrier((o_matrix, a_matrix, got, swapped))
     rim = (o_tiles * o_ch + (2 * a_levels * 3 + 1) * a_ch, LANES)
     surface = pltpu.VMEM((4 * band, LANES), F32)
-    weights = (flux_weight.T, temp_weight[:, None])
+    weights = (flux_weight, temp_weight.reshape(1, a_ch))
     even_out, odd_out, edge = call(
         force_halo_kernel,
         (shape(rim, BF16), shape(rim, BF16), shape((a_ch, LANES), F32)),
@@ -509,28 +546,30 @@
         ocean_mask, surface_temp, air_fluxes, got, ocean_grid, air_grid, *weights,
     )
 
-    o_taps, a_taps, o_gain, a_gain, o_up, a_up, o_down, a_down = lax.optimization_barrier(
-        (
-            taps_of(ocean_kernel), taps_of(air_kernel), ocean_gain[:, None], air_gain[:, None],
-            ocean_up.T, air_up.T, ocean_down.T, air_down.T,
-        )
-    )
-    o_matrix = toeplitz(o_taps, o_levels, "matrix_ocean")
-    a_matrix = toeplitz(a_taps, a_levels, "matrix_air")
     a_conv = convolution(conv_air_kernel, "conv_air", air_forced, even, odd, edge, a_matrix)
     a_other = lax.ppermute(a_conv, "ch", ring(2, 1))
     o_conv = convolution(conv_ocean_kernel, "conv_ocean", ocean_forced, even, odd, None, o_matrix)
     o_other = lax.ppermute(o_conv, "ch", ring(2, 1))
 
+    a_hid, o_hid = air_up.shape[1], ocean_up.shape[1]
     a_next = call(
         functools.partial(mlp_kernel, False), shape(a_grid, BF16),
-        [pltpu.VMEM((2, 2 * a_ch, 2 * LANES), F32)], "mlp_air", 10**9, 3 * 10**6,
-        a_conv, a_other, a_gain, a_up, a_down, air_top, air_forced,
+        [
+            pltpu.VMEM((2, 2 * a_ch, 2 * LANES), F32), pltpu.VMEM((a_hid, 2 * a_ch), BF16),
+            pltpu.VMEM((2 * a_ch, a_hid), BF16),
+        ],
+        "mlp_air", 10**9, 3 * 10**6,
+        a_conv, a_other, air_gain.reshape(1, -1), air_up, air_down.T, air_top, air_forced,
     )
     o_next = call(
         functools.partial(mlp_kernel, True), shape(o_grid, BF16),
-        [pltpu.VMEM((2, 2 * o_ch, 2 * LANES), F32)], "mlp_ocean", 10**9, 3 * 10**6,
-        o_conv, o_other, o_gain, o_up, o_down, ocean_top, ocean_forced, ocean_mask,
+        [
+            pltpu.VMEM((2, 2 * o_ch, 2 * LANES), F32), pltpu.VMEM((o_hid, 2 * o_ch), BF16),
+            pltpu.VMEM((2 * o_ch, o_hid), BF16),
+        ],
+        "mlp_ocean", 10**9, 3 * 10**6,
+        o_conv, o_other, ocean_gain.reshape(1, -1), ocean_up, ocean_down, ocean_top, ocean_forced,
+        ocean_mask,
     )
     ocean_next = jnp.transpose(o_next, (1, 3, 2, 0, 4)).reshape(ocean_state.shape)
     air_next = jnp.transpose(a_next, (1, 3, 2, 0, 4))

time: 81.4 us -> 58.8 us (0.72)
  Pallas kernels: 41.4 us -> 19.6 us
  local copies, waits for them, and re-layouts: 19.2 us -> 7.3 us
  waiting for transfers between devices: 5.77 us -> 15.2 us
  starting transfers between devices: 13.5 us -> 15 us
    pallas_call x5, Pallas kernels: 20.8 us -> 10.5 us  [call(): pl.pallas_call(kernel, out_shape=out_shape, in_specs=[VMEM] * len(args),...]
    ppermute x1, waiting for transfers between devices: 0.01 us -> 7.53 us  [per_device(): odd = lax.ppermute(odd_out, 'lon', pairs_of(lons, 1))]
    unnamed x38 -> x36, local copies, waits for them, and re-layouts: 12.8 us -> 5.76 us
    pallas_call x2, Pallas kernels: 12.5 us -> 6.69 us  [convolution(): pl.pallas_call(kernel, grid=(channels // count,), out_shape=jax.ShapeDtyp...]
    pallas_call x2 -> x1, Pallas kernels: 8.11 us -> 2.35 us  [toeplitz(): pl.pallas_call(both_toeplitz_kernel, grid=(2,), out_shape=[jax.ShapeDtype...]
    ppermute x1, waiting for transfers between devices: 0.01 us -> 4.82 us  [per_device(): o_other = lax.ppermute(o_conv, 'ch', ring(2, 1))]
    optimization_barrier x4 -> x1, local copies, waits for them, and re-layouts: 3.25 us -> 0.05 us  [per_device(): outward, _ = lax.optimization_barrier((outward, packed))]
    ppermute x1, waiting for transfers between devices: 3.19 us -> 0.01 us  [per_device(): a_other = lax.ppermute(a_conv, 'ch', ring(2, 1))]
  transfers between devices with their start and end apart: 6 -> 6, of which waited for: 2 -> 3; matrix products, arithmetic and copies ran while one was open for 15% -> 3% of each run, Pallas kernels for 30% -> 21%
where the time goes in v4:
time: 58.8 us; the launch traced here: 58 us
  Pallas kernels  19.6 us (33%)
  waiting for transfers between devices  15.2 us (26%)
  starting transfers between devices  15 us (26%)
  local copies, waits for them, and re-layouts  7.3 us (12%)
  between operations  0.89 us (2%)
    pallas_call x5, Pallas kernels, call(): pl.pallas_call(kernel, out_shape=out_shape, in_specs=[VMEM] * len(args),...  10.5 us
    ppermute x1, waiting for transfers between devices, per_device(): odd = lax.ppermute(odd_out, 'lon', pairs_of(lons, 1))  7.53 us
    ppermute x1, starting transfers between devices, per_device(): odd = lax.ppermute(odd_out, 'lon', pairs_of(lons, 1))  7.21 us
    pallas_call x2, Pallas kernels, convolution(): pl.pallas_call(kernel, grid=(channels // count,), out_shape=jax.ShapeDtyp...  6.69 us
    unnamed x36, local copies, waits for them, and re-layouts  5.76 us
    ppermute x1, waiting for transfers between devices, per_device(): o_other = lax.ppermute(o_conv, 'ch', ring(2, 1))  4.82 us
    ppermute x1, starting transfers between devices, per_device(): lax.ppermute(outward.reshape(o_tiles, o_ch, LANES), ('comp', 'lon'), swaps)  4.2 us
    ppermute x1, waiting for transfers between devices, per_device(): got = lax.ppermute(packed, 'comp', ring(2, 1))  2.88 us
  transfers between devices with their start and end apart: 6, of which 3 were waited for; matrix products, arithmetic and copies ran while one was open for 3% of the time, Pallas kernels for 21%

profile of v4, /device:TPU:8, one launch (start us, length us, event | category | flops | bytes accessed | tf_op | source)
XLA Modules:
  0.0 58.0 jit_solution(12779203462513091666)
XLA Ops:
  0.7 1.2 %reshape.28 = bf16[3,64,4,2,128]{4,3,2,1,0:T(2,128)(2,1)S(1)} reshape(bf16[3,64,4,256]{3,2,1,0:T(4,128)(2,1)} %param.15) | data formatting | bytes 786432 | tf_op jit(solution)/shard_map/reshape | solution.py:506
  1.8 1.1 %copy.35 = bf16[2,96,4,2,128]{4,1,2,0,3:T(8,128)(2,1)S(1)} copy(bf16[2,96,4,2,128]{4,3,2,1,0:T(2,128)(2,1)} %param.17) | data formatting | bytes 786432 | tf_op args[2]
  2.9 0.2 copy_bitcast_fusion.2
  3.1 0.7 %copy-done = f32[4,4,2,128]{3,2,1,0:T(2,128)S(1)} copy-done((f32[4,4,2,128]{3,2,1,0:T(2,128)S(1)}, f32[4,4,2,128]{3,2,1,0:T(2,128)}, u32[]{:S(2)}) %copy-start) | copy-done | bytes 16408
  3.9 0.7 %copy-done.2 = f32[4,256]{1,0:T(4,128)S(1)} copy-done((f32[4,256]{1,0:T(4,128)S(1)}, f32[4,256]{1,0:T(4,128)}, u32[]{:S(2)}) %copy-start.2) | copy-done | bytes 4120
  4.5 0.7 %copy-done.4 = s32[4,256]{1,0:T(4,128)S(1)} copy-done((s32[4,256]{1,0:T(4,128)S(1)}, s32[4,256]{1,0:T(4,128)}, u32[]{:S(2)}) %copy-start.4) | copy-done | bytes 4120
  5.5 4.2 %collective-permute-start.1 = (bf16[18,64,128]{2,1,0:T(8,128)(2,1)S(1)}, bf16[18,64,128]{2,1,0:T(8,128)(2,1)S(1)}, u32[]{:S(2)}, u32[]{:S(2)}) collective-permute-start(bf16[18,64,128]{2,1,0:T(8,128)(2,1)S(1)} %bitcast.31), channel_id=1, source_target_pairs={{0,128},{126,254},{128,0},{254,126},{1,129},{127,255},{129,1},{255... | collective-permute-start | bytes 884744 | tf_op jit(solution)/shard_map/ppermute | solution.py:525
  9.7 1.3 %collective-permute-start = (f32[144,128]{1,0:T(8,128)S(1)}, f32[144,128]{1,0:T(8,128)S(1)}, u32[]{:S(2)}, u32[]{:S(2)}) collective-permute-start(f32[144,128]{1,0:T(8,128)S(1)} %pack.1), channel_id=1, source_target_pairs={{0,128},{128,0},{1,129},{129,1},{2,130},{130,2},{3,131},{131,3},{4... | collective-permute-start | bytes 221192 | tf_op jit(solution)/shard_map/ppermute | solution.py:522
  11.1 2.4 %matrix.1 = (bf16[8,6,112,256]{3,2,1,0:T(8,128)(2,1)S(1)}, bf16[12,4,112,256]{3,2,1,0:T(8,128)(2,1)S(1)}) custom-call(f32[3,7,7,64]{3,2,1,0:T(8,128)S(1)} %bitcast.27, f32[3,7,7,96]{3,2,1,0:T(8,128)S(1)} %bitcast.28), custom_call_target="tpu_custom_call" | custom-call | flops 2000000000 | bytes 6000000 | tf_op jit(solution)/shard_map/matrix/pallas_call | solution.py:469
  13.5 2.9 %collective-permute-done.got_ref = f32[144,128]{1,0:T(8,128)S(1)} collective-permute-done((f32[144,128]{1,0:T(8,128)S(1)}, f32[144,128]{1,0:T(8,128)S(1)}, u32[]{:S(2)}, u32[]{:S(2)}) %collective-permute-start) | collective-permute-done | bytes 73760 | tf_op jit(solution)/shard_map/ppermute | solution.py:522
  16.4 0.4 force_halo.1
  16.9 7.2 %collective-permute-start.3 = (bf16[2400,128]{1,0:T(8,128)(2,1)S(1)}, bf16[2400,128]{1,0:T(8,128)(2,1)S(1)}, u32[]{:S(2)}, u32[]{:S(2)}) collective-permute-start(bf16[2400,128]{1,0:T(8,128)(2,1)S(1)} %get-tuple-element.23), channel_id=1, source_target_pairs={{2,4},{4,2},{6,8},{8,6},{10,12},{12,10},{14,16},{16,14},{18,20},{2... | collective-permute-start | bytes 1843208 | tf_op jit(solution)/shard_map/ppermute | solution.py:538
  24.2 0.3 force_own.1
  24.5 7.5 %collective-permute-done.3.odd_ref = bf16[2400,128]{1,0:T(8,128)(2,1)S(1)} collective-permute-done((bf16[2400,128]{1,0:T(8,128)(2,1)S(1)}, bf16[2400,128]{1,0:T(8,128)(2,1)S(1)}, u32[]{:S(2)}, u32[]{:S(2)}) %collective-permute-start.3) | collective-permute-done | bytes 614432 | tf_op jit(solution)/shard_map/ppermute | solution.py:538
  32.0 2.4 %conv_ocean.1.refs_0_ = bf16[2,3,4,64,128]{4,3,2,1,0:T(8,128)(2,1)S(1)} custom-call(bf16[2,3,4,64,128]{4,3,2,1,0:T(8,128)(2,1)S(1)} %get-tuple-element.20.own_ref.refs_6_, bf16[2400,128]{1,0:T(8,128)(2,1)S(1)} %collective-permute-done.2.even_ref, bf16[2400,128]{1,0:T(8,128)(2,1)S(1)} %collective-permute-done.3.odd_ref, ...), custom_call_target="tpu_custom_call" | custom-call | flops 2000000000 | bytes 4000000 | tf_op jit(solution)/shard_map/conv_ocean/pallas_call | solution.py:395
  34.4 0.5 collective-permute-start.4
  34.9 4.3 %conv_air.1.refs_0_ = bf16[2,2,4,96,128]{4,3,2,1,0:T(8,128)(2,1)S(1)} custom-call(bf16[2,2,4,96,128]{4,3,2,1,0:T(8,128)(2,1)S(1)} %get-tuple-element.26.own_ref.refs_6_, bf16[2400,128]{1,0:T(8,128)(2,1)S(1)} %collective-permute-done.2.even_ref, bf16[2400,128]{1,0:T(8,128)(2,1)S(1)} %collective-permute-done.3.odd_ref, ...), custom_call_target="tpu_custom_call" | custom-call | flops 2000000000 | bytes 4000000 | tf_op jit(solution)/shard_map/conv_air/pallas_call | solution.py:395
  39.3 1.7 %collective-permute-start.5 = (bf16[2,2,4,96,128]{4,3,2,1,0:T(8,128)(2,1)S(1)}, bf16[2,2,4,96,128]{4,3,2,1,0:T(8,128)(2,1)S(1)}, u32[]{:S(2)}, u32[]{:S(2)}) collective-permute-start(bf16[2,2,4,96,128]{4,3,2,1,0:T(8,128)(2,1)S(1)} %conv_air.1.refs_0_), channel_id=1, source_target_pairs={{0,1},{1,0},{2,3},{3,2},{4,5},{5,4},{6,7},{7,6},{8,9},{9,8},{10,11... | collective-permute-start | bytes 1179656 | tf_op jit(solution)/shard_map/ppermute | solution.py:550
  40.9 4.8 %collective-permute-done.4.refs_1_ = bf16[2,3,4,64,128]{4,3,2,1,0:T(8,128)(2,1)S(1)} collective-permute-done((bf16[2,3,4,64,128]{4,3,2,1,0:T(8,128)(2,1)S(1)}, bf16[2,3,4,64,128]{4,3,2,1,0:T(8,128)(2,1)S(1)}, u32[]{:S(2)}, u32[]{:S(2)}) %collective-permute-start.4) | collective-permute-done | bytes 393248 | tf_op jit(solution)/shard_map/ppermute | solution.py:552
  45.8 5.3 %mlp_ocean.1 = bf16[2,3,4,64,128]{4,3,2,1,0:T(8,128)(2,1)S(1)} custom-call(bf16[2,3,4,64,128]{4,3,2,1,0:T(8,128)(2,1)S(1)} %conv_ocean.1.refs_0_, bf16[2,3,4,64,128]{4,3,2,1,0:T(8,128)(2,1)S(1)} %collective-permute-done.4.refs_1_, f32[1,128]{1,0:T(1,128)S(1)} %bitcast.30, bf16[128,512]{1,0:T(8,128)(2,1)S(1)} %copy-done.10, bf16[512,128]{1,0:T(8,128)(2,1)S(1)} %copy-done.11, ...), custom_call_target="tpu_custom_call" | custom-call | flops 1000000000 | bytes 3000000 | tf_op jit(solution)/shard_map/mlp_ocean/pallas_call | solution.py:28
  51.0 0.4 copy.28
  51.5 1.0 %reshape.29 = bf16[3,64,4,256]{3,2,1,0:T(4,128)(2,1)} reshape(bf16[3,64,4,2,128]{4,3,2,1,0:T(2,128)(2,1)S(1)} %copy.28) | data formatting | bytes 786432
  52.5 4.4 %mlp_air.1 = bf16[2,2,4,96,128]{4,3,2,1,0:T(8,128)(2,1)S(1)} custom-call(bf16[2,2,4,96,128]{4,3,2,1,0:T(8,128)(2,1)S(1)} %conv_air.1.refs_0_, bf16[2,2,4,96,128]{4,3,2,1,0:T(8,128)(2,1)S(1)} %collective-permute-done.5.refs_1_, f32[1,192]{1,0:T(1,128)S(1)} %bitcast.29, bf16[192,768]{1,0:T(8,128)(2,1)S(1)} %copy-done.8, bf16[192,768]{1,0:T(8,128)(2,1)S(1)} %bitcast.26, ...), custom_call_target="tpu_custom_call" | custom-call | flops 1000000000 | bytes 3000000 | tf_op jit(solution)/shard_map/mlp_air/pallas_call | solution.py:28
  56.9 1.2 %copy.25 = bf16[2,96,4,2,128]{4,3,2,1,0:T(2,128)(2,1)} copy(bf16[2,96,4,2,128]{4,1,2,0,3:T(8,128)(2,1)S(1)} %bitcast.23) | data formatting | bytes 786432
  (36 shorter events, 0.5 us)
Async XLA Ops:
  0.6 10.4 %copy-start.13 = (f32[96,3,7,7]{0,3,2,1:T(8,128)S(1)}, f32[96,3,7,7]{0,3,2,1:T(8,128)}, u32[]{:S(2)}) copy-start(f32[96,3,7,7]{0,3,2,1:T(8,128)} %param.24) | copy-start | bytes 169348
  0.6 10.4 %copy-start.12 = (f32[64,3,7,7]{0,3,2,1:T(8,128)S(1)}, f32[64,3,7,7]{0,3,2,1:T(8,128)}, u32[]{:S(2)}) copy-start(f32[64,3,7,7]{0,3,2,1:T(8,128)} %param.20) | copy-start | bytes 112900
  3.1 0.7 %copy-start = (f32[4,4,2,128]{3,2,1,0:T(2,128)S(1)}, f32[4,4,2,128]{3,2,1,0:T(2,128)}, u32[]{:S(2)}) copy-start(f32[4,4,2,128]{3,2,1,0:T(2,128)} %flux_ref.5) | copy-start | bytes 49156
  3.9 0.7 %copy-start.2 = (f32[4,256]{1,0:T(4,128)S(1)}, f32[4,256]{1,0:T(4,128)}, u32[]{:S(2)}) copy-start(f32[4,256]{1,0:T(4,128)} %temp_ref.5) | copy-start | bytes 12292
  4.5 0.7 %copy-start.4 = (s32[4,256]{1,0:T(4,128)S(1)}, s32[4,256]{1,0:T(4,128)}, u32[]{:S(2)}) copy-start(s32[4,256]{1,0:T(4,128)} %refs_7_.1) | copy-start | bytes 12292
  5.5 10.9 %collective-permute-start.1 = (bf16[18,64,128]{2,1,0:T(8,128)(2,1)S(1)}, bf16[18,64,128]{2,1,0:T(8,128)(2,1)S(1)}, u32[]{:S(2)}, u32[]{:S(2)}) collective-permute-start(bf16[18,64,128]{2,1,0:T(8,128)(2,1)S(1)} %bitcast.31), channel_id=1, source_target_pairs={{0,128},{126,254},{128,0},{254,126},{1,129},{127,255},{129,1},{255... | collective-permute-start | bytes 884744 | tf_op jit(solution)/shard_map/ppermute | solution.py:525
  9.7 6.7 %collective-permute-start = (f32[144,128]{1,0:T(8,128)S(1)}, f32[144,128]{1,0:T(8,128)S(1)}, u32[]{:S(2)}, u32[]{:S(2)}) collective-permute-start(f32[144,128]{1,0:T(8,128)S(1)} %pack.1), channel_id=1, source_target_pairs={{0,128},{128,0},{1,129},{129,1},{2,130},{130,2},{3,131},{131,3},{4... | collective-permute-start | bytes 221192 | tf_op jit(solution)/shard_map/ppermute | solution.py:522
  11.0 5.4 %copy-start.1 = (f32[4,4,2,128]{3,2,1,0:T(2,128)S(1)}, f32[4,4,2,128]{3,2,1,0:T(2,128)}, u32[]{:S(2)}) copy-start(f32[4,4,2,128]{3,2,1,0:T(2,128)} %flux_ref.5) | copy-start | bytes 49156
  11.0 5.4 %copy-start.3 = (f32[4,256]{1,0:T(4,128)S(1)}, f32[4,256]{1,0:T(4,128)}, u32[]{:S(2)}) copy-start(f32[4,256]{1,0:T(4,128)} %temp_ref.5) | copy-start | bytes 12292
  11.0 5.4 %copy-start.5 = (s32[4,256]{1,0:T(4,128)S(1)}, s32[4,256]{1,0:T(4,128)}, u32[]{:S(2)}) copy-start(s32[4,256]{1,0:T(4,128)} %refs_7_.1) | copy-start | bytes 12292
  11.0 5.4 %copy-start.6 = (f32[4,64]{1,0:T(4,128)S(1)}, f32[4,64]{1,0:T(4,128)}, u32[]{:S(2)}) copy-start(f32[4,64]{1,0:T(4,128)} %fw_ref.3) | copy-start | bytes 3076
  11.0 5.4 %copy-start.7 = (f32[96]{0:T(128)S(1)}, f32[96]{0:T(128)}, u32[]{:S(2)}) copy-start(f32[96]{0:T(128)} %param.29) | copy-start | bytes 1156
  16.8 7.6 %collective-permute-start.2 = (bf16[2400,128]{1,0:T(8,128)(2,1)S(1)}, bf16[2400,128]{1,0:T(8,128)(2,1)S(1)}, u32[]{:S(2)}, u32[]{:S(2)}) collective-permute-start(bf16[2400,128]{1,0:T(8,128)(2,1)S(1)} %get-tuple-element.22), channel_id=1, source_target_pairs={{0,2},{2,0},{4,6},{6,4},{8,10},{10,8},{12,14},{14,12},{16,18},{18,... | collective-permute-start | bytes 1843208 | tf_op jit(solution)/shard_map/ppermute | solution.py:537
  16.9 15.0 %collective-permute-start.3 = (bf16[2400,128]{1,0:T(8,128)(2,1)S(1)}, bf16[2400,128]{1,0:T(8,128)(2,1)S(1)}, u32[]{:S(2)}, u32[]{:S(2)}) collective-permute-start(bf16[2400,128]{1,0:T(8,128)(2,1)S(1)} %get-tuple-element.23), channel_id=1, source_target_pairs={{2,4},{4,2},{6,8},{8,6},{10,12},{12,10},{14,16},{16,14},{18,20},{2... | collective-permute-start | bytes 1843208 | tf_op jit(solution)/shard_map/ppermute | solution.py:538
  34.4 11.4 %collective-permute-start.4 = (bf16[2,3,4,64,128]{4,3,2,1,0:T(8,128)(2,1)S(1)}, bf16[2,3,4,64,128]{4,3,2,1,0:T(8,128)(2,1)S(1)}, u32[]{:S(2)}, u32[]{:S(2)}) collective-permute-start(bf16[2,3,4,64,128]{4,3,2,1,0:T(8,128)(2,1)S(1)} %conv_ocean.1.refs_0_), channel_id=1, source_target_pairs={{0,1},{1,0},{2,3},{3,2},{4,5},{5,4},{6,7},{7,6},{8,9},{9,8},{10,11... | collective-permute-start | bytes 1179656 | tf_op jit(solution)/shard_map/ppermute | solution.py:552
  34.9 10.9 %copy-start.10 = (bf16[128,512]{1,0:T(8,128)(2,1)S(1)}, bf16[128,512]{1,0:T(8,128)(2,1)}, u32[]{:S(2)}) copy-start(bf16[128,512]{1,0:T(8,128)(2,1)} %refs_3_.2) | copy-start | bytes 393220
  34.9 10.9 %copy-start.11 = (bf16[512,128]{1,0:T(8,128)(2,1)S(1)}, bf16[512,128]{1,0:T(8,128)(2,1)}, u32[]{:S(2)}) copy-start(bf16[512,128]{1,0:T(8,128)(2,1)} %refs_4_.1) | copy-start | bytes 393220
  34.9 10.9 %copy-start.15 = (f32[128]{0:T(128)S(1)}, f32[128]{0:T(128)}, u32[]{:S(2)}) copy-start(f32[128]{0:T(128)} %param.21) | copy-start | bytes 1540
  39.2 13.2 %copy-start.8 = (bf16[192,768]{1,0:T(8,128)(2,1)S(1)}, bf16[192,768]{1,0:T(8,128)(2,1)}, u32[]{:S(2)}) copy-start(bf16[192,768]{1,0:T(8,128)(2,1)} %refs_3_.3) | copy-start | bytes 884740
  39.2 13.2 %copy-start.9 = (bf16[768,192]{0,1:T(8,128)(2,1)S(1)}, bf16[768,192]{0,1:T(8,128)(2,1)}, u32[]{:S(2)}) copy-start(bf16[768,192]{0,1:T(8,128)(2,1)} %param.27) | copy-start | bytes 884740
  39.2 13.2 %copy-start.14 = (f32[192]{0:T(256)S(1)}, f32[192]{0:T(256)}, u32[]{:S(2)}) copy-start(f32[192]{0:T(256)} %param.25) | copy-start | bytes 2308
  39.3 13.2 %collective-permute-start.5 = (bf16[2,2,4,96,128]{4,3,2,1,0:T(8,128)(2,1)S(1)}, bf16[2,2,4,96,128]{4,3,2,1,0:T(8,128)(2,1)S(1)}, u32[]{:S(2)}, u32[]{:S(2)}) collective-permute-start(bf16[2,2,4,96,128]{4,3,2,1,0:T(8,128)(2,1)S(1)} %conv_air.1.refs_0_), channel_id=1, source_target_pairs={{0,1},{1,0},{2,3},{3,2},{4,5},{5,4},{6,7},{7,6},{8,9},{9,8},{10,11... | collective-permute-start | bytes 1179656 | tf_op jit(solution)/shard_map/ppermute | solution.py:550

commit v5 on v4

--- a/solution.py
+++ b/solution.py
@@ -38,24 +38,21 @@
 
 
 def rows_of(fields, band):
-    temp = fields * band * 2
-    return temp, temp + 2 * band, temp + 4 * band
-
-
-def pack_kernel(mask_ref, temp_ref, flux_ref, air_ref, out_ref):
+    temp = fields * band
+    return temp, temp + 2 * band
+
+
+def pack_kernel(mask_hbm, temp_hbm, flux_hbm, air_ref, out_ref, mask_ref, temp_ref, flux_ref, sems):
+    copies = [
+        pltpu.make_async_copy(mask_hbm, mask_ref, sems.at[0]),
+        pltpu.make_async_copy(temp_hbm, temp_ref, sems.at[1]),
+        pltpu.make_async_copy(flux_hbm, flux_ref, sems.at[2]),
+    ]
+    for copy in copies:
+        copy.start()
     comp = lax.axis_index("comp")
     fields, band = flux_ref.shape[:2]
-    temp_row, sea_row, edge_row = rows_of(fields, band)
-    for k in range(fields):
-        for j in range(band):
-            at = (k * band + j) * 2
-            out_ref[at : at + 2, :] = flux_ref[k, j]
-    sea = mask_ref[...].astype(F32)
-    temp = temp_ref[...] * sea
-    for s in range(2):
-        lanes = slice(s * LANES, (s + 1) * LANES)
-        out_ref[temp_row + s * band : temp_row + (s + 1) * band, :] = temp[:, lanes]
-        out_ref[sea_row + s * band : sea_row + (s + 1) * band, :] = sea[:, lanes]
+    temp_row, edge_row = rows_of(fields, band)
     levels, channels = air_ref.shape[1], air_ref.shape[3]
     start = jnp.where(comp == 0, LANES - 8, 0)
     lane = lane_ids(channels)
@@ -69,6 +66,16 @@
                 )
                 packed = jnp.where((lane >> 3) == idx, rolled, packed)
     out_ref[edge_row : edge_row + channels, :] = packed
+    for copy in copies:
+        copy.wait()
+    for k in range(fields):
+        for j in range(band):
+            at = k * band + j
+            out_ref[at : at + 1, :] = flux_ref[k, j, pl.ds(1 - comp, 1), :]
+    temp = temp_ref[...] * mask_ref[...].astype(F32)
+    for s in range(2):
+        lanes = slice(s * LANES, (s + 1) * LANES)
+        out_ref[temp_row + s * band : temp_row + (s + 1) * band, :] = temp[:, lanes]
 
 
 def fill_surface(mask_ref, temp_ref, surface_ref):
@@ -81,13 +88,13 @@
         surface_ref[(2 + s) * band : (3 + s) * band, :] = sea[:, lanes]
 
 
-def inject_of(flux_ref, got_ref, fw, half, s, i):
+def inject_of(flux_ref, got_ref, fw, s, i):
     comp = lax.axis_index("comp")
     fields, band = flux_ref.shape[:2]
     total = None
     for k in range(fields):
-        mine = flux_ref[k, i, pl.ds(half, 1), :]
-        theirs = got_ref[pl.ds((k * band + i) * 2 + half, 1), :]
+        mine = flux_ref[k, i, pl.ds(comp, 1), :]
+        theirs = got_ref[pl.ds(k * band + i, 1), :]
         term = fw[k] * jnp.where(comp == s, mine, theirs)
         total = term if total is None else total + term
     return total
@@ -102,17 +109,15 @@
 
 
 def force_halo_kernel(
-    mask_ref, temp_ref, flux_ref, got_ref, ocean_ref, swapped_ref, air_ref, fw_ref, tw_ref,
-    even_ref, odd_ref, edge_ref, surface_ref,
+    mask_ref, temp_ref, flux_ref, got_ref, ocean_ref, air_ref, fw_ref, tw_ref,
+    even_ref, odd_ocean_ref, odd_air_ref, edge_ref, surface_ref,
 ):
     comp = lax.axis_index("comp")
-    lon = lax.axis_index("lon")
-    parity = (lon & 1)
-    at_end = (lon == 0) | (lon == lax.axis_size("lon") - 1)
+    parity = lax.axis_index("lon") & 1
     fields, band = flux_ref.shape[:2]
     o_levels, o_ch = ocean_ref.shape[1], ocean_ref.shape[3]
     a_levels, a_ch = air_ref.shape[1], air_ref.shape[3]
-    temp_row, sea_row, edge_row = rows_of(fields, band)
+    edge_row = rows_of(fields, band)[1]
     fill_surface(mask_ref, temp_ref, surface_ref)
     heat = column(tw_ref[...])
     fw = [column(fw_ref[k : k + 1, :]) for k in range(fields)]
@@ -132,33 +137,30 @@
     edge_ref[...] = edge
 
     first_air = 2 * o_levels * 3 * o_ch
-    for out_ref, offset, outer in ((even_ref, 1 - parity, None), (odd_ref, parity, at_end)):
+    for ocean_out, air_out, base, offset in (
+        (even_ref, even_ref, first_air, 1 - parity), (odd_ocean_ref, odd_air_ref, 0, parity)
+    ):
         for j in range(3):
             col = j + offset
-            half = comp if outer is None else jnp.where(outer, 1 - comp, comp)
             for s in range(2):
-                inject = inject_of(flux_ref, got_ref, fw, half, s, col)
+                inject = inject_of(flux_ref, got_ref, fw, s, col)
                 sea = surface_ref[pl.ds((2 + s) * band + col, 1), :]
-                if outer is not None:
-                    sea = jnp.where(outer, got_ref[pl.ds(sea_row + s * band + col, 1), :], sea)
                 for level in range(o_levels):
                     tile = (s * o_levels + level) * 3 + j
                     value = ocean_ref[s, level, col].astype(F32)
-                    if outer is not None:
-                        value = jnp.where(outer, swapped_ref[tile].astype(F32), value)
                     if level == 0:
                         value = value + inject
-                    out_ref[tile * o_ch : (tile + 1) * o_ch, :] = (value * sea).astype(BF16)
+                    ocean_out[tile * o_ch : (tile + 1) * o_ch, :] = (value * sea).astype(BF16)
             for h in range(2):
                 row = temp_of(surface_ref, got_ref, fields, band, h, comp, col)
                 for level in range(a_levels):
                     value = air_ref[h, level, col].astype(F32)
                     if level == 0:
                         value = value + heat * row
-                    at = first_air + ((h * a_levels + level) * 3 + j) * a_ch
-                    out_ref[at : at + a_ch, :] = value.astype(BF16)
-        at = first_air + 2 * a_levels * 3 * a_ch
-        out_ref[at : at + a_ch, :] = edge.astype(BF16)
+                    at = base + ((h * a_levels + level) * 3 + j) * a_ch
+                    air_out[at : at + a_ch, :] = value.astype(BF16)
+        at = base + 2 * a_levels * 3 * a_ch
+        air_out[at : at + a_ch, :] = edge.astype(BF16)
 
 
 def force_own_kernel(
@@ -173,7 +175,7 @@
     fw = [column(fw_ref[k : k + 1, :]) for k in range(fields)]
     for s in range(2):
         for i in range(band):
-            inject = inject_of(flux_ref, got_ref, fw, comp, s, i)
+            inject = inject_of(flux_ref, got_ref, fw, s, i)
             at = (2 + s) * band + i
             sea = surface_ref[at : at + 1, :]
             row = temp_of(surface_ref, got_ref, fields, band, s, comp, i)
@@ -191,13 +193,6 @@
                     value = value + heat * row
                     fa_ref[s, i] = value
                 ab_ref[s, level, i] = value.astype(BF16)
-
-
-def unpack_edge(packed, idx, shift, lane):
-    comp = lax.axis_index("comp")
-    start = (jnp.where(comp == 0, 0, LANES - 8) + shift) & (LANES - 1)
-    rolled = pltpu.roll(packed, (start - 8 * idx + 2 * LANES) & (LANES - 1), 1)
-    return jnp.where((lane >> 3) == (start >> 3), rolled, 0.0)
 
 
 TAPS = 7
@@ -247,9 +242,10 @@
     toeplitz_kernel(o_ref, o_out, o_rows)
 
 
-def rim_tile(even_ref, odd_ref, at, count):
-    rows = pl.ds(pl.multiple_of(at, 16), count)
-    return even_ref[rows, :].astype(F32), odd_ref[rows, :].astype(F32)
+def rim_tile(even_ref, odd_ref, even_at, odd_at, count):
+    even = even_ref[pl.ds(pl.multiple_of(even_at, 16), count), :]
+    odd = odd_ref[pl.ds(pl.multiple_of(odd_at, 16), count), :]
+    return even.astype(F32), odd.astype(F32)
 
 
 def conv_ocean_kernel(own_ref, even_ref, odd_ref, matrix_ref, out_ref, product_ref):
@@ -266,7 +262,7 @@
             west, east = [], []
             for i in range(3):
                 at = ((s * levels + level) * 3 + i) * channels + first
-                even, odd = rim_tile(even_ref, odd_ref, at, count)
+                even, odd = rim_tile(even_ref, odd_ref, at, at, count)
                 west.append(jnp.where(inner, even, odd))
                 east.append(jnp.where(inner, odd, even))
             own = [own_ref[s, level, i].astype(F32) for i in range(band)]
@@ -310,7 +306,8 @@
                     out_ref[s, level, i, rows] = sums[s].astype(BF16)
 
 
-def conv_air_kernel(own_ref, even_ref, odd_ref, packed_ref, matrix_ref, out_ref, product_ref):
+def conv_air_kernel(own_ref, even_ref, odd_ref, packed_ref, matrix_ref, *refs):
+    out_refs, product_ref = refs[:-1], refs[-1]
     _, levels, band, count, _ = own_ref.shape
     depth = matrix_ref.shape[-1]
     lon = lax.axis_index("lon")
@@ -318,12 +315,33 @@
     swap_west = jnp.where(lon == 0, 1, 0)
     swap_east = jnp.where(lon == lax.axis_size("lon") - 1, 1, 0)
     channels = pl.num_programs(0) * count
-    first = pl.program_id(0) * count + even_ref.shape[0] - (2 * levels * 3 + 1) * channels
+    first_odd = pl.program_id(0) * count
+    first_even = first_odd + even_ref.shape[0] - odd_ref.shape[0]
+
+    def tiles_at(tile):
+        at = tile * channels
+        return rim_tile(even_ref, odd_ref, first_even + at, first_odd + at, count)
+
+    start = jnp.where(lax.axis_index("comp") == 0, 0, LANES - 8)
+    wide = lane_ids(count)
+    even, odd = tiles_at(2 * levels * 3)
+    edge_tiles = []
+    for tile, swap in (
+        (packed_ref[...], None),
+        (jnp.where(inner, even, odd), swap_west),
+        (jnp.where(inner, odd, even), swap_east),
+    ):
+        if swap is not None:
+            span = 8 * band
+            other = jnp.where(
+                (wide & span) == 0, pltpu.roll(tile, LANES - span, 1), pltpu.roll(tile, span, 1)
+            )
+            tile = jnp.where(swap == 1, other, tile)
+        edge_tiles.append(pltpu.roll(tile, start, 1))
     lane = lane_ids(8)
-    even, odd = rim_tile(even_ref, odd_ref, first + 2 * levels * 3 * channels, count)
-    edge_tiles = [packed_ref[...], jnp.where(inner, even, odd), jnp.where(inner, odd, even)]
+    block = ((lane - start + LANES) & (LANES - 1)) >> 3
+    adjoining = (block == 0) | (block == band)
     all_tiles = []
-    beyond = []
     for h in range(2):
         west_h = jnp.abs(h - swap_west)
         east_h = jnp.abs(h - swap_east)
@@ -331,26 +349,28 @@
         for level in range(levels):
             west, east = [], []
             for i in range(3):
-                at = first + ((west_h * levels + level) * 3 + i) * channels
-                even, odd = rim_tile(even_ref, odd_ref, at, count)
+                even, odd = tiles_at((west_h * levels + level) * 3 + i)
                 west.append(jnp.where(inner, even, odd))
-                at = first + ((east_h * levels + level) * 3 + i) * channels
-                even, odd = rim_tile(even_ref, odd_ref, at, count)
+                even, odd = tiles_at((east_h * levels + level) * 3 + i)
                 east.append(jnp.where(inner, odd, even))
             tiles += west + [own_ref[h, level, i].astype(F32) for i in range(band)] + east
-            beyond += [(h, 1, (level * 2 + west_h) * band + i + band - 3) for i in range(3)]
-            beyond += [(h, 0, (level * 2 + h) * band + i) for i in range(band)]
-            beyond += [(h, 2, (level * 2 + east_h) * band + i) for i in range(3)]
         all_tiles.append(tiles)
+    beyond = []
+    for level in range(levels):
+        first = level * 2 * band
+        beyond += [(1, first + i + band - 3) for i in range(3)]
+        beyond += [(0, first + i) for i in range(band)]
+        beyond += [(2, first + i) for i in range(3)]
     for sub in range(count // 8):
         rows = slice(sub * 8, sub * 8 + 8)
         columns = [[tile[rows] for tile in tiles] for tiles in all_tiles]
         packed = [tile[rows] for tile in edge_tiles]
-        edges = [
-            [unpack_edge(packed[who], idx, h * 64, lane) for at_h, who, idx in beyond if at_h == h]
-            for h in range(2)
-        ]
-        columns.append([one + two for one, two in zip(*edges)])
+        columns.append(
+            [
+                jnp.where(adjoining, pltpu.roll(packed[who], -8 * idx % LANES, 1), 0.0)
+                for who, idx in beyond
+            ]
+        )
         pad = depth - len(columns[0]) * 8
         if pad:
             columns = [tiles + [jnp.zeros((pad, LANES), F32)] for tiles in columns]
@@ -370,12 +390,12 @@
                     for h in range(2):
                         part = product_ref[at, h * LANES : (h + 1) * LANES]
                         if off:
-                            here = edge if h == 0 else pltpu.roll(edge, 64, 1)
+                            here = edge if h == 0 else pltpu.roll(edge, LANES - 8 * band, 1)
                             inside = lane < off if off > 0 else lane >= LANES + off
                             part = pltpu.roll(jnp.where(inside, here, part), (LANES - off) % LANES, 1)
                         sums[h] = part if sums[h] is None else sums[h] + part
                 for h in range(2):
-                    out_ref[h, level, i, rows] = sums[h].astype(BF16)
+                    out_refs[level][h, 0, i, rows] = sums[h].astype(BF16)
 
 
 def convolution(kernel, name, own, even, odd, packed, matrix):
@@ -384,9 +404,9 @@
     count = 16
     lane_tiles = 2 if packed is None else 3
     grid_spec = pl.BlockSpec((2, levels, band, count, LANES), lambda g: (0, 0, 0, g, 0))
-    rim_spec = pl.BlockSpec(even.shape, lambda g: (0, 0))
     args = [own, even, odd]
-    specs = [grid_spec, rim_spec, rim_spec]
+    specs = [grid_spec] + [pl.BlockSpec(rim.shape, lambda g: (0, 0)) for rim in (even, odd)]
+    outs = [levels] if packed is None else [1] * levels
     if packed is not None:
         args.append(packed)
         specs.append(pl.BlockSpec((count, LANES), lambda g: (g, 0)))
@@ -395,9 +415,11 @@
     return pl.pallas_call(
         kernel,
         grid=(channels // count,),
-        out_shape=jax.ShapeDtypeStruct(own.shape, BF16),
+        out_shape=[jax.ShapeDtypeStruct((2, part) + own.shape[2:], BF16) for part in outs],
         in_specs=specs,
-        out_specs=grid_spec,
+        out_specs=[
+            pl.BlockSpec((2, part, band, count, LANES), lambda g: (0, 0, 0, g, 0)) for part in outs
+        ],
         scratch_shapes=[pltpu.VMEM((pairs * rows, lane_tiles * LANES), F32)],
         name=name,
         compiler_params=PARAMS,
@@ -405,9 +427,9 @@
     )(*args)
 
 
-def mlp_kernel(masked, *refs):
+def mlp_kernel(masked, first_level, *refs):
     own_ref, other_ref, gain_ref, up_ref, down_ref, top_ref, forced_ref = refs[:7]
-    mask_ref = refs[7] if masked else None
+    extra_ref = refs[7] if len(refs) > 11 else None
     out_ref, values_ref, wide_ref, narrow_ref = refs[-4:]
     _, levels, band, channels, _ = own_ref.shape
     ch = lax.axis_index("ch")
@@ -420,6 +442,9 @@
     else:
         narrow_ref[: channels] = down_ref[mine, :]
     down_rows = mine if masked else slice(0, channels)
+
+    if not masked and extra_ref is not None:
+        out_ref[:, :first_level] = extra_ref[...]
 
     def row(at, slot):
         level = at // band
@@ -441,16 +466,19 @@
         update = jnp.dot(narrow_ref[down_rows, :], doubled, preferred_element_type=F32) * 0.5
         update = update.astype(BF16).astype(F32)
         if masked:
-            mask = mask_ref[...]
+            mask = extra_ref[...]
             picked = lax.broadcasted_iota(jnp.int32, mask.shape, 0) == i
             sea = jnp.sum(jnp.where(picked, mask.astype(F32), 0.0), axis=0, keepdims=True)
         for s in range(2):
             lanes = slice(s * LANES, (s + 1) * LANES)
-            forced = jnp.where(level == 0, top_ref[s, i], forced_ref[s, level, i].astype(F32))
+            if first_level:
+                forced = forced_ref[s, first_level + level, i].astype(F32)
+            else:
+                forced = jnp.where(level == 0, top_ref[s, i], forced_ref[s, level, i].astype(F32))
             result = forced + update[:, lanes]
             if masked:
                 result = result * sea[:, lanes]
-            out_ref[s, level, i] = result.astype(BF16)
+            out_ref[s, first_level + level, i] = result.astype(BF16)
 
     def step(at, carry):
         row(at * 2, 0)
@@ -502,40 +530,49 @@
     fields = air_fluxes.shape[0]
     shape = jax.ShapeDtypeStruct
 
-    ocean_grid = jnp.transpose(
-        ocean_state.reshape(o_levels, o_ch, band, 2, LANES), (3, 0, 2, 1, 4)
-    )
     air_grid = jnp.transpose(air_state, (3, 0, 2, 1, 4))
     o_grid = (2, o_levels, band, o_ch, LANES)
     a_grid = (2, a_levels, band, a_ch, LANES)
 
     lons = lax.axis_size("lon")
     bands = lax.axis_size("comp") * lons
-    lon = lax.axis_index("lon")
-    outward = lax.dynamic_slice_in_dim(ocean_grid, jnp.where(lon == 0, 0, band - 3), 3, 2)
-    swaps = [(i, (i + lons) % bands) for i in (0, lons - 1, lons, bands - 1)]
     rows = rows_of(fields, band)[-1] + a_ch
-    packed = call(
-        pack_kernel, shape((rows, LANES), F32), [], "pack", 10**5, 10**6,
-        ocean_mask, surface_temp, air_fluxes, air_grid,
+    hbm = pl.BlockSpec(memory_space=pltpu.HBM)
+    surface_args = (ocean_mask, surface_temp, air_fluxes)
+    packed = pl.pallas_call(
+        pack_kernel,
+        out_shape=shape((rows, LANES), F32),
+        in_specs=[hbm, hbm, hbm, VMEM],
+        out_specs=VMEM,
+        scratch_shapes=[pltpu.VMEM(arg.shape, arg.dtype) for arg in surface_args]
+        + [pltpu.SemaphoreType.DMA((3,))],
+        name="pack",
+        compiler_params=PARAMS,
+    )(*surface_args, air_grid)
+    got = lax.ppermute(packed, "comp", ring(2, 1))
+    later_ocean, _ = lax.optimization_barrier((ocean_state, packed))
+    ocean_grid = jnp.transpose(
+        later_ocean.reshape(o_levels, o_ch, band, 2, LANES), (3, 0, 2, 1, 4)
     )
-    got = lax.ppermute(packed, "comp", ring(2, 1))
-    o_tiles = 2 * o_levels * 3
-    outward, _ = lax.optimization_barrier((outward, packed))
-    swapped = lax.ppermute(outward.reshape(o_tiles, o_ch, LANES), ("comp", "lon"), swaps)
+    ocean_grid, ocean_kernel = lax.optimization_barrier((ocean_grid, ocean_kernel))
     o_matrix, a_matrix = toeplitz(ocean_kernel, air_kernel, o_levels, a_levels)
-    o_matrix, a_matrix, got, swapped = lax.optimization_barrier((o_matrix, a_matrix, got, swapped))
-    rim = (o_tiles * o_ch + (2 * a_levels * 3 + 1) * a_ch, LANES)
+    o_matrix, a_matrix, got = lax.optimization_barrier((o_matrix, a_matrix, got))
+    o_rows = 2 * o_levels * 3 * o_ch
+    a_rows = (2 * a_levels * 3 + 1) * a_ch
     surface = pltpu.VMEM((4 * band, LANES), F32)
     weights = (flux_weight, temp_weight.reshape(1, a_ch))
-    even_out, odd_out, edge = call(
+    even_out, odd_out_o, odd_out_a, edge = call(
         force_halo_kernel,
-        (shape(rim, BF16), shape(rim, BF16), shape((a_ch, LANES), F32)),
+        (
+            shape((o_rows + a_rows, LANES), BF16), shape((o_rows, LANES), BF16),
+            shape((a_rows, LANES), BF16), shape((a_ch, LANES), F32),
+        ),
         [surface], "force_halo", 10**6, 4 * 10**6,
-        ocean_mask, surface_temp, air_fluxes, got, ocean_grid, swapped, air_grid, *weights,
+        *surface_args, got, ocean_grid, air_grid, *weights,
     )
     even = lax.ppermute(even_out, "lon", pairs_of(lons, 0))
-    odd = lax.ppermute(odd_out, "lon", pairs_of(lons, 1))
+    odd_o = lax.ppermute(odd_out_o, ("comp", "lon"), pairs_of(bands, 1))
+    odd_a = lax.ppermute(odd_out_a, "lon", pairs_of(lons, 1))
     ocean_top, air_top, ocean_forced, air_forced = call(
         force_own_kernel,
         (
@@ -543,26 +580,17 @@
             shape(o_grid, BF16), shape(a_grid, BF16),
         ),
         [surface], "force_own", 10**6, 4 * 10**6,
-        ocean_mask, surface_temp, air_fluxes, got, ocean_grid, air_grid, *weights,
+        *surface_args, got, ocean_grid, air_grid, *weights,
     )
 
-    a_conv = convolution(conv_air_kernel, "conv_air", air_forced, even, odd, edge, a_matrix)
-    a_other = lax.ppermute(a_conv, "ch", ring(2, 1))
-    o_conv = convolution(conv_ocean_kernel, "conv_ocean", ocean_forced, even, odd, None, o_matrix)
+    (o_conv,) = convolution(conv_ocean_kernel, "conv_ocean", ocean_forced, even, odd_o, None, o_matrix)
     o_other = lax.ppermute(o_conv, "ch", ring(2, 1))
+    a_convs = convolution(conv_air_kernel, "conv_air", air_forced, even, odd_a, edge, a_matrix)
+    a_others = [lax.ppermute(part, "ch", ring(2, 1)) for part in a_convs]
 
     a_hid, o_hid = air_up.shape[1], ocean_up.shape[1]
-    a_next = call(
-        functools.partial(mlp_kernel, False), shape(a_grid, BF16),
-        [
-            pltpu.VMEM((2, 2 * a_ch, 2 * LANES), F32), pltpu.VMEM((a_hid, 2 * a_ch), BF16),
-            pltpu.VMEM((2 * a_ch, a_hid), BF16),
-        ],
-        "mlp_air", 10**9, 3 * 10**6,
-        a_conv, a_other, air_gain.reshape(1, -1), air_up, air_down.T, air_top, air_forced,
-    )
     o_next = call(
-        functools.partial(mlp_kernel, True), shape(o_grid, BF16),
+        functools.partial(mlp_kernel, True, 0), shape(o_grid, BF16),
         [
             pltpu.VMEM((2, 2 * o_ch, 2 * LANES), F32), pltpu.VMEM((o_hid, 2 * o_ch), BF16),
             pltpu.VMEM((2 * o_ch, o_hid), BF16),
@@ -571,6 +599,20 @@
         o_conv, o_other, ocean_gain.reshape(1, -1), ocean_up, ocean_down, ocean_top, ocean_forced,
         ocean_mask,
     )
+    done = []
+    a_convs, o_next = lax.optimization_barrier((a_convs, o_next))
+    for level, (part, other) in enumerate(zip(a_convs, a_others)):
+        a_next = call(
+            functools.partial(mlp_kernel, False, level),
+            shape((2, level + 1) + a_grid[2:], BF16),
+            [
+                pltpu.VMEM((2, 2 * a_ch, 2 * LANES), F32), pltpu.VMEM((a_hid, 2 * a_ch), BF16),
+                pltpu.VMEM((2 * a_ch, a_hid), BF16),
+            ],
+            f"mlp_air{level}", 10**9, 3 * 10**6,
+            part, other, air_gain.reshape(1, -1), air_up, air_down.T, air_top, air_forced, *done,
+        )
+        done = [a_next]
     ocean_next = jnp.transpose(o_next, (1, 3, 2, 0, 4)).reshape(ocean_state.shape)
     air_next = jnp.transpose(a_next, (1, 3, 2, 0, 4))
     return (ocean_next, air_next)

time: 58.8 us -> 50.4 us (0.86)
  waiting for transfers between devices: 15.2 us -> 6.04 us
  Pallas kernels: 19.6 us -> 20.5 us
  starting transfers between devices: 15 us -> 15.6 us
    ppermute x1, waiting for transfers between devices: 4.82 us -> 0.41 us  [per_device(): o_other = lax.ppermute(o_conv, 'ch', ring(2, 1))]
    ppermute x1, waiting for transfers between devices: 2.88 us -> 0.01 us  [per_device(): got = lax.ppermute(packed, 'comp', ring(2, 1))]
    ppermute x3 -> x4, waiting for transfers between devices: 7.54 us -> 5.62 us  [the longest x1 4.21 us: per_device(): odd_o = lax.ppermute(odd_out_o, ('comp', 'lon'), pairs_of(bands, 1))]
    ppermute x3 -> x4, starting transfers between devices: 13.1 us -> 11.7 us  [the longest x1 9.61 us: per_device(): odd_o = lax.ppermute(odd_out_o, ('comp', 'lon'), pairs_of(bands, 1))]
    ppermute x1, starting transfers between devices: 1.32 us -> 2.38 us  [per_device(): got = lax.ppermute(packed, 'comp', ring(2, 1))]
    pallas_call x2 -> x3, Pallas kernels: 6.69 us -> 7.62 us  [the longest x2 7.4 us: convolution(): pl.pallas_call(kernel, grid=(channels // count,), out_shape=[jax.ShapeDty...]
    ppermute x1, starting transfers between devices: 0.52 us -> 1.44 us  [per_device(): o_other = lax.ppermute(o_conv, 'ch', ring(2, 1))]
  transfers between devices with their start and end apart: 6 -> 7, of which waited for: 3 -> 3; matrix products, arithmetic and copies ran while one was open for 3% -> 5% of each run, Pallas kernels for 21% -> 35%
where the time goes in v5:
time: 50.4 us; the launch traced here: 50.1 us
  Pallas kernels  20.5 us (41%)
  starting transfers between devices  15.6 us (31%)
  local copies, waits for them, and re-layouts  7.02 us (14%)
  waiting for transfers between devices  6.04 us (12%)
  between operations  0.91 us (2%)
    pallas_call x5, Pallas kernels, call(): pl.pallas_call(kernel, out_shape=out_shape, in_specs=[VMEM] * len(args),...  10.6 us
    ppermute x1, starting transfers between devices, per_device(): odd_o = lax.ppermute(odd_out_o, ('comp', 'lon'), pairs_of(bands, 1))  9.61 us
    pallas_call x2, Pallas kernels, convolution(): pl.pallas_call(kernel, grid=(channels // count,), out_shape=[jax.ShapeDty...  7.4 us
    unnamed x36, local copies, waits for them, and re-layouts  5.8 us
    ppermute x1, waiting for transfers between devices, per_device(): odd_o = lax.ppermute(odd_out_o, ('comp', 'lon'), pairs_of(bands, 1))  4.21 us
    ppermute x1, starting transfers between devices, per_device(): got = lax.ppermute(packed, 'comp', ring(2, 1))  2.38 us
    pallas_call x1, Pallas kernels, toeplitz(): pl.pallas_call(both_toeplitz_kernel, grid=(2,), out_shape=[jax.ShapeDtype...  2.35 us
    ppermute x2, starting transfers between devices, per_device(): a_others = [lax.ppermute(part, 'ch', ring(2, 1)) for part in a_convs]  2.11 us
  transfers between devices with their start and end apart: 7, of which 3 were waited for; matrix products, arithmetic and copies ran while one was open for 5% of the time, Pallas kernels for 35%

profile of v5, /device:TPU:8, one launch (start us, length us, event | category | flops | bytes accessed | tf_op | source)
XLA Modules:
  0.0 50.1 jit_solution(13633676049272285836)
XLA Ops:
  0.7 1.1 %copy.32 = bf16[2,96,4,2,128]{4,1,2,0,3:T(8,128)(2,1)S(1)} copy(bf16[2,96,4,2,128]{4,3,2,1,0:T(2,128)(2,1)} %param.17) | data formatting | bytes 786432 | tf_op args[2]
  1.8 0.7 %copy-done = f32[4,4,2,128]{3,2,1,0:T(2,128)S(1)} copy-done((f32[4,4,2,128]{3,2,1,0:T(2,128)S(1)}, f32[4,4,2,128]{3,2,1,0:T(2,128)}, u32[]{:S(2)}) %copy-start) | copy-done | bytes 16408
  2.5 0.7 %copy-done.2 = f32[4,256]{1,0:T(4,128)S(1)} copy-done((f32[4,256]{1,0:T(4,128)S(1)}, f32[4,256]{1,0:T(4,128)}, u32[]{:S(2)}) %copy-start.2) | copy-done | bytes 4120
  3.1 0.7 %copy-done.4 = s32[4,256]{1,0:T(4,128)S(1)} copy-done((s32[4,256]{1,0:T(4,128)S(1)}, s32[4,256]{1,0:T(4,128)}, u32[]{:S(2)}) %copy-start.4) | copy-done | bytes 4120
  4.1 2.4 %collective-permute-start = (f32[120,128]{1,0:T(8,128)S(1)}, f32[120,128]{1,0:T(8,128)S(1)}, u32[]{:S(2)}, u32[]{:S(2)}) collective-permute-start(f32[120,128]{1,0:T(8,128)S(1)} %pack.1), channel_id=1, source_target_pairs={{0,128},{128,0},{1,129},{129,1},{2,130},{130,2},{3,131},{131,3},{4... | collective-permute-start | bytes 184328 | tf_op jit(solution)/shard_map/ppermute | solution.py:552
  6.4 1.1 %reshape.25 = bf16[3,64,4,2,128]{4,3,2,1,0:T(2,128)(2,1)S(1)} reshape(bf16[3,64,4,256]{3,2,1,0:T(4,128)(2,1)} %param.15) | data formatting | bytes 786432 | tf_op jit(solution)/shard_map/reshape | solution.py:555
  7.8 2.4 %matrix.1 = (bf16[8,6,112,256]{3,2,1,0:T(8,128)(2,1)S(1)}, bf16[12,4,112,256]{3,2,1,0:T(8,128)(2,1)S(1)}) custom-call(f32[3,7,7,64]{3,2,1,0:T(8,128)S(1)} %bitcast.25, f32[3,7,7,96]{3,2,1,0:T(8,128)S(1)} %bitcast.26), custom_call_target="tpu_custom_call" | custom-call | flops 2000000000 | bytes 6000000 | tf_op jit(solution)/shard_map/matrix/pallas_call | solution.py:497
  10.2 0.4 force_halo.1
  10.7 9.6 %collective-permute-start.3 = (bf16[1152,128]{1,0:T(8,128)(2,1)S(1)}, bf16[1152,128]{1,0:T(8,128)(2,1)S(1)}, u32[]{:S(2)}, u32[]{:S(2)}) collective-permute-start(bf16[1152,128]{1,0:T(8,128)(2,1)S(1)} %get-tuple-element.37), channel_id=1, source_target_pairs={{2,4},{4,2},{6,8},{8,6},{10,12},{12,10},{14,16},{16,14},{18,20},{2... | collective-permute-start | bytes 884744 | tf_op jit(solution)/shard_map/ppermute | solution.py:574
  20.3 0.3 force_own.1
  20.6 4.2 %collective-permute-done.3.odd_ref = bf16[1152,128]{1,0:T(8,128)(2,1)S(1)} collective-permute-done((bf16[1152,128]{1,0:T(8,128)(2,1)S(1)}, bf16[1152,128]{1,0:T(8,128)(2,1)S(1)}, u32[]{:S(2)}, u32[]{:S(2)}) %collective-permute-start.3) | collective-permute-done | bytes 294944 | tf_op jit(solution)/shard_map/ppermute | solution.py:574
  24.8 2.4 %conv_ocean.1.refs_0_ = bf16[2,3,4,64,128]{4,3,2,1,0:T(8,128)(2,1)S(1)} custom-call(bf16[2,3,4,64,128]{4,3,2,1,0:T(8,128)(2,1)S(1)} %get-tuple-element.36.own_ref.refs_6_, bf16[2400,128]{1,0:T(8,128)(2,1)S(1)} %collective-permute-done.1.even_ref, bf16[1152,128]{1,0:T(8,128)(2,1)S(1)} %collective-permute-done.3.odd_ref, ...), custom_call_target="tpu_custom_call" | custom-call | flops 2000000000 | bytes 4000000 | tf_op jit(solution)/shard_map/conv_ocean/pallas_call | solution.py:415
  27.2 1.4 %collective-permute-start.4 = (bf16[2,3,4,64,128]{4,3,2,1,0:T(8,128)(2,1)S(1)}, bf16[2,3,4,64,128]{4,3,2,1,0:T(8,128)(2,1)S(1)}, u32[]{:S(2)}, u32[]{:S(2)}) collective-permute-start(bf16[2,3,4,64,128]{4,3,2,1,0:T(8,128)(2,1)S(1)} %conv_ocean.1.refs_0_), channel_id=1, source_target_pairs={{0,1},{1,0},{2,3},{3,2},{4,5},{5,4},{6,7},{7,6},{8,9},{9,8},{10,11... | collective-permute-start | bytes 1179656 | tf_op jit(solution)/shard_map/ppermute | solution.py:587
  28.6 1.4 %collective-permute-done.2.odd_ref = bf16[1248,128]{1,0:T(8,128)(2,1)S(1)} collective-permute-done((bf16[1248,128]{1,0:T(8,128)(2,1)S(1)}, bf16[1248,128]{1,0:T(8,128)(2,1)S(1)}, u32[]{:S(2)}, u32[]{:S(2)}) %collective-permute-start.2) | collective-permute-done | bytes 319520 | tf_op jit(solution)/shard_map/ppermute | solution.py:575
  30.0 5.0 %conv_air.1 = (bf16[2,1,4,96,128]{4,3,2,1,0:T(8,128)(2,1)S(1)}, bf16[2,1,4,96,128]{4,3,2,1,0:T(8,128)(2,1)S(1)}) custom-call(bf16[2,2,4,96,128]{4,3,2,1,0:T(8,128)(2,1)S(1)} %get-tuple-element.29.own_ref.refs_6_, bf16[2400,128]{1,0:T(8,128)(2,1)S(1)} %collective-permute-done.1.even_ref, bf16[1248,128]{1,0:T(8,128)(2,1)S(1)} %collective-permute-done.2.odd_ref, ...), custom_call_target="tpu_custom_call" | custom-call | flops 2000000000 | bytes 4000000 | tf_op jit(solution)/shard_map/conv_air/pallas_call | solution.py:415
  35.1 1.4 %collective-permute-start.6 = (bf16[2,1,4,96,128]{4,3,2,1,0:T(8,128)(2,1)S(1)}, bf16[2,1,4,96,128]{4,3,2,1,0:T(8,128)(2,1)S(1)}, u32[]{:S(2)}, u32[]{:S(2)}) collective-permute-start(bf16[2,1,4,96,128]{4,3,2,1,0:T(8,128)(2,1)S(1)} %get-tuple-element.43.refs_0_), channel_id=1, source_target_pairs={{0,1},{1,0},{2,3},{3,2},{4,5},{5,4},{6,7},{7,6},{8,9},{9,8},{10,11... | collective-permute-start | bytes 589832 | tf_op jit(solution)/shard_map/ppermute | solution.py:589
  36.5 0.7 %collective-permute-start.5 = (bf16[2,1,4,96,128]{4,3,2,1,0:T(8,128)(2,1)S(1)}, bf16[2,1,4,96,128]{4,3,2,1,0:T(8,128)(2,1)S(1)}, u32[]{:S(2)}, u32[]{:S(2)}) collective-permute-start(bf16[2,1,4,96,128]{4,3,2,1,0:T(8,128)(2,1)S(1)} %get-tuple-element.41.refs_0_), channel_id=1, source_target_pairs={{0,1},{1,0},{2,3},{3,2},{4,5},{5,4},{6,7},{7,6},{8,9},{9,8},{10,11... | collective-permute-start | bytes 589832 | tf_op jit(solution)/shard_map/ppermute | solution.py:589
  37.2 0.4 collective-permute-done.4.refs_1_
  37.6 5.3 %mlp_ocean.1 = bf16[2,3,4,64,128]{4,3,2,1,0:T(8,128)(2,1)S(1)} custom-call(bf16[2,3,4,64,128]{4,3,2,1,0:T(8,128)(2,1)S(1)} %conv_ocean.1.refs_0_, bf16[2,3,4,64,128]{4,3,2,1,0:T(8,128)(2,1)S(1)} %collective-permute-done.4.refs_1_, f32[1,128]{1,0:T(1,128)S(1)} %bitcast.29, bf16[128,512]{1,0:T(8,128)(2,1)S(1)} %copy-done.10, bf16[512,128]{1,0:T(8,128)(2,1)S(1)} %copy-done.11, ...), custom_call_target="tpu_custom_call" | custom-call | flops 1000000000 | bytes 3000000 | tf_op jit(solution)/shard_map/mlp_ocean/pallas_call | solution.py:28
  42.9 0.4 copy.27
  43.3 1.0 %reshape.26 = bf16[3,64,4,256]{3,2,1,0:T(4,128)(2,1)} reshape(bf16[3,64,4,2,128]{4,3,2,1,0:T(2,128)(2,1)S(1)} %copy.27) | data formatting | bytes 786432
  44.3 2.3 %mlp_air0.1.refs_7_ = bf16[2,1,4,96,128]{4,3,2,1,0:T(8,128)(2,1)S(1)} custom-call(bf16[2,1,4,96,128]{4,3,2,1,0:T(8,128)(2,1)S(1)} %get-tuple-element.43.refs_0_, bf16[2,1,4,96,128]{4,3,2,1,0:T(8,128)(2,1)S(1)} %collective-permute-done.6.refs_1_, f32[1,192]{1,0:T(1,128)S(1)} %bitcast.27, bf16[192,768]{1,0:T(8,128)(2,1)S(1)} %copy-done.8, ...), custom_call_target="tpu_custom_call" | custom-call | flops 1000000000 | bytes 3000000 | tf_op jit(solution)/shard_map/mlp_air0/pallas_call | solution.py:28
  46.7 2.3 %mlp_air1.1 = bf16[2,2,4,96,128]{4,3,2,1,0:T(8,128)(2,1)S(1)} custom-call(bf16[2,1,4,96,128]{4,3,2,1,0:T(8,128)(2,1)S(1)} %get-tuple-element.41.refs_0_, bf16[2,1,4,96,128]{4,3,2,1,0:T(8,128)(2,1)S(1)} %collective-permute-done.5.refs_1_, f32[1,192]{1,0:T(1,128)S(1)} %bitcast.28, bf16[192,768]{1,0:T(8,128)(2,1)S(1)} %copy-done.8, ...), custom_call_target="tpu_custom_call" | custom-call | flops 1000000000 | bytes 3000000 | tf_op jit(solution)/shard_map/mlp_air1/pallas_call | solution.py:28
  49.0 1.2 %copy.24 = bf16[2,96,4,2,128]{4,3,2,1,0:T(2,128)(2,1)} copy(bf16[2,96,4,2,128]{4,1,2,0,3:T(8,128)(2,1)S(1)} %bitcast.19) | data formatting | bytes 786432
  (37 shorter events, 0.5 us)
Async XLA Ops:
  0.6 7.1 %copy-start.12 = (f32[64,3,7,7]{0,3,2,1:T(8,128)S(1)}, f32[64,3,7,7]{0,3,2,1:T(8,128)}, u32[]{:S(2)}) copy-start(f32[64,3,7,7]{0,3,2,1:T(8,128)} %param.20) | copy-start | bytes 112900
  0.6 7.1 %copy-start.13 = (f32[96,3,7,7]{0,3,2,1:T(8,128)S(1)}, f32[96,3,7,7]{0,3,2,1:T(8,128)}, u32[]{:S(2)}) copy-start(f32[96,3,7,7]{0,3,2,1:T(8,128)} %param.24) | copy-start | bytes 169348
  1.7 0.7 %copy-start = (f32[4,4,2,128]{3,2,1,0:T(2,128)S(1)}, f32[4,4,2,128]{3,2,1,0:T(2,128)}, u32[]{:S(2)}) copy-start(f32[4,4,2,128]{3,2,1,0:T(2,128)} %flux_ref.3) | copy-start | bytes 49156
  2.5 0.7 %copy-start.2 = (f32[4,256]{1,0:T(4,128)S(1)}, f32[4,256]{1,0:T(4,128)}, u32[]{:S(2)}) copy-start(f32[4,256]{1,0:T(4,128)} %temp_ref.3) | copy-start | bytes 12292
  3.1 0.7 %copy-start.4 = (s32[4,256]{1,0:T(4,128)S(1)}, s32[4,256]{1,0:T(4,128)}, u32[]{:S(2)}) copy-start(s32[4,256]{1,0:T(4,128)} %refs_7_.1) | copy-start | bytes 12292
  4.1 6.1 %collective-permute-start = (f32[120,128]{1,0:T(8,128)S(1)}, f32[120,128]{1,0:T(8,128)S(1)}, u32[]{:S(2)}, u32[]{:S(2)}) collective-permute-start(f32[120,128]{1,0:T(8,128)S(1)} %pack.1), channel_id=1, source_target_pairs={{0,128},{128,0},{1,129},{129,1},{2,130},{130,2},{3,131},{131,3},{4... | collective-permute-start | bytes 184328 | tf_op jit(solution)/shard_map/ppermute | solution.py:552
  7.7 2.4 %copy-start.1 = (f32[4,4,2,128]{3,2,1,0:T(2,128)S(1)}, f32[4,4,2,128]{3,2,1,0:T(2,128)}, u32[]{:S(2)}) copy-start(f32[4,4,2,128]{3,2,1,0:T(2,128)} %flux_ref.3) | copy-start | bytes 49156
  7.7 2.4 %copy-start.3 = (f32[4,256]{1,0:T(4,128)S(1)}, f32[4,256]{1,0:T(4,128)}, u32[]{:S(2)}) copy-start(f32[4,256]{1,0:T(4,128)} %temp_ref.3) | copy-start | bytes 12292
  7.7 2.4 %copy-start.5 = (s32[4,256]{1,0:T(4,128)S(1)}, s32[4,256]{1,0:T(4,128)}, u32[]{:S(2)}) copy-start(s32[4,256]{1,0:T(4,128)} %refs_7_.1) | copy-start | bytes 12292
  7.7 2.4 %copy-start.6 = (f32[4,64]{1,0:T(4,128)S(1)}, f32[4,64]{1,0:T(4,128)}, u32[]{:S(2)}) copy-start(f32[4,64]{1,0:T(4,128)} %fw_ref.3) | copy-start | bytes 3076
  7.7 2.4 %copy-start.7 = (f32[96]{0:T(128)S(1)}, f32[96]{0:T(128)}, u32[]{:S(2)}) copy-start(f32[96]{0:T(128)} %param.29) | copy-start | bytes 1156
  10.6 14.2 %collective-permute-start.1 = (bf16[2400,128]{1,0:T(8,128)(2,1)S(1)}, bf16[2400,128]{1,0:T(8,128)(2,1)S(1)}, u32[]{:S(2)}, u32[]{:S(2)}) collective-permute-start(bf16[2400,128]{1,0:T(8,128)(2,1)S(1)} %get-tuple-element.30), channel_id=1, source_target_pairs={{0,2},{2,0},{4,6},{6,4},{8,10},{10,8},{12,14},{14,12},{16,18},{18,... | collective-permute-start | bytes 1843208 | tf_op jit(solution)/shard_map/ppermute | solution.py:573
  10.7 14.1 %collective-permute-start.3 = (bf16[1152,128]{1,0:T(8,128)(2,1)S(1)}, bf16[1152,128]{1,0:T(8,128)(2,1)S(1)}, u32[]{:S(2)}, u32[]{:S(2)}) collective-permute-start(bf16[1152,128]{1,0:T(8,128)(2,1)S(1)} %get-tuple-element.37), channel_id=1, source_target_pairs={{2,4},{4,2},{6,8},{8,6},{10,12},{12,10},{14,16},{16,14},{18,20},{2... | collective-permute-start | bytes 884744 | tf_op jit(solution)/shard_map/ppermute | solution.py:574
  20.3 9.7 %collective-permute-start.2 = (bf16[1248,128]{1,0:T(8,128)(2,1)S(1)}, bf16[1248,128]{1,0:T(8,128)(2,1)S(1)}, u32[]{:S(2)}, u32[]{:S(2)}) collective-permute-start(bf16[1248,128]{1,0:T(8,128)(2,1)S(1)} %get-tuple-element.31), channel_id=1, source_target_pairs={{2,4},{4,2},{6,8},{8,6},{10,12},{12,10},{14,16},{16,14},{18,20},{2... | collective-permute-start | bytes 958472 | tf_op jit(solution)/shard_map/ppermute | solution.py:575
  27.2 10.4 %collective-permute-start.4 = (bf16[2,3,4,64,128]{4,3,2,1,0:T(8,128)(2,1)S(1)}, bf16[2,3,4,64,128]{4,3,2,1,0:T(8,128)(2,1)S(1)}, u32[]{:S(2)}, u32[]{:S(2)}) collective-permute-start(bf16[2,3,4,64,128]{4,3,2,1,0:T(8,128)(2,1)S(1)} %conv_ocean.1.refs_0_), channel_id=1, source_target_pairs={{0,1},{1,0},{2,3},{3,2},{4,5},{5,4},{6,7},{7,6},{8,9},{9,8},{10,11... | collective-permute-start | bytes 1179656 | tf_op jit(solution)/shard_map/ppermute | solution.py:587
  30.0 7.6 %copy-start.10 = (bf16[128,512]{1,0:T(8,128)(2,1)S(1)}, bf16[128,512]{1,0:T(8,128)(2,1)}, u32[]{:S(2)}) copy-start(bf16[128,512]{1,0:T(8,128)(2,1)} %refs_3_.3) | copy-start | bytes 393220
  30.0 7.6 %copy-start.11 = (bf16[512,128]{1,0:T(8,128)(2,1)S(1)}, bf16[512,128]{1,0:T(8,128)(2,1)}, u32[]{:S(2)}) copy-start(bf16[512,128]{1,0:T(8,128)(2,1)} %refs_4_.1) | copy-start | bytes 393220
  30.0 7.6 %copy-start.15 = (f32[128]{0:T(128)S(1)}, f32[128]{0:T(128)}, u32[]{:S(2)}) copy-start(f32[128]{0:T(128)} %param.21) | copy-start | bytes 1540
  35.1 9.3 %copy-start.8 = (bf16[192,768]{1,0:T(8,128)(2,1)S(1)}, bf16[192,768]{1,0:T(8,128)(2,1)}, u32[]{:S(2)}) copy-start(bf16[192,768]{1,0:T(8,128)(2,1)} %refs_3_.5) | copy-start | bytes 884740
  35.1 9.2 %copy-start.9 = (bf16[768,192]{0,1:T(8,128)(2,1)S(1)}, bf16[768,192]{0,1:T(8,128)(2,1)}, u32[]{:S(2)}) copy-start(bf16[768,192]{0,1:T(8,128)(2,1)} %param.27) | copy-start | bytes 884740
  35.1 9.2 %copy-start.14 = (f32[192]{0:T(256)S(1)}, f32[192]{0:T(256)}, u32[]{:S(2)}) copy-start(f32[192]{0:T(256)} %param.25) | copy-start | bytes 2308
  35.1 9.2 %collective-permute-start.6 = (bf16[2,1,4,96,128]{4,3,2,1,0:T(8,128)(2,1)S(1)}, bf16[2,1,4,96,128]{4,3,2,1,0:T(8,128)(2,1)S(1)}, u32[]{:S(2)}, u32[]{:S(2)}) collective-permute-start(bf16[2,1,4,96,128]{4,3,2,1,0:T(8,128)(2,1)S(1)} %get-tuple-element.43.refs_0_), channel_id=1, source_target_pairs={{0,1},{1,0},{2,3},{3,2},{4,5},{5,4},{6,7},{7,6},{8,9},{9,8},{10,11... | collective-permute-start | bytes 589832 | tf_op jit(solution)/shard_map/ppermute | solution.py:589
  36.5 10.1 %collective-permute-start.5 = (bf16[2,1,4,96,128]{4,3,2,1,0:T(8,128)(2,1)S(1)}, bf16[2,1,4,96,128]{4,3,2,1,0:T(8,128)(2,1)S(1)}, u32[]{:S(2)}, u32[]{:S(2)}) collective-permute-start(bf16[2,1,4,96,128]{4,3,2,1,0:T(8,128)(2,1)S(1)} %get-tuple-element.41.refs_0_), channel_id=1, source_target_pairs={{0,1},{1,0},{2,3},{3,2},{4,5},{5,4},{6,7},{7,6},{8,9},{9,8},{10,11... | collective-permute-start | bytes 589832 | tf_op jit(solution)/shard_map/ppermute | solution.py:589

commit v6 on v5

--- a/solution.py
+++ b/solution.py
@@ -10,6 +10,7 @@
 F32 = jnp.float32
 BF16 = jnp.bfloat16
 LANES = 128
+TOGETHER = 4
 PARAMS = pltpu.CompilerParams(vmem_limit_bytes=24 * 2**20)
 VMEM = pl.BlockSpec(memory_space=pltpu.VMEM)
 
@@ -314,17 +315,19 @@
     inner = (lon & 1) == 1
     swap_west = jnp.where(lon == 0, 1, 0)
     swap_east = jnp.where(lon == lax.axis_size("lon") - 1, 1, 0)
-    channels = pl.num_programs(0) * count
     first_odd = pl.program_id(0) * count
     first_even = first_odd + even_ref.shape[0] - odd_ref.shape[0]
 
-    def tiles_at(tile):
-        at = tile * channels
-        return rim_tile(even_ref, odd_ref, first_even + at, first_odd + at, count)
+    stride = 3 * levels * out_refs[0].shape[3] * pl.num_programs(0)
+
+    def tiles_at(half, tile):
+        at = tile * (stride // (3 * levels))
+        moved = half * stride
+        return rim_tile(even_ref, odd_ref, first_even + moved + at, first_odd + moved + at, count)
 
     start = jnp.where(lax.axis_index("comp") == 0, 0, LANES - 8)
     wide = lane_ids(count)
-    even, odd = tiles_at(2 * levels * 3)
+    even, odd = tiles_at(0, 2 * levels * 3)
     edge_tiles = []
     for tile, swap in (
         (packed_ref[...], None),
@@ -349,9 +352,9 @@
         for level in range(levels):
             west, east = [], []
             for i in range(3):
-                even, odd = tiles_at((west_h * levels + level) * 3 + i)
+                even, odd = tiles_at(west_h, level * 3 + i)
                 west.append(jnp.where(inner, even, odd))
-                even, odd = tiles_at((east_h * levels + level) * 3 + i)
+                even, odd = tiles_at(east_h, level * 3 + i)
                 east.append(jnp.where(inner, odd, even))
             tiles += west + [own_ref[h, level, i].astype(F32) for i in range(band)] + east
         all_tiles.append(tiles)
@@ -445,17 +448,23 @@
 
     if not masked and extra_ref is not None:
         out_ref[:, :first_level] = extra_ref[...]
-
-    def row(at, slot):
-        level = at // band
-        i = lax.rem(at, band)
-        mine = pl.ds(pl.multiple_of(ch * channels, channels), channels)
-        theirs = pl.ds(pl.multiple_of((1 - ch) * channels, channels), channels)
-        for s in range(2):
-            lanes = slice(s * LANES, (s + 1) * LANES)
-            values_ref[slot, mine, lanes] = own_ref[s, level, i].astype(F32)
-            values_ref[slot, theirs, lanes] = other_ref[s, level, i].astype(F32)
-        values = values_ref[slot]
+    theirs = pl.ds(pl.multiple_of((1 - ch) * channels, channels), channels)
+    together = values_ref.shape[1] // (2 * LANES)
+    if masked:
+        sea = extra_ref[...].astype(F32)
+
+    def step(at, carry):
+        level = at // (band // together)
+        first = lax.rem(at, band // together) * together
+        blocks = [
+            (s, n, slice((n * 2 + s) * LANES, (n * 2 + s + 1) * LANES))
+            for n in range(together)
+            for s in range(2)
+        ]
+        for s, n, lanes in blocks:
+            values_ref[mine, lanes] = own_ref[s, level, first + n].astype(F32)
+            values_ref[theirs, lanes] = other_ref[s, level, first + n].astype(F32)
+        values = values_ref[...]
         center = jnp.sum(values, axis=0, keepdims=True) * (1.0 / total)
         values = values - center
         spread = jnp.sum(values * values, axis=0, keepdims=True) * (1.0 / total)
@@ -465,27 +474,21 @@
         doubled = (raw + raw * jnp.tanh(inner)).astype(BF16)
         update = jnp.dot(narrow_ref[down_rows, :], doubled, preferred_element_type=F32) * 0.5
         update = update.astype(BF16).astype(F32)
-        if masked:
-            mask = extra_ref[...]
-            picked = lax.broadcasted_iota(jnp.int32, mask.shape, 0) == i
-            sea = jnp.sum(jnp.where(picked, mask.astype(F32), 0.0), axis=0, keepdims=True)
-        for s in range(2):
-            lanes = slice(s * LANES, (s + 1) * LANES)
+        for s, n, lanes in blocks:
+            i = first + n
             if first_level:
                 forced = forced_ref[s, first_level + level, i].astype(F32)
             else:
                 forced = jnp.where(level == 0, top_ref[s, i], forced_ref[s, level, i].astype(F32))
             result = forced + update[:, lanes]
             if masked:
-                result = result * sea[:, lanes]
+                half = sea[:, s * LANES : (s + 1) * LANES]
+                picked = lax.broadcasted_iota(jnp.int32, half.shape, 0) == i
+                result = result * jnp.sum(jnp.where(picked, half, 0.0), axis=0, keepdims=True)
             out_ref[s, first_level + level, i] = result.astype(BF16)
-
-    def step(at, carry):
-        row(at * 2, 0)
-        row(at * 2 + 1, 1)
         return carry
 
-    lax.fori_loop(0, levels * band // 2, step, 0)
+    lax.fori_loop(0, levels * band // together, step, 0)
 
 
 def toeplitz(ocean_kernel, air_kernel, o_levels, a_levels):
@@ -547,7 +550,7 @@
         scratch_shapes=[pltpu.VMEM(arg.shape, arg.dtype) for arg in surface_args]
         + [pltpu.SemaphoreType.DMA((3,))],
         name="pack",
-        compiler_params=PARAMS,
+        compiler_params=pltpu.CompilerParams(vmem_limit_bytes=60 * 2**20),
     )(*surface_args, air_grid)
     got = lax.ppermute(packed, "comp", ring(2, 1))
     later_ocean, _ = lax.optimization_barrier((ocean_state, packed))
@@ -592,7 +595,7 @@
     o_next = call(
         functools.partial(mlp_kernel, True, 0), shape(o_grid, BF16),
         [
-            pltpu.VMEM((2, 2 * o_ch, 2 * LANES), F32), pltpu.VMEM((o_hid, 2 * o_ch), BF16),
+            pltpu.VMEM((2 * o_ch, TOGETHER * 2 * LANES), F32), pltpu.VMEM((o_hid, 2 * o_ch), BF16),
             pltpu.VMEM((2 * o_ch, o_hid), BF16),
         ],
         "mlp_ocean", 10**9, 3 * 10**6,
@@ -606,7 +609,7 @@
             functools.partial(mlp_kernel, False, level),
             shape((2, level + 1) + a_grid[2:], BF16),
             [
-                pltpu.VMEM((2, 2 * a_ch, 2 * LANES), F32), pltpu.VMEM((a_hid, 2 * a_ch), BF16),
+                pltpu.VMEM((2 * a_ch, TOGETHER * 2 * LANES), F32), pltpu.VMEM((a_hid, 2 * a_ch), BF16),
                 pltpu.VMEM((2 * a_ch, a_hid), BF16),
             ],
             f"mlp_air{level}", 10**9, 3 * 10**6,

time: 50.4 us -> 47.7 us (0.946)
  Pallas kernels: 20.5 us -> 19 us
  local copies, waits for them, and re-layouts: 7.02 us -> 5.68 us
    pallas_call x5, Pallas kernels: 10.6 us -> 6.89 us  [call(): pl.pallas_call(kernel, out_shape=out_shape, in_specs=[VMEM] * len(args),...]
    pallas_call x1, Pallas kernels: 0.22 us -> 2.43 us  [per_device(): pl.pallas_call(pack_kernel, out_shape=shape((rows, LANES), F32), in_specs...]
    unnamed x36 -> x32, local copies, waits for them, and re-layouts: 5.8 us -> 4.46 us
  transfers between devices with their start and end apart: 7 -> 7, of which waited for: 3 -> 3; matrix products, arithmetic and copies ran while one was open for 5% -> 6% of each run, Pallas kernels for 35% -> 31%
where the time goes in v6:
time: 47.7 us; the launch traced here: 47.5 us
  Pallas kernels  19 us (40%)
  starting transfers between devices  15.8 us (33%)
  waiting for transfers between devices  6.03 us (13%)
  local copies, waits for them, and re-layouts  5.68 us (12%)
  between operations  0.91 us (2%)
    ppermute x1, starting transfers between devices, per_device(): odd_o = lax.ppermute(odd_out_o, ('comp', 'lon'), pairs_of(bands, 1))  9.82 us
    pallas_call x2, Pallas kernels, convolution(): pl.pallas_call(kernel, grid=(channels // count,), out_shape=[jax.ShapeDty...  7.36 us
    pallas_call x5, Pallas kernels, call(): pl.pallas_call(kernel, out_shape=out_shape, in_specs=[VMEM] * len(args),...  6.89 us
    unnamed x32, local copies, waits for them, and re-layouts  4.46 us
    ppermute x1, waiting for transfers between devices, per_device(): odd_o = lax.ppermute(odd_out_o, ('comp', 'lon'), pairs_of(bands, 1))  4.21 us
    pallas_call x1, Pallas kernels, per_device(): pl.pallas_call(pack_kernel, out_shape=shape((rows, LANES), F32), in_specs...  2.43 us
    ppermute x1, starting transfers between devices, per_device(): got = lax.ppermute(packed, 'comp', ring(2, 1))  2.38 us
    pallas_call x1, Pallas kernels, toeplitz(): pl.pallas_call(both_toeplitz_kernel, grid=(2,), out_shape=[jax.ShapeDtype...  2.34 us
  transfers between devices with their start and end apart: 7, of which 3 were waited for; matrix products, arithmetic and copies ran while one was open for 6% of the time, Pallas kernels for 31%

profile of v6, /device:TPU:8, one launch (start us, length us, event | category | flops | bytes accessed | tf_op | source)
XLA Modules:
  0.0 47.5 jit_solution(13312522673294906304)
XLA Ops:
  0.7 1.8 %copy.32 = bf16[2,96,4,2,128]{4,1,2,0,3:T(8,128)(2,1)} copy(bf16[2,96,4,2,128]{4,3,2,1,0:T(2,128)(2,1)} %param.17) | data formatting | bytes 786432 | tf_op args[2]
  2.5 2.4 %pack.1 = f32[120,128]{1,0:T(8,128)} custom-call(s32[4,256]{1,0:T(4,128)} %refs_7_.1, f32[4,256]{1,0:T(4,128)} %temp_ref.3, f32[4,4,2,128]{3,2,1,0:T(2,128)} %flux_ref.3, bf16[2,2,4,96,128]{4,3,2,1,0:T(8,128)(2,1)} %bitcast.14), custom_call_target="tpu_custom_call" | custom-call | tf_op jit(solution)/shard_map/pack/pallas_call | solution.py:545
  4.9 2.4 %collective-permute-start = (f32[120,128]{1,0:T(8,128)}, f32[120,128]{1,0:T(8,128)S(1)}, u32[]{:S(2)}, u32[]{:S(2)}) collective-permute-start(f32[120,128]{1,0:T(8,128)} %pack.1), channel_id=1, source_target_pairs={{0,128},{128,0},{1,129},{129,1},{2,130},{130,2},{3,131},{131,3},{4... | collective-permute-start | bytes 184328 | tf_op jit(solution)/shard_map/ppermute | solution.py:555
  7.3 1.1 %reshape.25 = bf16[3,64,4,2,128]{4,3,2,1,0:T(2,128)(2,1)S(1)} reshape(bf16[3,64,4,256]{3,2,1,0:T(4,128)(2,1)} %param.15) | data formatting | bytes 786432 | tf_op jit(solution)/shard_map/reshape | solution.py:558
  8.5 0.1 copy.31
  8.6 2.3 %matrix.1 = (bf16[8,6,112,256]{3,2,1,0:T(8,128)(2,1)S(1)}, bf16[12,4,112,256]{3,2,1,0:T(8,128)(2,1)S(1)}) custom-call(f32[3,7,7,64]{3,2,1,0:T(8,128)S(1)} %bitcast.25, f32[3,7,7,96]{3,2,1,0:T(8,128)S(1)} %bitcast.26), custom_call_target="tpu_custom_call" | custom-call | flops 2000000000 | bytes 6000000 | tf_op jit(solution)/shard_map/matrix/pallas_call | solution.py:500
  11.1 0.4 force_halo.1
  11.4 0.1 collective-permute-start.1
  11.5 9.8 %collective-permute-start.3 = (bf16[1152,128]{1,0:T(8,128)(2,1)S(1)}, bf16[1152,128]{1,0:T(8,128)(2,1)S(1)}, u32[]{:S(2)}, u32[]{:S(2)}) collective-permute-start(bf16[1152,128]{1,0:T(8,128)(2,1)S(1)} %get-tuple-element.37), channel_id=1, source_target_pairs={{2,4},{4,2},{6,8},{8,6},{10,12},{12,10},{14,16},{16,14},{18,20},{2... | collective-permute-start | bytes 884744 | tf_op jit(solution)/shard_map/ppermute | solution.py:577
  21.4 0.3 force_own.1
  21.7 4.2 %collective-permute-done.3.odd_ref = bf16[1152,128]{1,0:T(8,128)(2,1)S(1)} collective-permute-done((bf16[1152,128]{1,0:T(8,128)(2,1)S(1)}, bf16[1152,128]{1,0:T(8,128)(2,1)S(1)}, u32[]{:S(2)}, u32[]{:S(2)}) %collective-permute-start.3) | collective-permute-done | bytes 294944 | tf_op jit(solution)/shard_map/ppermute | solution.py:577
  25.9 2.4 %conv_ocean.1.refs_0_ = bf16[2,3,4,64,128]{4,3,2,1,0:T(8,128)(2,1)S(1)} custom-call(bf16[2,3,4,64,128]{4,3,2,1,0:T(8,128)(2,1)S(1)} %get-tuple-element.36.own_ref.refs_6_, bf16[2400,128]{1,0:T(8,128)(2,1)S(1)} %collective-permute-done.1.even_ref, bf16[1152,128]{1,0:T(8,128)(2,1)S(1)} %collective-permute-done.3.odd_ref, ...), custom_call_target="tpu_custom_call" | custom-call | flops 2000000000 | bytes 4000000 | tf_op jit(solution)/shard_map/conv_ocean/pallas_call | solution.py:418
  28.3 1.4 %collective-permute-start.4 = (bf16[2,3,4,64,128]{4,3,2,1,0:T(8,128)(2,1)S(1)}, bf16[2,3,4,64,128]{4,3,2,1,0:T(8,128)(2,1)S(1)}, u32[]{:S(2)}, u32[]{:S(2)}) collective-permute-start(bf16[2,3,4,64,128]{4,3,2,1,0:T(8,128)(2,1)S(1)} %conv_ocean.1.refs_0_), channel_id=1, source_target_pairs={{0,1},{1,0},{2,3},{3,2},{4,5},{5,4},{6,7},{7,6},{8,9},{9,8},{10,11... | collective-permute-start | bytes 1179656 | tf_op jit(solution)/shard_map/ppermute | solution.py:590
  29.7 1.4 %collective-permute-done.2.odd_ref = bf16[1248,128]{1,0:T(8,128)(2,1)S(1)} collective-permute-done((bf16[1248,128]{1,0:T(8,128)(2,1)S(1)}, bf16[1248,128]{1,0:T(8,128)(2,1)S(1)}, u32[]{:S(2)}, u32[]{:S(2)}) %collective-permute-start.2) | collective-permute-done | bytes 319520 | tf_op jit(solution)/shard_map/ppermute | solution.py:578
  31.1 5.0 %conv_air.1 = (bf16[2,1,4,96,128]{4,3,2,1,0:T(8,128)(2,1)S(1)}, bf16[2,1,4,96,128]{4,3,2,1,0:T(8,128)(2,1)S(1)}) custom-call(bf16[2,2,4,96,128]{4,3,2,1,0:T(8,128)(2,1)S(1)} %get-tuple-element.29.own_ref.refs_6_, bf16[2400,128]{1,0:T(8,128)(2,1)S(1)} %collective-permute-done.1.even_ref, bf16[1248,128]{1,0:T(8,128)(2,1)S(1)} %collective-permute-done.2.odd_ref, ...), custom_call_target="tpu_custom_call" | custom-call | flops 2000000000 | bytes 4000000 | tf_op jit(solution)/shard_map/conv_air/pallas_call | solution.py:418
  36.1 1.4 %collective-permute-start.6 = (bf16[2,1,4,96,128]{4,3,2,1,0:T(8,128)(2,1)S(1)}, bf16[2,1,4,96,128]{4,3,2,1,0:T(8,128)(2,1)S(1)}, u32[]{:S(2)}, u32[]{:S(2)}) collective-permute-start(bf16[2,1,4,96,128]{4,3,2,1,0:T(8,128)(2,1)S(1)} %get-tuple-element.43.refs_0_), channel_id=1, source_target_pairs={{0,1},{1,0},{2,3},{3,2},{4,5},{5,4},{6,7},{7,6},{8,9},{9,8},{10,11... | collective-permute-start | bytes 589832 | tf_op jit(solution)/shard_map/ppermute | solution.py:592
  37.6 0.7 %collective-permute-start.5 = (bf16[2,1,4,96,128]{4,3,2,1,0:T(8,128)(2,1)S(1)}, bf16[2,1,4,96,128]{4,3,2,1,0:T(8,128)(2,1)S(1)}, u32[]{:S(2)}, u32[]{:S(2)}) collective-permute-start(bf16[2,1,4,96,128]{4,3,2,1,0:T(8,128)(2,1)S(1)} %get-tuple-element.41.refs_0_), channel_id=1, source_target_pairs={{0,1},{1,0},{2,3},{3,2},{4,5},{5,4},{6,7},{7,6},{8,9},{9,8},{10,11... | collective-permute-start | bytes 589832 | tf_op jit(solution)/shard_map/ppermute | solution.py:592
  38.2 0.4 collective-permute-done.4.refs_1_
  38.7 3.1 %mlp_ocean.1 = bf16[2,3,4,64,128]{4,3,2,1,0:T(8,128)(2,1)S(1)} custom-call(bf16[2,3,4,64,128]{4,3,2,1,0:T(8,128)(2,1)S(1)} %conv_ocean.1.refs_0_, bf16[2,3,4,64,128]{4,3,2,1,0:T(8,128)(2,1)S(1)} %collective-permute-done.4.refs_1_, f32[1,128]{1,0:T(1,128)S(1)} %bitcast.29, bf16[128,512]{1,0:T(8,128)(2,1)S(1)} %copy-done.8, bf16[512,128]{1,0:T(8,128)(2,1)S(1)} %copy-done.9, ...), custom_call_target="tpu_custom_call" | custom-call | flops 1000000000 | bytes 3000000 | tf_op jit(solution)/shard_map/mlp_ocean/pallas_call | solution.py:29
  41.8 0.4 copy.27
  42.2 1.0 %reshape.26 = bf16[3,64,4,256]{3,2,1,0:T(4,128)(2,1)} reshape(bf16[3,64,4,2,128]{4,3,2,1,0:T(2,128)(2,1)S(1)} %copy.27) | data formatting | bytes 786432
  43.2 1.5 %mlp_air0.1.refs_7_ = bf16[2,1,4,96,128]{4,3,2,1,0:T(8,128)(2,1)S(1)} custom-call(bf16[2,1,4,96,128]{4,3,2,1,0:T(8,128)(2,1)S(1)} %get-tuple-element.43.refs_0_, bf16[2,1,4,96,128]{4,3,2,1,0:T(8,128)(2,1)S(1)} %collective-permute-done.6.refs_1_, f32[1,192]{1,0:T(1,128)S(1)} %bitcast.27, bf16[192,768]{1,0:T(8,128)(2,1)S(1)} %copy-done.6, ...), custom_call_target="tpu_custom_call" | custom-call | flops 1000000000 | bytes 3000000 | tf_op jit(solution)/shard_map/mlp_air0/pallas_call | solution.py:29
  44.8 1.6 %mlp_air1.1 = bf16[2,2,4,96,128]{4,3,2,1,0:T(8,128)(2,1)S(1)} custom-call(bf16[2,1,4,96,128]{4,3,2,1,0:T(8,128)(2,1)S(1)} %get-tuple-element.41.refs_0_, bf16[2,1,4,96,128]{4,3,2,1,0:T(8,128)(2,1)S(1)} %collective-permute-done.5.refs_1_, f32[1,192]{1,0:T(1,128)S(1)} %bitcast.28, bf16[192,768]{1,0:T(8,128)(2,1)S(1)} %copy-done.6, ...), custom_call_target="tpu_custom_call" | custom-call | flops 1000000000 | bytes 3000000 | tf_op jit(solution)/shard_map/mlp_air1/pallas_call | solution.py:29
  46.3 1.2 %copy.24 = bf16[2,96,4,2,128]{4,3,2,1,0:T(2,128)(2,1)} copy(bf16[2,96,4,2,128]{4,1,2,0,3:T(8,128)(2,1)S(1)} %bitcast.19) | data formatting | bytes 786432
  (33 shorter events, 0.1 us)
Async XLA Ops:
  0.6 7.9 %copy-start.10 = (f32[64,3,7,7]{0,3,2,1:T(8,128)S(1)}, f32[64,3,7,7]{0,3,2,1:T(8,128)}, u32[]{:S(2)}) copy-start(f32[64,3,7,7]{0,3,2,1:T(8,128)} %param.20) | copy-start | bytes 112900
  0.6 7.9 %copy-start.11 = (f32[96,3,7,7]{0,3,2,1:T(8,128)S(1)}, f32[96,3,7,7]{0,3,2,1:T(8,128)}, u32[]{:S(2)}) copy-start(f32[96,3,7,7]{0,3,2,1:T(8,128)} %param.24) | copy-start | bytes 169348
  4.9 6.1 %collective-permute-start = (f32[120,128]{1,0:T(8,128)}, f32[120,128]{1,0:T(8,128)S(1)}, u32[]{:S(2)}, u32[]{:S(2)}) collective-permute-start(f32[120,128]{1,0:T(8,128)} %pack.1), channel_id=1, source_target_pairs={{0,128},{128,0},{1,129},{129,1},{2,130},{130,2},{3,131},{131,3},{4... | collective-permute-start | bytes 184328 | tf_op jit(solution)/shard_map/ppermute | solution.py:555
  8.6 2.4 %copy-start = (bf16[2,96,4,2,128]{4,1,2,0,3:T(8,128)(2,1)S(1)}, bf16[2,96,4,2,128]{4,1,2,0,3:T(8,128)(2,1)}, u32[]{:S(2)}) copy-start(bf16[2,96,4,2,128]{4,1,2,0,3:T(8,128)(2,1)} %copy.32) | copy-start | bytes 1179652
  8.6 2.4 %copy-start.1 = (f32[4,4,2,128]{3,2,1,0:T(2,128)S(1)}, f32[4,4,2,128]{3,2,1,0:T(2,128)}, u32[]{:S(2)}) copy-start(f32[4,4,2,128]{3,2,1,0:T(2,128)} %flux_ref.3) | copy-start | bytes 49156
  8.6 2.4 %copy-start.2 = (f32[4,256]{1,0:T(4,128)S(1)}, f32[4,256]{1,0:T(4,128)}, u32[]{:S(2)}) copy-start(f32[4,256]{1,0:T(4,128)} %temp_ref.3) | copy-start | bytes 12292
  8.6 2.4 %copy-start.3 = (s32[4,256]{1,0:T(4,128)S(1)}, s32[4,256]{1,0:T(4,128)}, u32[]{:S(2)}) copy-start(s32[4,256]{1,0:T(4,128)} %refs_7_.1) | copy-start | bytes 12292
  8.6 2.4 %copy-start.4 = (f32[4,64]{1,0:T(4,128)S(1)}, f32[4,64]{1,0:T(4,128)}, u32[]{:S(2)}) copy-start(f32[4,64]{1,0:T(4,128)} %fw_ref.3) | copy-start | bytes 3076
  8.6 2.4 %copy-start.5 = (f32[96]{0:T(128)S(1)}, f32[96]{0:T(128)}, u32[]{:S(2)}) copy-start(f32[96]{0:T(128)} %param.29) | copy-start | bytes 1156
  11.4 14.4 %collective-permute-start.1 = (bf16[2400,128]{1,0:T(8,128)(2,1)S(1)}, bf16[2400,128]{1,0:T(8,128)(2,1)S(1)}, u32[]{:S(2)}, u32[]{:S(2)}) collective-permute-start(bf16[2400,128]{1,0:T(8,128)(2,1)S(1)} %get-tuple-element.30), channel_id=1, source_target_pairs={{0,2},{2,0},{4,6},{6,4},{8,10},{10,8},{12,14},{14,12},{16,18},{18,... | collective-permute-start | bytes 1843208 | tf_op jit(solution)/shard_map/ppermute | solution.py:576
  11.5 14.3 %collective-permute-start.3 = (bf16[1152,128]{1,0:T(8,128)(2,1)S(1)}, bf16[1152,128]{1,0:T(8,128)(2,1)S(1)}, u32[]{:S(2)}, u32[]{:S(2)}) collective-permute-start(bf16[1152,128]{1,0:T(8,128)(2,1)S(1)} %get-tuple-element.37), channel_id=1, source_target_pairs={{2,4},{4,2},{6,8},{8,6},{10,12},{12,10},{14,16},{16,14},{18,20},{2... | collective-permute-start | bytes 884744 | tf_op jit(solution)/shard_map/ppermute | solution.py:577
  21.4 9.7 %collective-permute-start.2 = (bf16[1248,128]{1,0:T(8,128)(2,1)S(1)}, bf16[1248,128]{1,0:T(8,128)(2,1)S(1)}, u32[]{:S(2)}, u32[]{:S(2)}) collective-permute-start(bf16[1248,128]{1,0:T(8,128)(2,1)S(1)} %get-tuple-element.31), channel_id=1, source_target_pairs={{2,4},{4,2},{6,8},{8,6},{10,12},{12,10},{14,16},{16,14},{18,20},{2... | collective-permute-start | bytes 958472 | tf_op jit(solution)/shard_map/ppermute | solution.py:578
  28.3 10.4 %collective-permute-start.4 = (bf16[2,3,4,64,128]{4,3,2,1,0:T(8,128)(2,1)S(1)}, bf16[2,3,4,64,128]{4,3,2,1,0:T(8,128)(2,1)S(1)}, u32[]{:S(2)}, u32[]{:S(2)}) collective-permute-start(bf16[2,3,4,64,128]{4,3,2,1,0:T(8,128)(2,1)S(1)} %conv_ocean.1.refs_0_), channel_id=1, source_target_pairs={{0,1},{1,0},{2,3},{3,2},{4,5},{5,4},{6,7},{7,6},{8,9},{9,8},{10,11... | collective-permute-start | bytes 1179656 | tf_op jit(solution)/shard_map/ppermute | solution.py:590
  31.1 7.6 %copy-start.8 = (bf16[128,512]{1,0:T(8,128)(2,1)S(1)}, bf16[128,512]{1,0:T(8,128)(2,1)}, u32[]{:S(2)}) copy-start(bf16[128,512]{1,0:T(8,128)(2,1)} %refs_3_.3) | copy-start | bytes 393220
  31.1 7.6 %copy-start.9 = (bf16[512,128]{1,0:T(8,128)(2,1)S(1)}, bf16[512,128]{1,0:T(8,128)(2,1)}, u32[]{:S(2)}) copy-start(bf16[512,128]{1,0:T(8,128)(2,1)} %refs_4_.1) | copy-start | bytes 393220
  31.1 7.6 %copy-start.13 = (f32[128]{0:T(128)S(1)}, f32[128]{0:T(128)}, u32[]{:S(2)}) copy-start(f32[128]{0:T(128)} %param.21) | copy-start | bytes 1540
  36.1 7.1 %copy-start.6 = (bf16[192,768]{1,0:T(8,128)(2,1)S(1)}, bf16[192,768]{1,0:T(8,128)(2,1)}, u32[]{:S(2)}) copy-start(bf16[192,768]{1,0:T(8,128)(2,1)} %refs_3_.5) | copy-start | bytes 884740
  36.1 7.1 %copy-start.7 = (bf16[768,192]{0,1:T(8,128)(2,1)S(1)}, bf16[768,192]{0,1:T(8,128)(2,1)}, u32[]{:S(2)}) copy-start(bf16[768,192]{0,1:T(8,128)(2,1)} %param.27) | copy-start | bytes 884740
  36.1 7.1 %copy-start.12 = (f32[192]{0:T(256)S(1)}, f32[192]{0:T(256)}, u32[]{:S(2)}) copy-start(f32[192]{0:T(256)} %param.25) | copy-start | bytes 2308
  36.1 7.1 %collective-permute-start.6 = (bf16[2,1,4,96,128]{4,3,2,1,0:T(8,128)(2,1)S(1)}, bf16[2,1,4,96,128]{4,3,2,1,0:T(8,128)(2,1)S(1)}, u32[]{:S(2)}, u32[]{:S(2)}) collective-permute-start(bf16[2,1,4,96,128]{4,3,2,1,0:T(8,128)(2,1)S(1)} %get-tuple-element.43.refs_0_), channel_id=1, source_target_pairs={{0,1},{1,0},{2,3},{3,2},{4,5},{5,4},{6,7},{7,6},{8,9},{9,8},{10,11... | collective-permute-start | bytes 589832 | tf_op jit(solution)/shard_map/ppermute | solution.py:592
  37.6 7.2 %collective-permute-start.5 = (bf16[2,1,4,96,128]{4,3,2,1,0:T(8,128)(2,1)S(1)}, bf16[2,1,4,96,128]{4,3,2,1,0:T(8,128)(2,1)S(1)}, u32[]{:S(2)}, u32[]{:S(2)}) collective-permute-start(bf16[2,1,4,96,128]{4,3,2,1,0:T(8,128)(2,1)S(1)} %get-tuple-element.41.refs_0_), channel_id=1, source_target_pairs={{0,1},{1,0},{2,3},{3,2},{4,5},{5,4},{6,7},{7,6},{8,9},{9,8},{10,11... | collective-permute-start | bytes 589832 | tf_op jit(solution)/shard_map/ppermute | solution.py:592

commit v7 on v6

--- a/solution.py
+++ b/solution.py
@@ -43,18 +43,11 @@
     return temp, temp + 2 * band
 
 
-def pack_kernel(mask_hbm, temp_hbm, flux_hbm, air_ref, out_ref, mask_ref, temp_ref, flux_ref, sems):
-    copies = [
-        pltpu.make_async_copy(mask_hbm, mask_ref, sems.at[0]),
-        pltpu.make_async_copy(temp_hbm, temp_ref, sems.at[1]),
-        pltpu.make_async_copy(flux_hbm, flux_ref, sems.at[2]),
-    ]
-    for copy in copies:
-        copy.start()
+def pack_kernel(small_ref, air_ref, out_ref):
     comp = lax.axis_index("comp")
-    fields, band = flux_ref.shape[:2]
-    temp_row, edge_row = rows_of(fields, band)
-    levels, channels = air_ref.shape[1], air_ref.shape[3]
+    edge_row = small_ref.shape[0]
+    out_ref[:edge_row, :] = small_ref[...]
+    _, levels, band, channels, _ = air_ref.shape
     start = jnp.where(comp == 0, LANES - 8, 0)
     lane = lane_ids(channels)
     packed = jnp.zeros((channels, LANES), F32)
@@ -66,17 +59,7 @@
                     air_ref[h, level, j].astype(F32), (8 * idx - start + LANES) & (LANES - 1), 1
                 )
                 packed = jnp.where((lane >> 3) == idx, rolled, packed)
-    out_ref[edge_row : edge_row + channels, :] = packed
-    for copy in copies:
-        copy.wait()
-    for k in range(fields):
-        for j in range(band):
-            at = k * band + j
-            out_ref[at : at + 1, :] = flux_ref[k, j, pl.ds(1 - comp, 1), :]
-    temp = temp_ref[...] * mask_ref[...].astype(F32)
-    for s in range(2):
-        lanes = slice(s * LANES, (s + 1) * LANES)
-        out_ref[temp_row + s * band : temp_row + (s + 1) * band, :] = temp[:, lanes]
+    out_ref[edge_row:, :] = packed
 
 
 def fill_surface(mask_ref, temp_ref, surface_ref):
@@ -279,15 +262,15 @@
             halves.append(jnp.concatenate(tiles, axis=0))
         data = jnp.concatenate(halves, axis=1).astype(BF16)
         matrix = matrix_ref[sub].reshape(-1, depth)
-        product_ref[...] = jnp.dot(matrix, data, preferred_element_type=F32)
+        product_ref[sub % 2] = jnp.dot(matrix, data, preferred_element_type=F32)
         for level in range(levels):
             for i in range(band):
                 base = ((i // 2 * levels + level) * 2 + i % 2) * TAPS
                 sums = [None, None]
                 for d in range(TAPS):
                     at = slice((base + d) * 8, (base + d) * 8 + 8)
-                    first = product_ref[at, :LANES]
-                    second = product_ref[at, LANES:]
+                    first = product_ref[sub % 2, at, :LANES]
+                    second = product_ref[sub % 2, at, LANES:]
                     off = d - 3
                     if off > 0:
                         first, second = (
@@ -381,7 +364,7 @@
             [jnp.concatenate(tiles, axis=0) for tiles in columns], axis=1
         ).astype(BF16)
         matrix = matrix_ref[sub].reshape(-1, depth)
-        product_ref[...] = jnp.dot(matrix, data, preferred_element_type=F32)
+        product_ref[sub % 2] = jnp.dot(matrix, data, preferred_element_type=F32)
         for level in range(levels):
             for i in range(band):
                 base = ((i // 2 * levels + level) * 2 + i % 2) * TAPS
@@ -389,9 +372,9 @@
                 for d in range(TAPS):
                     at = slice((base + d) * 8, (base + d) * 8 + 8)
                     off = d - 3
-                    edge = product_ref[at, 2 * LANES :] if off else None
+                    edge = product_ref[sub % 2, at, 2 * LANES :] if off else None
                     for h in range(2):
-                        part = product_ref[at, h * LANES : (h + 1) * LANES]
+                        part = product_ref[sub % 2, at, h * LANES : (h + 1) * LANES]
                         if off:
                             here = edge if h == 0 else pltpu.roll(edge, LANES - 8 * band, 1)
                             inside = lane < off if off > 0 else lane >= LANES + off
@@ -404,7 +387,7 @@
 def convolution(kernel, name, own, even, odd, packed, matrix):
     _, levels, band, channels, _ = own.shape
     groups, pairs, rows, depth = matrix.shape
-    count = 16
+    count = 32
     lane_tiles = 2 if packed is None else 3
     grid_spec = pl.BlockSpec((2, levels, band, count, LANES), lambda g: (0, 0, 0, g, 0))
     args = [own, even, odd]
@@ -423,7 +406,7 @@
         out_specs=[
             pl.BlockSpec((2, part, band, count, LANES), lambda g: (0, 0, 0, g, 0)) for part in outs
         ],
-        scratch_shapes=[pltpu.VMEM((pairs * rows, lane_tiles * LANES), F32)],
+        scratch_shapes=[pltpu.VMEM((2, pairs * rows, lane_tiles * LANES), F32)],
         name=name,
         compiler_params=PARAMS,
         cost_estimate=pl.CostEstimate(flops=2 * 10**9, bytes_accessed=4 * 10**6, transcendentals=0),
@@ -485,7 +468,10 @@
                 half = sea[:, s * LANES : (s + 1) * LANES]
                 picked = lax.broadcasted_iota(jnp.int32, half.shape, 0) == i
                 result = result * jnp.sum(jnp.where(picked, half, 0.0), axis=0, keepdims=True)
-            out_ref[s, first_level + level, i] = result.astype(BF16)
+            if masked:
+                out_ref[level, i, :, s * LANES : (s + 1) * LANES] = result.astype(BF16)
+            else:
+                out_ref[s, first_level + level, i] = result.astype(BF16)
         return carry
 
     lax.fori_loop(0, levels * band // together, step, 0)
@@ -540,18 +526,18 @@
     lons = lax.axis_size("lon")
     bands = lax.axis_size("comp") * lons
     rows = rows_of(fields, band)[-1] + a_ch
-    hbm = pl.BlockSpec(memory_space=pltpu.HBM)
     surface_args = (ocean_mask, surface_temp, air_fluxes)
-    packed = pl.pallas_call(
-        pack_kernel,
-        out_shape=shape((rows, LANES), F32),
-        in_specs=[hbm, hbm, hbm, VMEM],
-        out_specs=VMEM,
-        scratch_shapes=[pltpu.VMEM(arg.shape, arg.dtype) for arg in surface_args]
-        + [pltpu.SemaphoreType.DMA((3,))],
-        name="pack",
-        compiler_params=pltpu.CompilerParams(vmem_limit_bytes=60 * 2**20),
-    )(*surface_args, air_grid)
+    partner = 1 - lax.axis_index("comp")
+    temp_rows = (surface_temp * ocean_mask.astype(F32)).reshape(band, 2, LANES)
+    small = jnp.concatenate(
+        [
+            lax.dynamic_index_in_dim(air_fluxes, partner, 2, False).reshape(-1, LANES),
+            jnp.transpose(temp_rows, (1, 0, 2)).reshape(-1, LANES),
+        ]
+    )
+    packed = call(
+        pack_kernel, shape((rows, LANES), F32), [], "pack", 10**5, 10**6, small, air_grid
+    )
     got = lax.ppermute(packed, "comp", ring(2, 1))
     later_ocean, _ = lax.optimization_barrier((ocean_state, packed))
     ocean_grid = jnp.transpose(
@@ -593,7 +579,7 @@
 
     a_hid, o_hid = air_up.shape[1], ocean_up.shape[1]
     o_next = call(
-        functools.partial(mlp_kernel, True, 0), shape(o_grid, BF16),
+        functools.partial(mlp_kernel, True, 0), shape((o_levels, band, o_ch, lats), BF16),
         [
             pltpu.VMEM((2 * o_ch, TOGETHER * 2 * LANES), F32), pltpu.VMEM((o_hid, 2 * o_ch), BF16),
             pltpu.VMEM((2 * o_ch, o_hid), BF16),
@@ -616,7 +602,7 @@
             part, other, air_gain.reshape(1, -1), air_up, air_down.T, air_top, air_forced, *done,
         )
         done = [a_next]
-    ocean_next = jnp.transpose(o_next, (1, 3, 2, 0, 4)).reshape(ocean_state.shape)
+    ocean_next = jnp.transpose(o_next, (0, 2, 1, 3))
     air_next = jnp.transpose(a_next, (1, 3, 2, 0, 4))
     return (ocean_next, air_next)
 

time: 47.7 us -> 45.2 us (0.948)
  Pallas kernels: 19 us -> 14.9 us
  waiting for transfers between devices: 6.03 us -> 7.06 us
  other arithmetic: 0 us -> 0.72 us
    pallas_call x1 -> x0, Pallas kernels: 2.43 us -> none  [per_device(): pl.pallas_call(pack_kernel, out_shape=shape((rows, LANES), F32), in_specs...]
    pallas_call x2, Pallas kernels: 7.36 us -> 5.43 us  [convolution(): pl.pallas_call(kernel, grid=(channels // count,), out_shape=[jax.ShapeDty...]
    unnamed x32 -> x29, local copies, waits for them, and re-layouts: 4.46 us -> 3.36 us
    dynamic_slice x0 -> x1, local copies, waits for them, and re-layouts: none -> 0.73 us  [per_device(): lax.dynamic_index_in_dim(air_fluxes, partner, 2, False).reshape(-1, LANES)]
    mul x0 -> x1, other arithmetic: none -> 0.71 us  [per_device(): temp_rows = (surface_temp * ocean_mask.astype(F32)).reshape(band, 2, LANES)]
    ppermute x1, waiting for transfers between devices: 1.41 us -> 1.97 us  [per_device(): odd_a = lax.ppermute(odd_out_a, 'lon', pairs_of(lons, 1))]
    pallas_call x5 -> x6, Pallas kernels: 6.89 us -> 7.13 us  [call(): pl.pallas_call(kernel, out_shape=out_shape, in_specs=[VMEM] * len(args),...]
  transfers between devices with their start and end apart: 7 -> 7, of which waited for: 3 -> 3; matrix products, arithmetic and copies ran while one was open for 6% -> 5% of each run, Pallas kernels for 31% -> 29%
where the time goes in v7:
time: 45.2 us; the launch traced here: 44.5 us
  starting transfers between devices  15.6 us (35%)
  Pallas kernels  14.9 us (33%)
  waiting for transfers between devices  7.06 us (16%)
  local copies, waits for them, and re-layouts  5.3 us (12%)
  between operations  0.9 us (2%)
  other arithmetic  0.72 us (2%)
    ppermute x1, starting transfers between devices, per_device(): odd_o = lax.ppermute(odd_out_o, ('comp', 'lon'), pairs_of(bands, 1))  9.6 us
    pallas_call x6, Pallas kernels, call(): pl.pallas_call(kernel, out_shape=out_shape, in_specs=[VMEM] * len(args),...  7.13 us
    pallas_call x2, Pallas kernels, convolution(): pl.pallas_call(kernel, grid=(channels // count,), out_shape=[jax.ShapeDty...  5.43 us
    ppermute x1, waiting for transfers between devices, per_device(): odd_o = lax.ppermute(odd_out_o, ('comp', 'lon'), pairs_of(bands, 1))  4.21 us
    unnamed x29, local copies, waits for them, and re-layouts  3.36 us
    ppermute x1, starting transfers between devices, per_device(): got = lax.ppermute(packed, 'comp', ring(2, 1))  2.38 us
    pallas_call x1, Pallas kernels, toeplitz(): pl.pallas_call(both_toeplitz_kernel, grid=(2,), out_shape=[jax.ShapeDtype...  2.36 us
    ppermute x2, starting transfers between devices, per_device(): a_others = [lax.ppermute(part, 'ch', ring(2, 1)) for part in a_convs]  2.11 us
  transfers between devices with their start and end apart: 7, of which 3 were waited for; matrix products, arithmetic and copies ran while one was open for 5% of the time, Pallas kernels for 29%

profile of v7, /device:TPU:8, one launch (start us, length us, event | category | flops | bytes accessed | tf_op | source)
XLA Modules:
  0.0 44.5 jit_solution(14769305665523460141)
XLA Ops:
  0.7 1.1 %copy.32 = bf16[2,96,4,2,128]{4,1,2,0,3:T(8,128)(2,1)S(1)} copy(bf16[2,96,4,2,128]{4,3,2,1,0:T(2,128)(2,1)} %param.17) | data formatting | bytes 786432 | tf_op args[2]
  1.7 0.7 %convert_multiply_fusion = f32[4,256]{1,0:T(4,128)S(1)} fusion(f32[4,256]{1,0:T(4,128)} %temp_ref.3, s32[4,256]{1,0:T(4,128)} %refs_7_.1), kind=kLoop, calls=%fused_computation.3 | loop fusion | flops 2048 | bytes 12288 | tf_op jit(solution)/shard_map/mul | solution.py:531
  2.5 0.7 %constant_dynamic-slice_fusion = f32[4,4,1,128]{3,2,1,0:T(1,128)S(1)} fusion(f32[4,4,2,128]{3,2,1,0:T(2,128)} %flux_ref.3, s32[]{:T(128)S(6)} %select_n.4), kind=kLoop, calls=%fused_computation.4 | loop fusion | bytes 16388 | tf_op jit(solution)/shard_map/jit(dynamic_index_in_dim)/dynamic_slice | solution.py:534
  3.2 0.2 pack.1
  3.4 2.4 %collective-permute-start = (f32[120,128]{1,0:T(8,128)S(1)}, f32[120,128]{1,0:T(8,128)S(1)}, u32[]{:S(2)}, u32[]{:S(2)}) collective-permute-start(f32[120,128]{1,0:T(8,128)S(1)} %pack.1), channel_id=1, source_target_pairs={{0,128},{128,0},{1,129},{129,1},{2,130},{130,2},{3,131},{131,3},{4... | collective-permute-start | bytes 184328 | tf_op jit(solution)/shard_map/ppermute | solution.py:541
  5.8 1.1 %reshape.34 = bf16[3,64,4,2,128]{4,3,2,1,0:T(2,128)(2,1)S(1)} reshape(bf16[3,64,4,256]{3,2,1,0:T(4,128)(2,1)} %param.15) | data formatting | bytes 786432 | tf_op jit(solution)/shard_map/reshape | solution.py:544
  7.1 2.4 %matrix.1 = (bf16[8,6,112,256]{3,2,1,0:T(8,128)(2,1)S(1)}, bf16[12,4,112,256]{3,2,1,0:T(8,128)(2,1)S(1)}) custom-call(f32[3,7,7,64]{3,2,1,0:T(8,128)S(1)} %bitcast.31, f32[3,7,7,96]{3,2,1,0:T(8,128)S(1)} %bitcast.32), custom_call_target="tpu_custom_call" | custom-call | flops 2000000000 | bytes 6000000 | tf_op jit(solution)/shard_map/matrix/pallas_call | solution.py:486
  9.5 0.4 force_halo.1
  9.9 0.1 collective-permute-start.1
  10.0 9.6 %collective-permute-start.3 = (bf16[1152,128]{1,0:T(8,128)(2,1)S(1)}, bf16[1152,128]{1,0:T(8,128)(2,1)S(1)}, u32[]{:S(2)}, u32[]{:S(2)}) collective-permute-start(bf16[1152,128]{1,0:T(8,128)(2,1)S(1)} %get-tuple-element.37), channel_id=1, source_target_pairs={{2,4},{4,2},{6,8},{8,6},{10,12},{12,10},{14,16},{16,14},{18,20},{2... | collective-permute-start | bytes 884744 | tf_op jit(solution)/shard_map/ppermute | solution.py:563
  19.6 0.3 force_own.1
  19.9 4.2 %collective-permute-done.3.odd_ref = bf16[1152,128]{1,0:T(8,128)(2,1)S(1)} collective-permute-done((bf16[1152,128]{1,0:T(8,128)(2,1)S(1)}, bf16[1152,128]{1,0:T(8,128)(2,1)S(1)}, u32[]{:S(2)}, u32[]{:S(2)}) %collective-permute-start.3) | collective-permute-done | bytes 294944 | tf_op jit(solution)/shard_map/ppermute | solution.py:563
  24.1 1.8 %conv_ocean.1.refs_0_ = bf16[2,3,4,64,128]{4,3,2,1,0:T(8,128)(2,1)S(1)} custom-call(bf16[2,3,4,64,128]{4,3,2,1,0:T(8,128)(2,1)S(1)} %get-tuple-element.36.own_ref.refs_6_, bf16[2400,128]{1,0:T(8,128)(2,1)S(1)} %collective-permute-done.1.even_ref, bf16[1152,128]{1,0:T(8,128)(2,1)S(1)} %collective-permute-done.3.odd_ref, ...), custom_call_target="tpu_custom_call" | custom-call | flops 2000000000 | bytes 4000000 | tf_op jit(solution)/shard_map/conv_ocean/pallas_call | solution.py:401
  25.9 1.4 %collective-permute-start.4 = (bf16[2,3,4,64,128]{4,3,2,1,0:T(8,128)(2,1)S(1)}, bf16[2,3,4,64,128]{4,3,2,1,0:T(8,128)(2,1)S(1)}, u32[]{:S(2)}, u32[]{:S(2)}) collective-permute-start(bf16[2,3,4,64,128]{4,3,2,1,0:T(8,128)(2,1)S(1)} %conv_ocean.1.refs_0_), channel_id=1, source_target_pairs={{0,1},{1,0},{2,3},{3,2},{4,5},{5,4},{6,7},{7,6},{8,9},{9,8},{10,11... | collective-permute-start | bytes 1179656 | tf_op jit(solution)/shard_map/ppermute | solution.py:576
  27.4 2.0 %collective-permute-done.2.odd_ref = bf16[1248,128]{1,0:T(8,128)(2,1)S(1)} collective-permute-done((bf16[1248,128]{1,0:T(8,128)(2,1)S(1)}, bf16[1248,128]{1,0:T(8,128)(2,1)S(1)}, u32[]{:S(2)}, u32[]{:S(2)}) %collective-permute-start.2) | collective-permute-done | bytes 319520 | tf_op jit(solution)/shard_map/ppermute | solution.py:564
  29.3 3.6 %conv_air.1 = (bf16[2,1,4,96,128]{4,3,2,1,0:T(8,128)(2,1)S(1)}, bf16[2,1,4,96,128]{4,3,2,1,0:T(8,128)(2,1)S(1)}) custom-call(bf16[2,2,4,96,128]{4,3,2,1,0:T(8,128)(2,1)S(1)} %get-tuple-element.29.own_ref.refs_6_, bf16[2400,128]{1,0:T(8,128)(2,1)S(1)} %collective-permute-done.1.even_ref, bf16[1248,128]{1,0:T(8,128)(2,1)S(1)} %collective-permute-done.2.odd_ref, ...), custom_call_target="tpu_custom_call" | custom-call | flops 2000000000 | bytes 4000000 | tf_op jit(solution)/shard_map/conv_air/pallas_call | solution.py:401
  33.0 1.4 %collective-permute-start.6 = (bf16[2,1,4,96,128]{4,3,2,1,0:T(8,128)(2,1)S(1)}, bf16[2,1,4,96,128]{4,3,2,1,0:T(8,128)(2,1)S(1)}, u32[]{:S(2)}, u32[]{:S(2)}) collective-permute-start(bf16[2,1,4,96,128]{4,3,2,1,0:T(8,128)(2,1)S(1)} %get-tuple-element.43.refs_0_), channel_id=1, source_target_pairs={{0,1},{1,0},{2,3},{3,2},{4,5},{5,4},{6,7},{7,6},{8,9},{9,8},{10,11... | collective-permute-start | bytes 589832 | tf_op jit(solution)/shard_map/ppermute | solution.py:578
  34.4 0.7 %collective-permute-start.5 = (bf16[2,1,4,96,128]{4,3,2,1,0:T(8,128)(2,1)S(1)}, bf16[2,1,4,96,128]{4,3,2,1,0:T(8,128)(2,1)S(1)}, u32[]{:S(2)}, u32[]{:S(2)}) collective-permute-start(bf16[2,1,4,96,128]{4,3,2,1,0:T(8,128)(2,1)S(1)} %get-tuple-element.41.refs_0_), channel_id=1, source_target_pairs={{0,1},{1,0},{2,3},{3,2},{4,5},{5,4},{6,7},{7,6},{8,9},{9,8},{10,11... | collective-permute-start | bytes 589832 | tf_op jit(solution)/shard_map/ppermute | solution.py:578
  35.1 0.9 %collective-permute-done.4.refs_1_ = bf16[2,3,4,64,128]{4,3,2,1,0:T(8,128)(2,1)S(1)} collective-permute-done((bf16[2,3,4,64,128]{4,3,2,1,0:T(8,128)(2,1)S(1)}, bf16[2,3,4,64,128]{4,3,2,1,0:T(8,128)(2,1)S(1)}, u32[]{:S(2)}, u32[]{:S(2)}) %collective-permute-start.4) | collective-permute-done | bytes 393248 | tf_op jit(solution)/shard_map/ppermute | solution.py:576
  36.0 3.1 %mlp_ocean.1 = bf16[3,4,64,256]{3,2,1,0:T(8,128)(2,1)S(1)} custom-call(bf16[2,3,4,64,128]{4,3,2,1,0:T(8,128)(2,1)S(1)} %conv_ocean.1.refs_0_, bf16[2,3,4,64,128]{4,3,2,1,0:T(8,128)(2,1)S(1)} %collective-permute-done.4.refs_1_, f32[1,128]{1,0:T(1,128)S(1)} %bitcast.35, bf16[128,512]{1,0:T(8,128)(2,1)S(1)} %copy-done.7, bf16[512,128]{1,0:T(8,128)(2,1)S(1)} %copy-done.8, ...), custom_call_target="tpu_custom_call" | custom-call | flops 1000000000 | bytes 3000000 | tf_op jit(solution)/shard_map/mlp_ocean/pallas_call | solution.py:29
  39.1 1.1 %copy.25 = bf16[3,64,4,256]{3,2,1,0:T(4,128)(2,1)} copy(bf16[3,64,4,256]{3,1,2,0:T(8,128)(2,1)S(1)} %bitcast.26) | data formatting | bytes 786432
  40.2 1.6 %mlp_air0.1.refs_7_ = bf16[2,1,4,96,128]{4,3,2,1,0:T(8,128)(2,1)S(1)} custom-call(bf16[2,1,4,96,128]{4,3,2,1,0:T(8,128)(2,1)S(1)} %get-tuple-element.43.refs_0_, bf16[2,1,4,96,128]{4,3,2,1,0:T(8,128)(2,1)S(1)} %collective-permute-done.6.refs_1_, f32[1,192]{1,0:T(1,128)S(1)} %bitcast.33, bf16[192,768]{1,0:T(8,128)(2,1)S(1)} %copy-done.5, ...), custom_call_target="tpu_custom_call" | custom-call | flops 1000000000 | bytes 3000000 | tf_op jit(solution)/shard_map/mlp_air0/pallas_call | solution.py:29
  41.8 1.6 %mlp_air1.1 = bf16[2,2,4,96,128]{4,3,2,1,0:T(8,128)(2,1)S(1)} custom-call(bf16[2,1,4,96,128]{4,3,2,1,0:T(8,128)(2,1)S(1)} %get-tuple-element.41.refs_0_, bf16[2,1,4,96,128]{4,3,2,1,0:T(8,128)(2,1)S(1)} %collective-permute-done.5.refs_1_, f32[1,192]{1,0:T(1,128)S(1)} %bitcast.34, bf16[192,768]{1,0:T(8,128)(2,1)S(1)} %copy-done.5, ...), custom_call_target="tpu_custom_call" | custom-call | flops 1000000000 | bytes 3000000 | tf_op jit(solution)/shard_map/mlp_air1/pallas_call | solution.py:29
  43.4 1.2 %copy.26 = bf16[2,96,4,2,128]{4,3,2,1,0:T(2,128)(2,1)} copy(bf16[2,96,4,2,128]{4,1,2,0,3:T(8,128)(2,1)S(1)} %bitcast.25) | data formatting | bytes 786432
  (33 shorter events, 0.2 us)
Async XLA Ops:
  0.6 6.4 %copy-start.9 = (f32[64,3,7,7]{0,3,2,1:T(8,128)S(1)}, f32[64,3,7,7]{0,3,2,1:T(8,128)}, u32[]{:S(2)}) copy-start(f32[64,3,7,7]{0,3,2,1:T(8,128)} %param.20) | copy-start | bytes 112900
  0.6 6.4 %copy-start.10 = (f32[96,3,7,7]{0,3,2,1:T(8,128)S(1)}, f32[96,3,7,7]{0,3,2,1:T(8,128)}, u32[]{:S(2)}) copy-start(f32[96,3,7,7]{0,3,2,1:T(8,128)} %param.24) | copy-start | bytes 169348
  3.4 6.1 %collective-permute-start = (f32[120,128]{1,0:T(8,128)S(1)}, f32[120,128]{1,0:T(8,128)S(1)}, u32[]{:S(2)}, u32[]{:S(2)}) collective-permute-start(f32[120,128]{1,0:T(8,128)S(1)} %pack.1), channel_id=1, source_target_pairs={{0,128},{128,0},{1,129},{129,1},{2,130},{130,2},{3,131},{131,3},{4... | collective-permute-start | bytes 184328 | tf_op jit(solution)/shard_map/ppermute | solution.py:541
  7.0 2.4 %copy-start = (f32[4,4,2,128]{3,2,1,0:T(2,128)S(1)}, f32[4,4,2,128]{3,2,1,0:T(2,128)}, u32[]{:S(2)}) copy-start(f32[4,4,2,128]{3,2,1,0:T(2,128)} %flux_ref.3) | copy-start | bytes 49156
  7.0 2.4 %copy-start.1 = (f32[4,256]{1,0:T(4,128)S(1)}, f32[4,256]{1,0:T(4,128)}, u32[]{:S(2)}) copy-start(f32[4,256]{1,0:T(4,128)} %temp_ref.3) | copy-start | bytes 12292
  7.0 2.4 %copy-start.2 = (s32[4,256]{1,0:T(4,128)S(1)}, s32[4,256]{1,0:T(4,128)}, u32[]{:S(2)}) copy-start(s32[4,256]{1,0:T(4,128)} %refs_7_.1) | copy-start | bytes 12292
  7.0 2.4 %copy-start.3 = (f32[4,64]{1,0:T(4,128)S(1)}, f32[4,64]{1,0:T(4,128)}, u32[]{:S(2)}) copy-start(f32[4,64]{1,0:T(4,128)} %fw_ref.3) | copy-start | bytes 3076
  7.1 2.4 %copy-start.4 = (f32[96]{0:T(128)S(1)}, f32[96]{0:T(128)}, u32[]{:S(2)}) copy-start(f32[96]{0:T(128)} %param.29) | copy-start | bytes 1156
  9.9 14.2 %collective-permute-start.1 = (bf16[2400,128]{1,0:T(8,128)(2,1)S(1)}, bf16[2400,128]{1,0:T(8,128)(2,1)S(1)}, u32[]{:S(2)}, u32[]{:S(2)}) collective-permute-start(bf16[2400,128]{1,0:T(8,128)(2,1)S(1)} %get-tuple-element.30), channel_id=1, source_target_pairs={{0,2},{2,0},{4,6},{6,4},{8,10},{10,8},{12,14},{14,12},{16,18},{18,... | collective-permute-start | bytes 1843208 | tf_op jit(solution)/shard_map/ppermute | solution.py:562
  10.0 14.1 %collective-permute-start.3 = (bf16[1152,128]{1,0:T(8,128)(2,1)S(1)}, bf16[1152,128]{1,0:T(8,128)(2,1)S(1)}, u32[]{:S(2)}, u32[]{:S(2)}) collective-permute-start(bf16[1152,128]{1,0:T(8,128)(2,1)S(1)} %get-tuple-element.37), channel_id=1, source_target_pairs={{2,4},{4,2},{6,8},{8,6},{10,12},{12,10},{14,16},{16,14},{18,20},{2... | collective-permute-start | bytes 884744 | tf_op jit(solution)/shard_map/ppermute | solution.py:563
  19.6 9.7 %collective-permute-start.2 = (bf16[1248,128]{1,0:T(8,128)(2,1)S(1)}, bf16[1248,128]{1,0:T(8,128)(2,1)S(1)}, u32[]{:S(2)}, u32[]{:S(2)}) collective-permute-start(bf16[1248,128]{1,0:T(8,128)(2,1)S(1)} %get-tuple-element.31), channel_id=1, source_target_pairs={{2,4},{4,2},{6,8},{8,6},{10,12},{12,10},{14,16},{16,14},{18,20},{2... | collective-permute-start | bytes 958472 | tf_op jit(solution)/shard_map/ppermute | solution.py:564
  25.9 10.1 %collective-permute-start.4 = (bf16[2,3,4,64,128]{4,3,2,1,0:T(8,128)(2,1)S(1)}, bf16[2,3,4,64,128]{4,3,2,1,0:T(8,128)(2,1)S(1)}, u32[]{:S(2)}, u32[]{:S(2)}) collective-permute-start(bf16[2,3,4,64,128]{4,3,2,1,0:T(8,128)(2,1)S(1)} %conv_ocean.1.refs_0_), channel_id=1, source_target_pairs={{0,1},{1,0},{2,3},{3,2},{4,5},{5,4},{6,7},{7,6},{8,9},{9,8},{10,11... | collective-permute-start | bytes 1179656 | tf_op jit(solution)/shard_map/ppermute | solution.py:576
  29.3 6.7 %copy-start.7 = (bf16[128,512]{1,0:T(8,128)(2,1)S(1)}, bf16[128,512]{1,0:T(8,128)(2,1)}, u32[]{:S(2)}) copy-start(bf16[128,512]{1,0:T(8,128)(2,1)} %refs_3_.3) | copy-start | bytes 393220
  29.3 6.7 %copy-start.8 = (bf16[512,128]{1,0:T(8,128)(2,1)S(1)}, bf16[512,128]{1,0:T(8,128)(2,1)}, u32[]{:S(2)}) copy-start(bf16[512,128]{1,0:T(8,128)(2,1)} %refs_4_.1) | copy-start | bytes 393220
  29.3 6.7 %copy-start.12 = (f32[128]{0:T(128)S(1)}, f32[128]{0:T(128)}, u32[]{:S(2)}) copy-start(f32[128]{0:T(128)} %param.21) | copy-start | bytes 1540
  33.0 7.2 %copy-start.5 = (bf16[192,768]{1,0:T(8,128)(2,1)S(1)}, bf16[192,768]{1,0:T(8,128)(2,1)}, u32[]{:S(2)}) copy-start(bf16[192,768]{1,0:T(8,128)(2,1)} %refs_3_.5) | copy-start | bytes 884740
  33.0 7.2 %copy-start.6 = (bf16[768,192]{0,1:T(8,128)(2,1)S(1)}, bf16[768,192]{0,1:T(8,128)(2,1)}, u32[]{:S(2)}) copy-start(bf16[768,192]{0,1:T(8,128)(2,1)} %param.27) | copy-start | bytes 884740
  33.0 7.2 %copy-start.11 = (f32[192]{0:T(256)S(1)}, f32[192]{0:T(256)}, u32[]{:S(2)}) copy-start(f32[192]{0:T(256)} %param.25) | copy-start | bytes 2308
  33.0 7.2 %collective-permute-start.6 = (bf16[2,1,4,96,128]{4,3,2,1,0:T(8,128)(2,1)S(1)}, bf16[2,1,4,96,128]{4,3,2,1,0:T(8,128)(2,1)S(1)}, u32[]{:S(2)}, u32[]{:S(2)}) collective-permute-start(bf16[2,1,4,96,128]{4,3,2,1,0:T(8,128)(2,1)S(1)} %get-tuple-element.43.refs_0_), channel_id=1, source_target_pairs={{0,1},{1,0},{2,3},{3,2},{4,5},{5,4},{6,7},{7,6},{8,9},{9,8},{10,11... | collective-permute-start | bytes 589832 | tf_op jit(solution)/shard_map/ppermute | solution.py:578
  34.4 7.3 %collective-permute-start.5 = (bf16[2,1,4,96,128]{4,3,2,1,0:T(8,128)(2,1)S(1)}, bf16[2,1,4,96,128]{4,3,2,1,0:T(8,128)(2,1)S(1)}, u32[]{:S(2)}, u32[]{:S(2)}) collective-permute-start(bf16[2,1,4,96,128]{4,3,2,1,0:T(8,128)(2,1)S(1)} %get-tuple-element.41.refs_0_), channel_id=1, source_target_pairs={{0,1},{1,0},{2,3},{3,2},{4,5},{5,4},{6,7},{7,6},{8,9},{9,8},{10,11... | collective-permute-start | bytes 589832 | tf_op jit(solution)/shard_map/ppermute | solution.py:578

commit v8 on v7

--- a/solution.py
+++ b/solution.py
@@ -10,6 +10,7 @@
 F32 = jnp.float32
 BF16 = jnp.bfloat16
 LANES = 128
+OCEAN_TOGETHER = 12
 TOGETHER = 4
 PARAMS = pltpu.CompilerParams(vmem_limit_bytes=24 * 2**20)
 VMEM = pl.BlockSpec(memory_space=pltpu.VMEM)
@@ -413,22 +414,21 @@
     )(*args)
 
 
+def flip_kernel(*refs):
+    count = len(refs) // 2
+    for source, target in zip(refs[:count], refs[count:]):
+        target[...] = source[...].astype(F32).T.astype(BF16)
+
+
 def mlp_kernel(masked, first_level, *refs):
     own_ref, other_ref, gain_ref, up_ref, down_ref, top_ref, forced_ref = refs[:7]
-    extra_ref = refs[7] if len(refs) > 11 else None
-    out_ref, values_ref, wide_ref, narrow_ref = refs[-4:]
+    extra_ref = refs[7] if len(refs) > 9 else None
+    out_ref, values_ref = refs[-2:]
     _, levels, band, channels, _ = own_ref.shape
     ch = lax.axis_index("ch")
     total = 2 * channels
     gain = column(gain_ref[...])
-    wide_ref[...] = up_ref[...].astype(F32).T.astype(BF16)
     mine = pl.ds(pl.multiple_of(ch * channels, channels), channels)
-    if masked:
-        narrow_ref[...] = down_ref[...].astype(F32).T.astype(BF16)
-    else:
-        narrow_ref[: channels] = down_ref[mine, :]
-    down_rows = mine if masked else slice(0, channels)
-
     if not masked and extra_ref is not None:
         out_ref[:, :first_level] = extra_ref[...]
     theirs = pl.ds(pl.multiple_of((1 - ch) * channels, channels), channels)
@@ -437,28 +437,29 @@
         sea = extra_ref[...].astype(F32)
 
     def step(at, carry):
-        level = at // (band // together)
-        first = lax.rem(at, band // together) * together
-        blocks = [
-            (s, n, slice((n * 2 + s) * LANES, (n * 2 + s + 1) * LANES))
-            for n in range(together)
-            for s in range(2)
-        ]
-        for s, n, lanes in blocks:
-            values_ref[mine, lanes] = own_ref[s, level, first + n].astype(F32)
-            values_ref[theirs, lanes] = other_ref[s, level, first + n].astype(F32)
+        blocks = []
+        for n in range(together):
+            index = at * together + n
+            spot = (index // band, lax.rem(index, band))
+            if together % band == 0:
+                spot = (at * (together // band) + n // band, n % band)
+            for s in range(2):
+                at_lane = (n * 2 + s) * LANES
+                blocks.append((s, *spot, slice(at_lane, at_lane + LANES)))
+        for s, level, i, lanes in blocks:
+            values_ref[mine, lanes] = own_ref[s, level, i].astype(F32)
+            values_ref[theirs, lanes] = other_ref[s, level, i].astype(F32)
         values = values_ref[...]
         center = jnp.sum(values, axis=0, keepdims=True) * (1.0 / total)
         values = values - center
         spread = jnp.sum(values * values, axis=0, keepdims=True) * (1.0 / total)
         normed = (values * lax.rsqrt(spread + 1e-06) * gain).astype(BF16)
-        raw = jnp.dot(wide_ref[...], normed, preferred_element_type=F32)
+        raw = jnp.dot(up_ref[...], normed, preferred_element_type=F32)
         inner = raw * (0.7978845608028654 + 0.035677408136300125 * (raw * raw))
         doubled = (raw + raw * jnp.tanh(inner)).astype(BF16)
-        update = jnp.dot(narrow_ref[down_rows, :], doubled, preferred_element_type=F32) * 0.5
+        update = jnp.dot(down_ref[mine, :], doubled, preferred_element_type=F32) * 0.5
         update = update.astype(BF16).astype(F32)
-        for s, n, lanes in blocks:
-            i = first + n
+        for s, level, i, lanes in blocks:
             if first_level:
                 forced = forced_ref[s, first_level + level, i].astype(F32)
             else:
@@ -572,20 +573,25 @@
         *surface_args, got, ocean_grid, air_grid, *weights,
     )
 
+    sources = (ocean_up, ocean_down, air_up)
+    *sources, ocean_forced = lax.optimization_barrier((*sources, ocean_forced))
+    o_wide, o_narrow, a_wide = call(
+        flip_kernel, tuple(shape(part.shape[::-1], BF16) for part in sources), [], "flip",
+        10**6, 10**6, *sources,
+    )
+    o_wide, o_narrow, a_wide, ocean_forced = lax.optimization_barrier(
+        (o_wide, o_narrow, a_wide, ocean_forced)
+    )
     (o_conv,) = convolution(conv_ocean_kernel, "conv_ocean", ocean_forced, even, odd_o, None, o_matrix)
     o_other = lax.ppermute(o_conv, "ch", ring(2, 1))
     a_convs = convolution(conv_air_kernel, "conv_air", air_forced, even, odd_a, edge, a_matrix)
     a_others = [lax.ppermute(part, "ch", ring(2, 1)) for part in a_convs]
 
-    a_hid, o_hid = air_up.shape[1], ocean_up.shape[1]
     o_next = call(
         functools.partial(mlp_kernel, True, 0), shape((o_levels, band, o_ch, lats), BF16),
-        [
-            pltpu.VMEM((2 * o_ch, TOGETHER * 2 * LANES), F32), pltpu.VMEM((o_hid, 2 * o_ch), BF16),
-            pltpu.VMEM((2 * o_ch, o_hid), BF16),
-        ],
+        [pltpu.VMEM((2 * o_ch, OCEAN_TOGETHER * 2 * LANES), F32)],
         "mlp_ocean", 10**9, 3 * 10**6,
-        o_conv, o_other, ocean_gain.reshape(1, -1), ocean_up, ocean_down, ocean_top, ocean_forced,
+        o_conv, o_other, ocean_gain.reshape(1, -1), o_wide, o_narrow, ocean_top, ocean_forced,
         ocean_mask,
     )
     done = []
@@ -594,12 +600,9 @@
         a_next = call(
             functools.partial(mlp_kernel, False, level),
             shape((2, level + 1) + a_grid[2:], BF16),
-            [
-                pltpu.VMEM((2 * a_ch, TOGETHER * 2 * LANES), F32), pltpu.VMEM((a_hid, 2 * a_ch), BF16),
-                pltpu.VMEM((2 * a_ch, a_hid), BF16),
-            ],
+            [pltpu.VMEM((2 * a_ch, TOGETHER * 2 * LANES), F32)],
             f"mlp_air{level}", 10**9, 3 * 10**6,
-            part, other, air_gain.reshape(1, -1), air_up, air_down.T, air_top, air_forced, *done,
+            part, other, air_gain.reshape(1, -1), a_wide, air_down.T, air_top, air_forced, *done,
         )
         done = [a_next]
     ocean_next = jnp.transpose(o_next, (0, 2, 1, 3))

time: 45.2 us -> 44.7 us (0.989)
    pallas_call x6 -> x7, Pallas kernels: 7.13 us -> 6.92 us  [call(): pl.pallas_call(kernel, out_shape=out_shape, in_specs=[VMEM] * len(args),...]
where the time goes in v8:
time: 44.7 us; the launch traced here: 44.1 us
  starting transfers between devices  15.6 us (35%)
  Pallas kernels  14.7 us (33%)
  waiting for transfers between devices  6.83 us (15%)
  local copies, waits for them, and re-layouts  5.31 us (12%)
  between operations  0.93 us (2%)
  other arithmetic  0.72 us (2%)
    ppermute x1, starting transfers between devices, per_device(): odd_o = lax.ppermute(odd_out_o, ('comp', 'lon'), pairs_of(bands, 1))  9.57 us
    pallas_call x7, Pallas kernels, call(): pl.pallas_call(kernel, out_shape=out_shape, in_specs=[VMEM] * len(args),...  6.92 us
    pallas_call x2, Pallas kernels, convolution(): pl.pallas_call(kernel, grid=(channels // count,), out_shape=[jax.ShapeDty...  5.43 us
    ppermute x1, waiting for transfers between devices, per_device(): odd_o = lax.ppermute(odd_out_o, ('comp', 'lon'), pairs_of(bands, 1))  3.94 us
    unnamed x29, local copies, waits for them, and re-layouts  3.36 us
    ppermute x1, starting transfers between devices, per_device(): got = lax.ppermute(packed, 'comp', ring(2, 1))  2.38 us
    pallas_call x1, Pallas kernels, toeplitz(): pl.pallas_call(both_toeplitz_kernel, grid=(2,), out_shape=[jax.ShapeDtype...  2.35 us
    ppermute x2, starting transfers between devices, per_device(): a_others = [lax.ppermute(part, 'ch', ring(2, 1)) for part in a_convs]  2.11 us
  transfers between devices with their start and end apart: 7, of which 3 were waited for; matrix products, arithmetic and copies ran while one was open for 5% of the time, Pallas kernels for 29%

profile of v8, /device:TPU:8, one launch (start us, length us, event | category | flops | bytes accessed | tf_op | source)
XLA Modules:
  0.0 44.1 jit_solution(3724232982250926750)
XLA Ops:
  0.7 1.1 %copy.32 = bf16[2,96,4,2,128]{4,1,2,0,3:T(8,128)(2,1)S(1)} copy(bf16[2,96,4,2,128]{4,3,2,1,0:T(2,128)(2,1)} %param.17) | data formatting | bytes 786432 | tf_op args[2]
  1.7 0.7 %convert_multiply_fusion = f32[4,256]{1,0:T(4,128)S(1)} fusion(f32[4,256]{1,0:T(4,128)} %temp_ref.3, s32[4,256]{1,0:T(4,128)} %refs_7_.1), kind=kLoop, calls=%fused_computation.3 | loop fusion | flops 2048 | bytes 12288 | tf_op jit(solution)/shard_map/mul | solution.py:532
  2.5 0.7 %constant_dynamic-slice_fusion = f32[4,4,1,128]{3,2,1,0:T(1,128)S(1)} fusion(f32[4,4,2,128]{3,2,1,0:T(2,128)} %flux_ref.3, s32[]{:T(128)S(6)} %select_n.4), kind=kLoop, calls=%fused_computation.4 | loop fusion | bytes 16388 | tf_op jit(solution)/shard_map/jit(dynamic_index_in_dim)/dynamic_slice | solution.py:535
  3.2 0.2 pack.1
  3.4 2.4 %collective-permute-start = (f32[120,128]{1,0:T(8,128)S(1)}, f32[120,128]{1,0:T(8,128)S(1)}, u32[]{:S(2)}, u32[]{:S(2)}) collective-permute-start(f32[120,128]{1,0:T(8,128)S(1)} %pack.1), channel_id=1, source_target_pairs={{0,128},{128,0},{1,129},{129,1},{2,130},{130,2},{3,131},{131,3},{4... | collective-permute-start | bytes 184328 | tf_op jit(solution)/shard_map/ppermute | solution.py:542
  5.8 1.1 %reshape.34 = bf16[3,64,4,2,128]{4,3,2,1,0:T(2,128)(2,1)S(1)} reshape(bf16[3,64,4,256]{3,2,1,0:T(4,128)(2,1)} %param.15) | data formatting | bytes 786432 | tf_op jit(solution)/shard_map/reshape | solution.py:545
  7.1 2.4 %matrix.1 = (bf16[8,6,112,256]{3,2,1,0:T(8,128)(2,1)S(1)}, bf16[12,4,112,256]{3,2,1,0:T(8,128)(2,1)S(1)}) custom-call(f32[3,7,7,64]{3,2,1,0:T(8,128)S(1)} %bitcast.31, f32[3,7,7,96]{3,2,1,0:T(8,128)S(1)} %bitcast.32), custom_call_target="tpu_custom_call" | custom-call | flops 2000000000 | bytes 6000000 | tf_op jit(solution)/shard_map/matrix/pallas_call | solution.py:487
  9.5 0.4 force_halo.1
  10.0 9.6 %collective-permute-start.3 = (bf16[1152,128]{1,0:T(8,128)(2,1)S(1)}, bf16[1152,128]{1,0:T(8,128)(2,1)S(1)}, u32[]{:S(2)}, u32[]{:S(2)}) collective-permute-start(bf16[1152,128]{1,0:T(8,128)(2,1)S(1)} %get-tuple-element.56), channel_id=1, source_target_pairs={{2,4},{4,2},{6,8},{8,6},{10,12},{12,10},{14,16},{16,14},{18,20},{2... | collective-permute-start | bytes 884744 | tf_op jit(solution)/shard_map/ppermute | solution.py:564
  19.6 0.3 force_own.1
  19.9 0.2 flip.1
  20.2 3.9 %collective-permute-done.3.odd_ref = bf16[1152,128]{1,0:T(8,128)(2,1)S(1)} collective-permute-done((bf16[1152,128]{1,0:T(8,128)(2,1)S(1)}, bf16[1152,128]{1,0:T(8,128)(2,1)S(1)}, u32[]{:S(2)}, u32[]{:S(2)}) %collective-permute-start.3) | collective-permute-done | bytes 294944 | tf_op jit(solution)/shard_map/ppermute | solution.py:564
  24.1 1.8 %conv_ocean.1.refs_0_ = bf16[2,3,4,64,128]{4,3,2,1,0:T(8,128)(2,1)S(1)} custom-call(bf16[2,3,4,64,128]{4,3,2,1,0:T(8,128)(2,1)S(1)} %get-tuple-element.55.own_ref.refs_6_, bf16[2400,128]{1,0:T(8,128)(2,1)S(1)} %collective-permute-done.1.even_ref, bf16[1152,128]{1,0:T(8,128)(2,1)S(1)} %collective-permute-done.3.odd_ref, ...), custom_call_target="tpu_custom_call" | custom-call | flops 2000000000 | bytes 4000000 | tf_op jit(solution)/shard_map/conv_ocean/pallas_call | solution.py:402
  25.9 1.4 %collective-permute-start.4 = (bf16[2,3,4,64,128]{4,3,2,1,0:T(8,128)(2,1)S(1)}, bf16[2,3,4,64,128]{4,3,2,1,0:T(8,128)(2,1)S(1)}, u32[]{:S(2)}, u32[]{:S(2)}) collective-permute-start(bf16[2,3,4,64,128]{4,3,2,1,0:T(8,128)(2,1)S(1)} %conv_ocean.1.refs_0_), channel_id=1, source_target_pairs={{0,1},{1,0},{2,3},{3,2},{4,5},{5,4},{6,7},{7,6},{8,9},{9,8},{10,11... | collective-permute-start | bytes 1179656 | tf_op jit(solution)/shard_map/ppermute | solution.py:586
  27.4 2.0 %collective-permute-done.2.odd_ref = bf16[1248,128]{1,0:T(8,128)(2,1)S(1)} collective-permute-done((bf16[1248,128]{1,0:T(8,128)(2,1)S(1)}, bf16[1248,128]{1,0:T(8,128)(2,1)S(1)}, u32[]{:S(2)}, u32[]{:S(2)}) %collective-permute-start.2) | collective-permute-done | bytes 319520 | tf_op jit(solution)/shard_map/ppermute | solution.py:565
  29.3 3.6 %conv_air.1 = (bf16[2,1,4,96,128]{4,3,2,1,0:T(8,128)(2,1)S(1)}, bf16[2,1,4,96,128]{4,3,2,1,0:T(8,128)(2,1)S(1)}) custom-call(bf16[2,2,4,96,128]{4,3,2,1,0:T(8,128)(2,1)S(1)} %get-tuple-element.40.own_ref.refs_6_, bf16[2400,128]{1,0:T(8,128)(2,1)S(1)} %collective-permute-done.1.even_ref, bf16[1248,128]{1,0:T(8,128)(2,1)S(1)} %collective-permute-done.2.odd_ref, ...), custom_call_target="tpu_custom_call" | custom-call | flops 2000000000 | bytes 4000000 | tf_op jit(solution)/shard_map/conv_air/pallas_call | solution.py:402
  33.0 1.4 %collective-permute-start.6 = (bf16[2,1,4,96,128]{4,3,2,1,0:T(8,128)(2,1)S(1)}, bf16[2,1,4,96,128]{4,3,2,1,0:T(8,128)(2,1)S(1)}, u32[]{:S(2)}, u32[]{:S(2)}) collective-permute-start(bf16[2,1,4,96,128]{4,3,2,1,0:T(8,128)(2,1)S(1)} %get-tuple-element.65.refs_0_), channel_id=1, source_target_pairs={{0,1},{1,0},{2,3},{3,2},{4,5},{5,4},{6,7},{7,6},{8,9},{9,8},{10,11... | collective-permute-start | bytes 589832 | tf_op jit(solution)/shard_map/ppermute | solution.py:588
  34.4 0.7 %collective-permute-start.5 = (bf16[2,1,4,96,128]{4,3,2,1,0:T(8,128)(2,1)S(1)}, bf16[2,1,4,96,128]{4,3,2,1,0:T(8,128)(2,1)S(1)}, u32[]{:S(2)}, u32[]{:S(2)}) collective-permute-start(bf16[2,1,4,96,128]{4,3,2,1,0:T(8,128)(2,1)S(1)} %get-tuple-element.62.refs_0_), channel_id=1, source_target_pairs={{0,1},{1,0},{2,3},{3,2},{4,5},{5,4},{6,7},{7,6},{8,9},{9,8},{10,11... | collective-permute-start | bytes 589832 | tf_op jit(solution)/shard_map/ppermute | solution.py:588
  35.1 0.9 %collective-permute-done.4.refs_1_ = bf16[2,3,4,64,128]{4,3,2,1,0:T(8,128)(2,1)S(1)} collective-permute-done((bf16[2,3,4,64,128]{4,3,2,1,0:T(8,128)(2,1)S(1)}, bf16[2,3,4,64,128]{4,3,2,1,0:T(8,128)(2,1)S(1)}, u32[]{:S(2)}, u32[]{:S(2)}) %collective-permute-start.4) | collective-permute-done | bytes 393248 | tf_op jit(solution)/shard_map/ppermute | solution.py:586
  36.0 2.8 %mlp_ocean.1 = bf16[3,4,64,256]{3,2,1,0:T(8,128)(2,1)S(1)} custom-call(bf16[2,3,4,64,128]{4,3,2,1,0:T(8,128)(2,1)S(1)} %conv_ocean.1.refs_0_, bf16[2,3,4,64,128]{4,3,2,1,0:T(8,128)(2,1)S(1)} %collective-permute-done.4.refs_1_, f32[1,128]{1,0:T(1,128)S(1)} %bitcast.35, bf16[512,128]{1,0:T(8,128)(2,1)S(1)} %get-tuple-element.58.refs_3_, ...), custom_call_target="tpu_custom_call" | custom-call | flops 1000000000 | bytes 3000000 | tf_op jit(solution)/shard_map/mlp_ocean/pallas_call | solution.py:30
  38.8 1.1 %copy.25 = bf16[3,64,4,256]{3,2,1,0:T(4,128)(2,1)} copy(bf16[3,64,4,256]{3,1,2,0:T(8,128)(2,1)S(1)} %bitcast.25) | data formatting | bytes 786432
  39.9 1.5 %mlp_air0.1.refs_7_ = bf16[2,1,4,96,128]{4,3,2,1,0:T(8,128)(2,1)S(1)} custom-call(bf16[2,1,4,96,128]{4,3,2,1,0:T(8,128)(2,1)S(1)} %get-tuple-element.65.refs_0_, bf16[2,1,4,96,128]{4,3,2,1,0:T(8,128)(2,1)S(1)} %collective-permute-done.6.refs_1_, f32[1,192]{1,0:T(1,128)S(1)} %bitcast.33, bf16[768,192]{1,0:T(8,128)(2,1)S(1)} %get-tuple-element.63.refs_3_, ...), custom_call_target="tpu_custom_call" | custom-call | flops 1000000000 | bytes 3000000 | tf_op jit(solution)/shard_map/mlp_air0/pallas_call | solution.py:30
  41.4 1.5 %mlp_air1.1 = bf16[2,2,4,96,128]{4,3,2,1,0:T(8,128)(2,1)S(1)} custom-call(bf16[2,1,4,96,128]{4,3,2,1,0:T(8,128)(2,1)S(1)} %get-tuple-element.62.refs_0_, bf16[2,1,4,96,128]{4,3,2,1,0:T(8,128)(2,1)S(1)} %collective-permute-done.5.refs_1_, f32[1,192]{1,0:T(1,128)S(1)} %bitcast.34, bf16[768,192]{1,0:T(8,128)(2,1)S(1)} %get-tuple-element.63.refs_3_, ...), custom_call_target="tpu_custom_call" | custom-call | flops 1000000000 | bytes 3000000 | tf_op jit(solution)/shard_map/mlp_air1/pallas_call | solution.py:30
  42.9 1.2 %copy.26 = bf16[2,96,4,2,128]{4,3,2,1,0:T(2,128)(2,1)} copy(bf16[2,96,4,2,128]{4,1,2,0,3:T(8,128)(2,1)S(1)} %bitcast.26) | data formatting | bytes 786432
  (34 shorter events, 0.3 us)
Async XLA Ops:
  0.6 6.4 %copy-start.9 = (f32[64,3,7,7]{0,3,2,1:T(8,128)S(1)}, f32[64,3,7,7]{0,3,2,1:T(8,128)}, u32[]{:S(2)}) copy-start(f32[64,3,7,7]{0,3,2,1:T(8,128)} %param.20) | copy-start | bytes 112900
  0.6 6.4 %copy-start.10 = (f32[96,3,7,7]{0,3,2,1:T(8,128)S(1)}, f32[96,3,7,7]{0,3,2,1:T(8,128)}, u32[]{:S(2)}) copy-start(f32[96,3,7,7]{0,3,2,1:T(8,128)} %param.24) | copy-start | bytes 169348
  3.4 6.1 %collective-permute-start = (f32[120,128]{1,0:T(8,128)S(1)}, f32[120,128]{1,0:T(8,128)S(1)}, u32[]{:S(2)}, u32[]{:S(2)}) collective-permute-start(f32[120,128]{1,0:T(8,128)S(1)} %pack.1), channel_id=1, source_target_pairs={{0,128},{128,0},{1,129},{129,1},{2,130},{130,2},{3,131},{131,3},{4... | collective-permute-start | bytes 184328 | tf_op jit(solution)/shard_map/ppermute | solution.py:542
  7.0 2.5 %copy-start.3 = (f32[4,4,2,128]{3,2,1,0:T(2,128)S(1)}, f32[4,4,2,128]{3,2,1,0:T(2,128)}, u32[]{:S(2)}) copy-start(f32[4,4,2,128]{3,2,1,0:T(2,128)} %flux_ref.3) | copy-start | bytes 49156
  7.0 2.5 %copy-start.4 = (f32[4,256]{1,0:T(4,128)S(1)}, f32[4,256]{1,0:T(4,128)}, u32[]{:S(2)}) copy-start(f32[4,256]{1,0:T(4,128)} %temp_ref.3) | copy-start | bytes 12292
  7.0 2.5 %copy-start.5 = (s32[4,256]{1,0:T(4,128)S(1)}, s32[4,256]{1,0:T(4,128)}, u32[]{:S(2)}) copy-start(s32[4,256]{1,0:T(4,128)} %refs_7_.1) | copy-start | bytes 12292
  7.0 2.5 %copy-start.6 = (f32[4,64]{1,0:T(4,128)S(1)}, f32[4,64]{1,0:T(4,128)}, u32[]{:S(2)}) copy-start(f32[4,64]{1,0:T(4,128)} %fw_ref.3) | copy-start | bytes 3076
  7.1 2.5 %copy-start.7 = (f32[96]{0:T(128)S(1)}, f32[96]{0:T(128)}, u32[]{:S(2)}) copy-start(f32[96]{0:T(128)} %param.29) | copy-start | bytes 1156
  7.1 12.8 %copy-start = (bf16[192,768]{1,0:T(8,128)(2,1)S(1)}, bf16[192,768]{1,0:T(8,128)(2,1)}, u32[]{:S(2)}) copy-start(bf16[192,768]{1,0:T(8,128)(2,1)} %refs_2_) | copy-start | bytes 884740
  7.1 12.8 %copy-start.1 = (bf16[128,512]{1,0:T(8,128)(2,1)S(1)}, bf16[128,512]{1,0:T(8,128)(2,1)}, u32[]{:S(2)}) copy-start(bf16[128,512]{1,0:T(8,128)(2,1)} %refs_0_) | copy-start | bytes 393220
  7.1 12.8 %copy-start.2 = (bf16[512,128]{1,0:T(8,128)(2,1)S(1)}, bf16[512,128]{1,0:T(8,128)(2,1)}, u32[]{:S(2)}) copy-start(bf16[512,128]{1,0:T(8,128)(2,1)} %refs_1_) | copy-start | bytes 393220
  9.9 14.2 %collective-permute-start.1 = (bf16[2400,128]{1,0:T(8,128)(2,1)S(1)}, bf16[2400,128]{1,0:T(8,128)(2,1)S(1)}, u32[]{:S(2)}, u32[]{:S(2)}) collective-permute-start(bf16[2400,128]{1,0:T(8,128)(2,1)S(1)} %get-tuple-element.41), channel_id=1, source_target_pairs={{0,2},{2,0},{4,6},{6,4},{8,10},{10,8},{12,14},{14,12},{16,18},{18,... | collective-permute-start | bytes 1843208 | tf_op jit(solution)/shard_map/ppermute | solution.py:563
  10.0 14.1 %collective-permute-start.3 = (bf16[1152,128]{1,0:T(8,128)(2,1)S(1)}, bf16[1152,128]{1,0:T(8,128)(2,1)S(1)}, u32[]{:S(2)}, u32[]{:S(2)}) collective-permute-start(bf16[1152,128]{1,0:T(8,128)(2,1)S(1)} %get-tuple-element.56), channel_id=1, source_target_pairs={{2,4},{4,2},{6,8},{8,6},{10,12},{12,10},{14,16},{16,14},{18,20},{2... | collective-permute-start | bytes 884744 | tf_op jit(solution)/shard_map/ppermute | solution.py:564
  19.6 9.7 %collective-permute-start.2 = (bf16[1248,128]{1,0:T(8,128)(2,1)S(1)}, bf16[1248,128]{1,0:T(8,128)(2,1)S(1)}, u32[]{:S(2)}, u32[]{:S(2)}) collective-permute-start(bf16[1248,128]{1,0:T(8,128)(2,1)S(1)} %get-tuple-element.42), channel_id=1, source_target_pairs={{2,4},{4,2},{6,8},{8,6},{10,12},{12,10},{14,16},{16,14},{18,20},{2... | collective-permute-start | bytes 958472 | tf_op jit(solution)/shard_map/ppermute | solution.py:565
  25.9 10.1 %collective-permute-start.4 = (bf16[2,3,4,64,128]{4,3,2,1,0:T(8,128)(2,1)S(1)}, bf16[2,3,4,64,128]{4,3,2,1,0:T(8,128)(2,1)S(1)}, u32[]{:S(2)}, u32[]{:S(2)}) collective-permute-start(bf16[2,3,4,64,128]{4,3,2,1,0:T(8,128)(2,1)S(1)} %conv_ocean.1.refs_0_), channel_id=1, source_target_pairs={{0,1},{1,0},{2,3},{3,2},{4,5},{5,4},{6,7},{7,6},{8,9},{9,8},{10,11... | collective-permute-start | bytes 1179656 | tf_op jit(solution)/shard_map/ppermute | solution.py:586
  29.3 6.7 %copy-start.12 = (f32[128]{0:T(128)S(1)}, f32[128]{0:T(128)}, u32[]{:S(2)}) copy-start(f32[128]{0:T(128)} %param.21) | copy-start | bytes 1540
  33.0 6.9 %copy-start.8 = (bf16[768,192]{0,1:T(8,128)(2,1)S(1)}, bf16[768,192]{0,1:T(8,128)(2,1)}, u32[]{:S(2)}) copy-start(bf16[768,192]{0,1:T(8,128)(2,1)} %param.27) | copy-start | bytes 884740
  33.0 6.9 %copy-start.11 = (f32[192]{0:T(256)S(1)}, f32[192]{0:T(256)}, u32[]{:S(2)}) copy-start(f32[192]{0:T(256)} %param.25) | copy-start | bytes 2308
  33.0 6.9 %collective-permute-start.6 = (bf16[2,1,4,96,128]{4,3,2,1,0:T(8,128)(2,1)S(1)}, bf16[2,1,4,96,128]{4,3,2,1,0:T(8,128)(2,1)S(1)}, u32[]{:S(2)}, u32[]{:S(2)}) collective-permute-start(bf16[2,1,4,96,128]{4,3,2,1,0:T(8,128)(2,1)S(1)} %get-tuple-element.65.refs_0_), channel_id=1, source_target_pairs={{0,1},{1,0},{2,3},{3,2},{4,5},{5,4},{6,7},{7,6},{8,9},{9,8},{10,11... | collective-permute-start | bytes 589832 | tf_op jit(solution)/shard_map/ppermute | solution.py:588
  34.4 7.0 %collective-permute-start.5 = (bf16[2,1,4,96,128]{4,3,2,1,0:T(8,128)(2,1)S(1)}, bf16[2,1,4,96,128]{4,3,2,1,0:T(8,128)(2,1)S(1)}, u32[]{:S(2)}, u32[]{:S(2)}) collective-permute-start(bf16[2,1,4,96,128]{4,3,2,1,0:T(8,128)(2,1)S(1)} %get-tuple-element.62.refs_0_), channel_id=1, source_target_pairs={{0,1},{1,0},{2,3},{3,2},{4,5},{5,4},{6,7},{7,6},{8,9},{9,8},{10,11... | collective-permute-start | bytes 589832 | tf_op jit(solution)/shard_map/ppermute | solution.py:588
